TPU v7x, 512 devices: a whole 4x4x16 slice. The times are simulated.
512 devices in a mesh: band: 16 (over y, x_lo, core), fft: 32 (over z, x_hi).
Axes of the slice: x: 4 (x_hi: 2, x_lo: 2; x = x_hi * 2 + x_lo), y: 4, z: 16, core: 2. Of those that a mesh axis runs over, the one named last changes fastest.
Arguments:
- wave_coeffs: bfloat16 [16, 2, 192, 192, 256], P('band', None, None, 'fft'), may hold values from -4 to 4
- occupation: float32 [16, 2], P('band'), may hold values from 0.05 to 0.2
- potential: bfloat16 [192, 192, 256], P('fft'), may hold values from -1.5 to 1.5
- projectors: bfloat16 [128, 8, 64, 128], P('fft'), may hold values from -0.0625 to 0.0625
- coupling: float32 [8, 8], replicated, may hold values from -4 to 4
- sphere_blocks: int32 [128, 64], replicated, may hold values from 0 to 73727, as said below
Outputs:
- applied: bfloat16 [16, 2, 192, 192, 256], P('band', None, None, 'fft')
- rho: bfloat16 [192, 192, 256], P('fft')
- projections: float32 [16, 128, 2, 8], P('band', 'fft')
Inputs may be any that keep to these rules, and one draw needn't show every extreme that they name: `sphere_blocks`: row a holds 64 distinct block numbers. The first-dimension planes of all of them lie among the planes b * 6 - 6 to b * 6 + 11, counted around the periodic grid, with b = a // 4; every row has 16 blocks in the lowest of these planes and 16 in the highest.
All inputs are finite; a program needn't handle non-finite values.
Results may differ from a plain program's by a relative error of at most 0.025.
Values may be sent and summed in bfloat16 or wider, within the bound.
A program may use at most 64 MiB of HBM per device.

v0:
```python
import math

import jax
import jax.numpy as jnp
from jax import lax
from jax.sharding import PartitionSpec as P

HALO = 6


def extended_2(shard, sides, width):
    for axis, dim in sides:
        count, length = (lax.axis_size(axis), shard.shape[dim])
        up = [(i, (i + 1) % count) for i in range(count)]
        down = [(j, i) for i, j in up]
        last = lax.slice_in_dim(shard, length - width, length, axis=dim)
        first = lax.slice_in_dim(shard, 0, width, axis=dim)
        before = lax.ppermute(last, axis, up)
        after = lax.ppermute(first, axis, down)
        shard = jnp.concatenate([before, shard, after], axis=dim)
    return shard


def passed_along(block, axis, distance):
    devices = range(lax.axis_size(axis))
    route = [((i - distance) % len(devices), i) for i in devices]
    return lax.ppermute(block, axis, route)


def dft_table(length, sign_value):
    indices = jnp.arange(length, dtype=jnp.int32)
    phases = indices[:, None] * indices[None, :] % length
    angles = 2.0 * math.pi / length * phases.astype(jnp.float32)
    factor = 1.0 / math.sqrt(length)
    cosine = jnp.cos(angles) * factor
    sine_part = jnp.sin(angles) * (sign_value * factor)
    upper_rows = jnp.stack([cosine, -sine_part])
    bottom = jnp.stack([sine_part, cosine])
    return jnp.stack([upper_rows, bottom]).astype(jnp.bfloat16)


def wave_squares(indices, length):
    frequency = (
        jnp.where(2 * indices < length, indices, indices - length).astype(jnp.float32) / length
    )
    return frequency * frequency


def per_device(wave_coeffs, occupation, potential, projectors, coupling, sphere_blocks):
    pieces = lax.axis_size("fft")
    slab_index = lax.axis_index("fft")
    coeffs = wave_coeffs[0]
    size_x = coeffs.shape[1]
    columns = coeffs.shape[2]
    size_z = coeffs.shape[3]
    slab_planes = potential.shape[0]
    size_y = potential.shape[1]
    atom_dev = projectors.shape[0]
    nproj_count = projectors.shape[1]
    block_cells = projectors.shape[3]
    zblocks = size_z // block_cells
    plane_blocks = size_y * zblocks
    table_x = dft_table(size_x, 1.0).transpose(0, 2, 1, 3).reshape(2 * size_x, 2 * size_x)
    inverse_y = dft_table(size_y, 1.0)
    inverse_z = dft_table(size_z, 1.0)
    flattened = coeffs.reshape(2 * size_x, columns * size_z)
    along_x = jnp.dot(table_x, flattened, preferred_element_type=jnp.float32)
    along_x = along_x.reshape(2, size_x, columns, size_z).astype(jnp.bfloat16)
    along_y = jnp.einsum(
        "abyk,bxkz->axyz",
        inverse_y,
        lax.all_to_all(along_x, "fft", split_axis=1, concat_axis=2, tiled=True),
        preferred_element_type=jnp.float32,
    ).astype(jnp.bfloat16)
    wave_field = jnp.einsum(
        "abzk,bxyk->axyz", inverse_z, along_y, preferred_element_type=jnp.float32
    ).astype(jnp.bfloat16)
    weights = occupation[0]
    real_part = wave_field[0].astype(jnp.float32)
    imag_part = wave_field[1].astype(jnp.float32)
    partial_density = weights[0] * real_part * real_part + weights[1] * imag_part * imag_part
    density = lax.psum(partial_density.astype(jnp.bfloat16), "band")
    strength = 3.0 * math.sqrt(block_cells * projectors.shape[2]) / nproj_count
    coupled = (coupling + coupling.T) * (0.5 * strength)
    extended = extended_2(wave_field, (("fft", 1),), HALO)
    span_planes = slab_planes + 2 * HALO
    blocks_ext = extended.reshape(2, span_planes * plane_blocks, block_cells)
    own_blocks = lax.dynamic_slice_in_dim(sphere_blocks, slab_index * atom_dev, atom_dev, 0)
    plane_index = own_blocks // plane_blocks
    ext_plane = (plane_index - slab_index * slab_planes + HALO) % (slab_planes * pieces)
    local_index = ext_plane * plane_blocks + own_blocks % plane_blocks
    gathered = blocks_ext[:, local_index]
    projections_own = jnp.einsum(
        "ajsk,bask->abj", projectors, gathered, preferred_element_type=jnp.float32
    )
    energy = jnp.einsum("ij,abj->abi", coupled, projections_own, precision=lax.Precision.HIGHEST)
    spread = jnp.einsum(
        "ajsk,abj->bask", projectors.astype(jnp.float32), energy, precision=lax.Precision.HIGHEST
    )
    accumulated = (
        jnp.zeros((2, span_planes * plane_blocks, block_cells), jnp.float32)
        .at[:, local_index]
        .add(spread)
    )
    accumulated = accumulated.reshape(2, span_planes, size_y, size_z)
    from_below = passed_along(
        accumulated[:, slab_planes + HALO :].astype(jnp.bfloat16), "fft", 1
    ).astype(jnp.float32)
    from_above = passed_along(accumulated[:, :HALO].astype(jnp.bfloat16), "fft", -1).astype(
        jnp.float32
    )
    core_field = accumulated[:, HALO : HALO + slab_planes]
    core_field = core_field.at[:, :HALO].add(from_below)
    nonlocal_term = core_field.at[:, slab_planes - HALO :].add(from_above)
    total_field = (
        potential.astype(jnp.float32)[None] * wave_field.astype(jnp.float32) + nonlocal_term
    ).astype(jnp.bfloat16)
    forward_z = dft_table(size_z, -1.0)
    forward_y = dft_table(size_y, -1.0)
    forward_x = dft_table(size_x, -1.0)
    back_z = jnp.einsum(
        "abzk,bxyk->axyz", forward_z, total_field, preferred_element_type=jnp.float32
    ).astype(jnp.bfloat16)
    back_y = jnp.einsum(
        "abyk,bxkz->axyz", forward_y, back_z, preferred_element_type=jnp.float32
    ).astype(jnp.bfloat16)
    transformed = jnp.einsum(
        "abxk,bkyz->axyz",
        forward_x,
        lax.all_to_all(back_y, "fft", split_axis=2, concat_axis=1, tiled=True),
        preferred_element_type=jnp.float32,
    )
    index_x = jnp.arange(size_x, dtype=jnp.int32)
    index_y = slab_index * columns + jnp.arange(columns, dtype=jnp.int32)
    index_z = jnp.arange(size_z, dtype=jnp.int32)
    kinetic = (
        wave_squares(index_x, size_x)[:, None, None]
        + wave_squares(index_y, size_y)[None, :, None]
        + wave_squares(index_z, size_z)[None, None, :]
    )
    applied = (transformed + kinetic[None] * coeffs.astype(jnp.float32)).astype(jnp.bfloat16)
    return (applied[None], density, projections_own[None])


def solution(mesh):
    placed = (
        P("band", None, None, "fft", None),
        P("band", None),
        P("fft", None, None),
        P("fft", None, None, None),
        P(),
        P(),
    )
    return jax.shard_map(
        per_device,
        mesh=mesh,
        in_specs=placed,
        out_specs=(
            P("band", None, None, "fft", None),
            P("fft", None, None),
            P("band", "fft", None, None),
        ),
        check_vma=False,
    )
```

profile of v0, /device:TPU:6, one launch (start us, length us, event | category | flops | bytes accessed | tf_op | source)
XLA Modules:
  0.0 461.2 jit_solution(15319921789126454849)
XLA Ops:
  14.4 2.2 copy.76
  16.7 18.2 %all-to-all-start = ((bf16[2,192,6,256]{3,0,2,1:T(2,128)(2,1)}), bf16[2,192,6,256]{3,0,2,1:T(2,128)(2,1)S(1)}, u32[]{:S(2)}, u32[]{:S(2)}) async-start(bf16[2,192,6,256]{3,0,2,1:T(2,128)(2,1)} %copy.76), calls=%async_computation | async-start | bytes 2359296 | tf_op jit(solution)/shard_map/all_to_all | solution.py:72
  36.9 1.1 multiply_convert_fusion
  38.0 1.0 fusion.40
  39.0 54.9 %all-to-all-done = bf16[2,192,6,256]{3,0,2,1:T(2,128)(2,1)S(1)} async-done(((bf16[2,192,6,256]{3,0,2,1:T(2,128)(2,1)}), bf16[2,192,6,256]{3,0,2,1:T(2,128)(2,1)S(1)}, u32[]{:S(2)}, u32[]{:S(2)}) %all-to-all-start) | async-done | bytes 1179680 | tf_op jit(solution)/shard_map/all_to_all | solution.py:72
  94.9 2.6 fusion.6
  97.4 3.5 collective-permute-start
  100.9 4.1 collective-permute-start.1
  105.4 48.2 %collective-permute-done = bf16[2,6,192,256]{3,2,0,1:T(8,128)(2,1)S(1)} collective-permute-done((bf16[2,6,192,256]{3,2,0,1:T(8,128)(2,1)S(1)}, bf16[2,6,192,256]{3,2,0,1:T(8,128)(2,1)S(1)}, u32[]{:S(2)}, u32[]{:S(2)}) %collective-permute-start) | collective-permute-done | bytes 1179680 | tf_op jit(solution)/shard_map/ppermute | solution.py:18
  153.7 1.5 pad_maximum_fusion
  155.2 2.2 copy.80
  157.3 6.4 %reshape.363 = bf16[2,6912,128]{2,1,0:T(8,128)(2,1)} reshape(bf16[2,18,192,256]{3,2,1,0:T(8,128)(2,1)} %copy.80) | data formatting | bytes 7077888 | tf_op jit(solution)/shard_map/reshape | solution.py:87
  163.8 25.7 %copy.81 = bf16[2,6912,128]{2,0,1:T(2,128)(2,1)} copy(bf16[2,6912,128]{2,1,0:T(8,128)(2,1)} %reshape.363) | data formatting | bytes 7077888 | tf_op jit(solution)/shard_map/reshape | solution.py:87
  189.4 2.9 gather_fusion
  193.9 5.0 %broadcast_in_dim.8 = f32[2,6912,128]{2,0,1:T(2,128)} broadcast(f32[]{:T(128)} %constant.162.clone.1), dimensions={} | broadcast | bytes 7077892 | tf_op jit(solution)/shard_map/broadcast_in_dim | solution.py:101
  198.9 24.7 %scatter_fusion = f32[2,6912,128]{2,0,1:T(2,128)} fusion(f32[2,6912,128]{2,0,1:T(2,128)} %broadcast_in_dim.8, s32[256]{0:T(256)S(1)} %reshape.378, f32[256,2,128]{2,1,0:T(2,128)S(1)} %bitcast.172), kind=kCustom, calls=%fused_computation.1 | custom fusion | flops 65536 | bytes 787456 | tf_op jit(solution)/shard_map/scatter-add | solution.py:103
  223.6 6.4 %copy.85 = f32[2,6912,128]{2,1,0:T(8,128)} copy(f32[2,6912,128]{2,0,1:T(2,128)} %scatter_fusion) | data formatting | bytes 14155776 | tf_op jit(solution)/shard_map/scatter-add | solution.py:103
  230.0 9.0 %reshape.364 = f32[2,18,192,256]{3,2,1,0:T(8,128)} reshape(f32[2,6912,128]{2,1,0:T(8,128)} %copy.85) | data formatting | bytes 14155776 | tf_op jit(solution)/shard_map/reshape | solution.py:105
  239.1 2.8 fusion.86
  241.8 3.4 collective-permute-start.2
  245.3 4.1 collective-permute-start.3
  249.5 47.8 %collective-permute-done.2 = bf16[2,6,192,256]{3,2,0,1:T(8,128)(2,1)S(1)} collective-permute-done((bf16[2,6,192,256]{3,2,0,1:T(8,128)(2,1)S(1)}, bf16[2,6,192,256]{3,2,0,1:T(8,128)(2,1)S(1)}, u32[]{:S(2)}, u32[]{:S(2)}) %collective-permute-start.2) | collective-permute-done | bytes 1179680 | tf_op jit(solution)/shard_map/ppermute | solution.py:27
  297.3 1.2 collective-permute-done.3
  298.5 1.0 copy-done.16
  299.5 4.9 %fusion.8 = bf16[2,6,192,256]{3,2,0,1:T(8,128)(2,1)} fusion(bf16[2,6,192,256]{3,2,0,1:T(8,128)(2,1)} %copy-done.16, bf16[2,6,192,256]{3,2,0,1:T(8,128)(2,1)} %copy-done.15, bf16[2,6,192,256]{3,2,0,1:T(8,128)(2,1)S(1)} %fusion.6, f32[6,192,256]{2,1,0:T(8,128)S(1)} %convert_element_type.181, bf16[1,2,256,256]{3,2,1,0:T(8,128)(2,1)S(1)} %copy-done.10, ...), kind=kOutput, calls=%fused_computation.20 | convolution fusion | flops 1064501248 | bytes 9076736 | tf_op jit(solution)/shard_map/abyk,bxkz->axyz/dot_general | solution.py:124
  304.4 3.5 copy.88
  307.9 8.7 %all-to-all-start.1 = ((bf16[2,6,192,256]{3,0,1,2:T(2,128)(2,1)}), bf16[2,6,192,256]{3,0,1,2:T(2,128)(2,1)S(1)}, u32[]{:S(2)}, u32[]{:S(2)}) async-start(bf16[2,6,192,256]{3,0,1,2:T(2,128)(2,1)} %copy.88), calls=%async_computation.1 | async-start | bytes 2359296 | tf_op jit(solution)/shard_map/all_to_all | solution.py:130
  317.5 2.4 fusion.11
  320.1 55.6 %all-to-all-done.1 = bf16[2,6,192,256]{3,0,1,2:T(2,128)(2,1)S(1)} async-done(((bf16[2,6,192,256]{3,0,1,2:T(2,128)(2,1)}), bf16[2,6,192,256]{3,0,1,2:T(2,128)(2,1)S(1)}, u32[]{:S(2)}, u32[]{:S(2)}) %all-to-all-start.1) | async-done | bytes 1179680 | tf_op jit(solution)/shard_map/all_to_all | solution.py:130
  377.0 1.9 fusion.9
  378.9 73.6 %all-reduce.2.cloned.1.call-done = bf16[6,192,256]{2,1,0:T(8,128)(2,1)} async-done(((bf16[6,192,256]{2,1,0:T(8,128)(2,1)}), bf16[6,192,256]{2,1,0:T(8,128)(2,1)}) %all-reduce.2.cloned.1.call-update) | async-done | bytes 589840 | tf_op jit(solution)/shard_map/psum | solution.py:82
  452.5 1.9 copy.133
  (66 shorter events, 14.4 us)
Async XLA Ops:
  7.2 185.2 %copy-start = (bf16[4,8,64,128]{3,2,1,0:T(8,128)(2,1)S(1)}, bf16[4,8,64,128]{3,2,1,0:T(8,128)(2,1)}, u32[]{:S(2)}) copy-start(bf16[4,8,64,128]{3,2,1,0:T(8,128)(2,1)} %param.17) | copy-start | bytes 1572868
  10.4 0.7 copy-start.5
  10.4 0.7 copy-start.7
  10.4 1.5 copy-start.2
  16.7 77.3 %all-to-all-start = ((bf16[2,192,6,256]{3,0,2,1:T(2,128)(2,1)}), bf16[2,192,6,256]{3,0,2,1:T(2,128)(2,1)S(1)}, u32[]{:S(2)}, u32[]{:S(2)}) async-start(bf16[2,192,6,256]{3,0,2,1:T(2,128)(2,1)} %copy.76), calls=%async_computation | async-start | bytes 2359296 | tf_op jit(solution)/shard_map/all_to_all | solution.py:72
  94.0 0.9 copy-start.6
  94.9 10.2 %copy-start.11 = (s32[128,64]{0,1:T(8,128)S(1)}, s32[128,64]{0,1:T(8,128)}, u32[]{:S(2)}) copy-start(s32[128,64]{0,1:T(8,128)} %param.19) | copy-start | bytes 98308
  94.9 10.5 %copy-start.12 = (f32[8,8]{1,0:T(8,128)S(1)}, f32[8,8]{1,0:T(8,128)}, u32[]{:S(2)}) copy-start(f32[8,8]{1,0:T(8,128)} %param.18) | copy-start | bytes 772
  97.4 56.2 %collective-permute-start = (bf16[2,6,192,256]{3,2,0,1:T(8,128)(2,1)S(1)}, bf16[2,6,192,256]{3,2,0,1:T(8,128)(2,1)S(1)}, u32[]{:S(2)}, u32[]{:S(2)}) collective-permute-start(bf16[2,6,192,256]{3,2,0,1:T(8,128)(2,1)S(1)} %fusion.6), channel_id=1, source_target_pairs={{0,1},{1,2},{2,3},{3,4},{4,5},{5,6},{6,7},{7,8},{8,9},{9,10},{10,1... | collective-permute-start | bytes 3538952 | tf_op jit(solution)/shard_map/ppermute | solution.py:18
  100.9 52.7 %collective-permute-start.1 = (bf16[2,6,192,256]{3,2,0,1:T(8,128)(2,1)S(1)}, bf16[2,6,192,256]{3,2,0,1:T(8,128)(2,1)}, u32[]{:S(2)}, u32[]{:S(2)}) collective-permute-start(bf16[2,6,192,256]{3,2,0,1:T(8,128)(2,1)S(1)} %fusion.6), channel_id=1, source_target_pairs={{1,0},{2,1},{3,2},{4,3},{5,4},{6,5},{7,6},{8,7},{9,8},{10,9},{11,1... | collective-permute-start | bytes 3538952 | tf_op jit(solution)/shard_map/ppermute | solution.py:19
  193.0 5.9 %copy-start.13 = (f32[4,2,8,1]{2,1,3,0:T(2,128)}, f32[4,2,8,1]{2,1,3,0:T(2,128)S(1)}, u32[]{:S(2)}) copy-start(f32[4,2,8,1]{2,1,3,0:T(2,128)S(1)} %fusion.30) | copy-start | bytes 772
  239.1 10.3 %copy-start.8 = (bf16[6,192,256]{2,1,0:T(8,128)(2,1)S(1)}, bf16[6,192,256]{2,1,0:T(8,128)(2,1)}, u32[]{:S(2)}) copy-start(bf16[6,192,256]{2,1,0:T(8,128)(2,1)} %param.16) | copy-start | bytes 1769476
  241.8 57.7 %copy-start.4 = (bf16[1,2,192,192]{3,2,1,0:T(8,128)(2,1)S(1)}, bf16[1,2,192,192]{3,2,1,0:T(8,128)(2,1)}, u32[]{:S(2)}) copy-start(bf16[1,2,192,192]{3,2,1,0:T(8,128)(2,1)} %get-tuple-element.52) | copy-start | bytes 442372
  241.8 57.7 %copy-start.9 = (bf16[1,2,256,256]{3,2,1,0:T(8,128)(2,1)S(1)}, bf16[1,2,256,256]{3,2,1,0:T(8,128)(2,1)}, u32[]{:S(2)}) copy-start(bf16[1,2,256,256]{3,2,1,0:T(8,128)(2,1)} %get-tuple-element.45) | copy-start | bytes 786436
  241.8 57.7 %copy-start.10 = (bf16[1,2,256,256]{3,2,1,0:T(8,128)(2,1)S(1)}, bf16[1,2,256,256]{3,2,1,0:T(8,128)(2,1)}, u32[]{:S(2)}) copy-start(bf16[1,2,256,256]{3,2,1,0:T(8,128)(2,1)} %get-tuple-element.46) | copy-start | bytes 786436
  241.8 55.4 %collective-permute-start.2 = (bf16[2,6,192,256]{3,2,0,1:T(8,128)(2,1)S(1)}, bf16[2,6,192,256]{3,2,0,1:T(8,128)(2,1)S(1)}, u32[]{:S(2)}, u32[]{:S(2)}) collective-permute-start(bf16[2,6,192,256]{3,2,0,1:T(8,128)(2,1)S(1)} %get-tuple-element.43), channel_id=1, source_target_pairs={{31,0},{0,1},{1,2},{2,3},{3,4},{4,5},{5,6},{6,7},{7,8},{8,9},{9,10... | collective-permute-start | bytes 3538952 | tf_op jit(solution)/shard_map/ppermute | solution.py:27
  245.3 53.2 %collective-permute-start.3 = (bf16[2,6,192,256]{3,2,0,1:T(8,128)(2,1)S(1)}, bf16[2,6,192,256]{3,2,0,1:T(8,128)(2,1)S(1)}, u32[]{:S(2)}, u32[]{:S(2)}) collective-permute-start(bf16[2,6,192,256]{3,2,0,1:T(8,128)(2,1)S(1)} %get-tuple-element.44), channel_id=1, source_target_pairs={{1,0},{2,1},{3,2},{4,3},{5,4},{6,5},{7,6},{8,7},{9,8},{10,9},{11,1... | collective-permute-start | bytes 3538952 | tf_op jit(solution)/shard_map/ppermute | solution.py:27
  297.3 1.2 copy-start.15
  298.5 1.0 copy-start.16
  307.9 8.8 %copy-start.14 = (f32[1,2]{1,0:T(1,128)S(1)}, f32[1,2]{1,0:T(1,128)}, u32[]{:S(2)}) copy-start(f32[1,2]{1,0:T(1,128)} %param.15) | copy-start | bytes 28
  307.9 67.8 %all-to-all-start.1 = ((bf16[2,6,192,256]{3,0,1,2:T(2,128)(2,1)}), bf16[2,6,192,256]{3,0,1,2:T(2,128)(2,1)S(1)}, u32[]{:S(2)}, u32[]{:S(2)}) async-start(bf16[2,6,192,256]{3,0,1,2:T(2,128)(2,1)} %copy.88), calls=%async_computation.1 | async-start | bytes 2359296 | tf_op jit(solution)/shard_map/all_to_all | solution.py:130
  316.7 135.8 %all-reduce.2.cloned.1.call-start = ((), (), s32[]{:S(2)}) async-start(), calls=%async_computation.2 | async-start | bytes 1179648 | tf_op jit(solution)/shard_map/psum | solution.py:82
  375.7 1.3 copy-start.3
  377.0 77.4 %copy-start.1 = (bf16[4,8,64,128]{3,2,1,0:T(8,128)(2,1)S(1)}, bf16[4,8,64,128]{3,2,1,0:T(8,128)(2,1)}, u32[]{:S(2)}) copy-start(bf16[4,8,64,128]{3,2,1,0:T(8,128)(2,1)} %param.17) | copy-start | bytes 1572868
Sparse Core Ops, SparseCore 0:
  321.0 131.4 all-reduce.1
where the time goes:
time: 466 us; the launch traced here: 461 us
  waiting for transfers between devices  281 us (60%)
  local copies, waits for them, and re-layouts  75.3 us (16%)
  starting transfers between devices  42 us (9%)
  other arithmetic  36.5 us (8%)
  between operations  14.3 us (3%)
  matrix products  11.7 us (3%)
    psum x1, waiting for transfers between devices, per_device(): density = lax.psum(partial_density.astype(jnp.bfloat16), 'band')  73.6 us
    all_to_all x1, waiting for transfers between devices, per_device(): lax.all_to_all(back_y, 'fft', split_axis=2, concat_axis=1, tiled=True)  55.6 us
    all_to_all x1, waiting for transfers between devices, per_device(): lax.all_to_all(along_x, 'fft', split_axis=1, concat_axis=2, tiled=True)  54.9 us
    ppermute x2, waiting for transfers between devices, passed_along(): return lax.ppermute(block, axis, route)  49 us
    ppermute x1, waiting for transfers between devices, extended_2(): before = lax.ppermute(last, axis, up)  48.2 us
    reshape x2, local copies, waits for them, and re-layouts, per_device(): blocks_ext = extended.reshape(2, span_planes * plane_blocks, block_cells)  32.1 us
    scatter-add x1, other arithmetic, per_device(): accumulated = jnp.zeros((2, span_planes * plane_blocks, block_cells), jnp...  24.7 us
    all_to_all x1, starting transfers between devices, per_device(): lax.all_to_all(along_x, 'fft', split_axis=1, concat_axis=2, tiled=True)  18.2 us
  transfers between devices with their start and end apart: 7, of which 6 were waited for; matrix products, arithmetic and copies ran while one was open for 2% of the time, Pallas kernels for 0%

commit v1 on v0

--- a/solution.py
+++ b/solution.py
@@ -82,14 +82,19 @@
     density = lax.psum(partial_density.astype(jnp.bfloat16), "band")
     strength = 3.0 * math.sqrt(block_cells * projectors.shape[2]) / nproj_count
     coupled = (coupling + coupling.T) * (0.5 * strength)
-    extended = extended_2(wave_field, (("fft", 1),), HALO)
-    span_planes = slab_planes + 2 * HALO
-    blocks_ext = extended.reshape(2, span_planes * plane_blocks, block_cells)
-    own_blocks = lax.dynamic_slice_in_dim(sphere_blocks, slab_index * atom_dev, atom_dev, 0)
-    plane_index = own_blocks // plane_blocks
-    ext_plane = (plane_index - slab_index * slab_planes + HALO) % (slab_planes * pieces)
-    local_index = ext_plane * plane_blocks + own_blocks % plane_blocks
-    gathered = blocks_ext[:, local_index]
+    own_blocks = wave_field.reshape(2, slab_planes * plane_blocks, block_cells)
+    slab_blocks = slab_planes * plane_blocks
+    around = [(slab_index + shift) % pieces for shift in (-1, 0, 1)]
+    atom_rows = jnp.stack(
+        [lax.dynamic_slice_in_dim(sphere_blocks, d * atom_dev, atom_dev, 0) for d in around]
+    )
+    local_index = atom_rows - slab_index * slab_blocks
+    is_mine = (atom_rows // slab_blocks) == slab_index
+    safe_index = jnp.where(is_mine, local_index, 0)
+    picked = jnp.where(is_mine[None, ..., None], own_blocks[:, safe_index], 0).astype(jnp.bfloat16)
+    from_right = passed_along(picked[:, 0], "fft", -1)
+    from_left = passed_along(picked[:, 2], "fft", 1)
+    gathered = picked[:, 1] + from_right + from_left
     projections_own = jnp.einsum(
         "ajsk,bask->abj", projectors, gathered, preferred_element_type=jnp.float32
     )
@@ -97,21 +102,16 @@
     spread = jnp.einsum(
         "ajsk,abj->bask", projectors.astype(jnp.float32), energy, precision=lax.Precision.HIGHEST
     )
-    accumulated = (
-        jnp.zeros((2, span_planes * plane_blocks, block_cells), jnp.float32)
-        .at[:, local_index]
-        .add(spread)
-    )
-    accumulated = accumulated.reshape(2, span_planes, size_y, size_z)
-    from_below = passed_along(
-        accumulated[:, slab_planes + HALO :].astype(jnp.bfloat16), "fft", 1
-    ).astype(jnp.float32)
-    from_above = passed_along(accumulated[:, :HALO].astype(jnp.bfloat16), "fft", -1).astype(
-        jnp.float32
-    )
-    core_field = accumulated[:, HALO : HALO + slab_planes]
-    core_field = core_field.at[:, :HALO].add(from_below)
-    nonlocal_term = core_field.at[:, slab_planes - HALO :].add(from_above)
+    spread_sent = spread.astype(jnp.bfloat16)
+    spread_left = passed_along(spread_sent, "fft", 1).astype(jnp.float32)
+    spread_right = passed_along(spread_sent, "fft", -1).astype(jnp.float32)
+    spread_all = jnp.stack([spread_left, spread, spread_right], axis=1)
+    drop_index = jnp.where(is_mine, local_index, slab_blocks)
+    nonlocal_term = (
+        jnp.zeros((2, slab_blocks, block_cells), jnp.float32)
+        .at[:, drop_index]
+        .add(spread_all, mode="drop")
+    ).reshape(2, slab_planes, size_y, size_z)
     total_field = (
         potential.astype(jnp.float32)[None] * wave_field.astype(jnp.float32) + nonlocal_term
     ).astype(jnp.bfloat16)

time: 466 us -> 370 us (0.79)
  the two profiles are of different devices: /device:TPU:6 before, /device:TPU:4 now
where the time goes in v1:
time: 370 us; the launch traced here: 365 us
  waiting for transfers between devices  194 us (52%)
  other arithmetic  63 us (17%)
  starting transfers between devices  46.6 us (13%)
  local copies, waits for them, and re-layouts  36.8 us (10%)
  between operations  14.4 us (4%)
  matrix products  11.1 us (3%)
    psum x1, waiting for transfers between devices, per_device(): density = lax.psum(partial_density.astype(jnp.bfloat16), 'band')  79.8 us
    all_to_all x1, waiting for transfers between devices, per_device(): lax.all_to_all(along_x, 'fft', split_axis=1, concat_axis=2, tiled=True)  54.4 us
    all_to_all x1, waiting for transfers between devices, per_device(): lax.all_to_all(back_y, 'fft', split_axis=2, concat_axis=1, tiled=True)  52.8 us
    scatter-add x1, other arithmetic, per_device(): nonlocal_term = jnp.zeros((2, slab_blocks, block_cells), jnp.float32).at[...  49.2 us
    all_to_all x1, starting transfers between devices, per_device(): lax.all_to_all(along_x, 'fft', split_axis=1, concat_axis=2, tiled=True)  18.3 us
    ppermute x4, starting transfers between devices, passed_along(): return lax.ppermute(block, axis, route)  16.7 us
    reshape x2, local copies, waits for them, and re-layouts, per_device(): own_blocks = wave_field.reshape(2, slab_planes * plane_blocks, block_cells)  12.3 us
    all_to_all x1, starting transfers between devices, per_device(): lax.all_to_all(back_y, 'fft', split_axis=2, concat_axis=1, tiled=True)  11.5 us
  transfers between devices with their start and end apart: 7, of which 7 were waited for; matrix products, arithmetic and copies ran while one was open for 3% of the time, Pallas kernels for 0%

profile of v1, /device:TPU:4, one launch (start us, length us, event | category | flops | bytes accessed | tf_op | source)
XLA Modules:
  0.0 365.5 jit_solution(5529370944716579704)
XLA Ops:
  14.4 2.2 copy.90
  16.6 18.3 %all-to-all-start = ((bf16[2,192,6,256]{3,0,2,1:T(2,128)(2,1)}), bf16[2,192,6,256]{3,0,2,1:T(2,128)(2,1)S(1)}, u32[]{:S(2)}, u32[]{:S(2)}) async-start(bf16[2,192,6,256]{3,0,2,1:T(2,128)(2,1)} %copy.90), calls=%async_computation | async-start | bytes 2359296 | tf_op jit(solution)/shard_map/all_to_all | solution.py:72
  36.5 1.0 negate_convert_fusion
  37.5 1.1 multiply_convert_fusion
  38.7 1.0 fusion.39
  39.7 54.4 %all-to-all-done = bf16[2,192,6,256]{3,0,2,1:T(2,128)(2,1)S(1)} async-done(((bf16[2,192,6,256]{3,0,2,1:T(2,128)(2,1)}), bf16[2,192,6,256]{3,0,2,1:T(2,128)(2,1)S(1)}, u32[]{:S(2)}, u32[]{:S(2)}) %all-to-all-start) | async-done | bytes 1179680 | tf_op jit(solution)/shard_map/all_to_all | solution.py:72
  95.0 2.5 fusion.4
  97.5 1.2 copy.99
  99.0 2.2 reshape.640
  101.2 10.1 %copy.100 = bf16[2,2304,128]{2,0,1:T(2,128)(2,1)S(1)} copy(bf16[2,2304,128]{2,1,0:T(8,128)(2,1)S(1)} %reshape.640) | data formatting | bytes 2359296 | tf_op jit(solution)/shard_map/reshape | solution.py:85
  111.3 2.9 gather_fusion
  114.1 1.2 fusion.30
  115.5 2.3 collective-permute-start
  117.8 6.0 %collective-permute-start.1 = (bf16[2,4,64,128]{3,0,2,1:T(2,128)(2,1)S(1)}, bf16[2,4,64,128]{3,0,2,1:T(2,128)(2,1)S(1)}, u32[]{:S(2)}, u32[]{:S(2)}) collective-permute-start(bf16[2,4,64,128]{3,0,2,1:T(2,128)(2,1)S(1)} %get-tuple-element.6), channel_id=1, source_target_pairs={{31,0},{0,1},{1,2},{2,3},{3,4},{4,5},{5,6},{6,7},{7,8},{8,9},{9,10... | collective-permute-start | bytes 393224 | tf_op jit(solution)/shard_map/ppermute | solution.py:27
  123.8 1.1 collective-permute-done
  124.9 2.7 collective-permute-done.1
  129.3 2.5 collective-permute-start.3
  132.0 1.1 convert_element_type.180
  133.1 5.9 %collective-permute-start.2 = (bf16[2,4,64,128]{3,0,2,1:T(2,128)(2,1)S(1)}, bf16[2,4,64,128]{3,0,2,1:T(2,128)(2,1)S(1)}, u32[]{:S(2)}, u32[]{:S(2)}) collective-permute-start(bf16[2,4,64,128]{3,0,2,1:T(2,128)(2,1)S(1)} %get-tuple-element.20), channel_id=1, source_target_pairs={{31,0},{0,1},{1,2},{2,3},{3,4},{4,5},{5,6},{6,7},{7,8},{8,9},{9,10... | collective-permute-start | bytes 393224 | tf_op jit(solution)/shard_map/ppermute | solution.py:27
  139.2 2.7 collective-permute-done.2
  141.9 1.3 pad_maximum_fusion
  143.9 49.2 %scatter_fusion = f32[2,2304,128]{2,0,1:T(2,128)S(1)} fusion(f32[2,2304,128]{2,0,1:T(2,128)S(1)} %broadcast_in_dim.21, s32[768]{0:T(1024)S(1)} %reshape.657, f32[768,2,128]{2,1,0:T(2,128)} %bitcast.199), kind=kCustom, calls=%fused_computation.1 | custom fusion | flops 196608 | bytes 2362368 | tf_op jit(solution)/shard_map/scatter-add | solution.py:113
  193.1 1.6 copy.104
  194.7 3.6 reshape.641
  198.3 4.2 %fusion.6 = bf16[2,6,192,256]{3,2,0,1:T(8,128)(2,1)} fusion(f32[2,6,192,256]{3,2,1,0:T(8,128)} %reshape.641, bf16[2,6,192,256]{3,2,0,1:T(8,128)(2,1)S(1)} %copy-done.2, f32[6,192,256]{2,1,0:T(8,128)S(1)} %copy-done.5, bf16[1,2,256,256]{3,2,1,0:T(8,128)(2,1)} %get-tuple-element.8, bf16[1,2,256,256]{3,2,1,0:T(8,128)(2,1)} %get-tuple-element.7, ...), kind=kOutput, calls=%fused_computation.17 | convolution fusion | flops 1062141952 | bytes 6717440 | tf_op jit(solution)/shard_map/abyk,bxkz->axyz/dot_general | solution.py:124
  202.6 3.5 copy.106
  206.1 11.5 %all-to-all-start.1 = ((bf16[2,6,192,256]{3,0,1,2:T(2,128)(2,1)}), bf16[2,6,192,256]{3,0,1,2:T(2,128)(2,1)S(1)}, u32[]{:S(2)}, u32[]{:S(2)}) async-start(bf16[2,6,192,256]{3,0,1,2:T(2,128)(2,1)} %copy.106), calls=%async_computation.1 | async-start | bytes 2359296 | tf_op jit(solution)/shard_map/all_to_all | solution.py:130
  218.3 2.4 fusion.9
  221.0 52.8 %all-to-all-done.1 = bf16[2,6,192,256]{3,0,1,2:T(2,128)(2,1)S(1)} async-done(((bf16[2,6,192,256]{3,0,1,2:T(2,128)(2,1)}), bf16[2,6,192,256]{3,0,1,2:T(2,128)(2,1)S(1)}, u32[]{:S(2)}, u32[]{:S(2)}) %all-to-all-start.1) | async-done | bytes 1179680 | tf_op jit(solution)/shard_map/all_to_all | solution.py:130
  275.1 1.9 fusion.7
  276.9 79.8 %all-reduce.2.cloned.1.call-done = bf16[6,192,256]{2,1,0:T(8,128)(2,1)} async-done(((bf16[6,192,256]{2,1,0:T(8,128)(2,1)}), bf16[6,192,256]{2,1,0:T(8,128)(2,1)}) %all-reduce.2.cloned.1.call-update) | async-done | bytes 589840 | tf_op jit(solution)/shard_map/psum | solution.py:82
  356.7 1.9 copy.154
  (71 shorter events, 14.9 us)
Async XLA Ops:
  7.2 120.5 %copy-start = (bf16[4,8,64,128]{3,2,1,0:T(8,128)(2,1)S(1)}, bf16[4,8,64,128]{3,2,1,0:T(8,128)(2,1)}, u32[]{:S(2)}) copy-start(bf16[4,8,64,128]{3,2,1,0:T(8,128)(2,1)} %param.9) | copy-start | bytes 1572868
  10.3 0.7 copy-start.7
  10.3 0.7 copy-start.9
  10.3 1.5 copy-start.3
  16.6 18.4 %copy-start.11 = (s32[128,64]{0,1:T(8,128)S(1)}, s32[128,64]{0,1:T(8,128)}, u32[]{:S(2)}) copy-start(s32[128,64]{0,1:T(8,128)} %param.11) | copy-start | bytes 98308
  16.6 77.4 %all-to-all-start = ((bf16[2,192,6,256]{3,0,2,1:T(2,128)(2,1)}), bf16[2,192,6,256]{3,0,2,1:T(2,128)(2,1)S(1)}, u32[]{:S(2)}, u32[]{:S(2)}) async-start(bf16[2,192,6,256]{3,0,2,1:T(2,128)(2,1)} %copy.90), calls=%async_computation | async-start | bytes 2359296 | tf_op jit(solution)/shard_map/all_to_all | solution.py:72
  94.1 0.9 copy-start.8
  97.5 1.4 copy-start.1
  111.2 12.5 %copy-start.12 = (f32[8,8]{1,0:T(8,128)S(1)}, f32[8,8]{1,0:T(8,128)}, u32[]{:S(2)}) copy-start(f32[8,8]{1,0:T(8,128)} %param.10) | copy-start | bytes 772
  115.5 9.4 %collective-permute-start = (bf16[2,4,64,128]{3,0,2,1:T(2,128)(2,1)S(1)}, bf16[2,4,64,128]{3,0,2,1:T(2,128)(2,1)S(1)}, u32[]{:S(2)}, u32[]{:S(2)}) collective-permute-start(bf16[2,4,64,128]{3,0,2,1:T(2,128)(2,1)S(1)} %get-tuple-element.5), channel_id=1, source_target_pairs={{1,0},{2,1},{3,2},{4,3},{5,4},{6,5},{7,6},{8,7},{9,8},{10,9},{11,1... | collective-permute-start | bytes 393224 | tf_op jit(solution)/shard_map/ppermute | solution.py:27
  117.8 9.9 %collective-permute-start.1 = (bf16[2,4,64,128]{3,0,2,1:T(2,128)(2,1)S(1)}, bf16[2,4,64,128]{3,0,2,1:T(2,128)(2,1)S(1)}, u32[]{:S(2)}, u32[]{:S(2)}) collective-permute-start(bf16[2,4,64,128]{3,0,2,1:T(2,128)(2,1)S(1)} %get-tuple-element.6), channel_id=1, source_target_pairs={{31,0},{0,1},{1,2},{2,3},{3,4},{4,5},{5,6},{6,7},{7,8},{8,9},{9,10... | collective-permute-start | bytes 393224 | tf_op jit(solution)/shard_map/ppermute | solution.py:27
  123.8 8.1 %copy-start.10 = (bf16[6,192,256]{2,1,0:T(8,128)(2,1)S(1)}, bf16[6,192,256]{2,1,0:T(8,128)(2,1)}, u32[]{:S(2)}) copy-start(bf16[6,192,256]{2,1,0:T(8,128)(2,1)} %param.8) | copy-start | bytes 1769476
  128.4 4.6 %copy-start.13 = (f32[4,2,8,1]{2,1,3,0:T(2,128)}, f32[4,2,8,1]{2,1,3,0:T(2,128)S(1)}, u32[]{:S(2)}) copy-start(f32[4,2,8,1]{2,1,3,0:T(2,128)S(1)} %fusion.28) | copy-start | bytes 772
  129.3 9.8 %collective-permute-start.3 = (bf16[2,4,64,128]{3,0,2,1:T(2,128)(2,1)S(1)}, bf16[2,4,64,128]{3,0,2,1:T(2,128)(2,1)S(1)}, u32[]{:S(2)}, u32[]{:S(2)}) collective-permute-start(bf16[2,4,64,128]{3,0,2,1:T(2,128)(2,1)S(1)} %get-tuple-element.20), channel_id=1, source_target_pairs={{1,0},{2,1},{3,2},{4,3},{5,4},{6,5},{7,6},{8,7},{9,8},{10,9},{11,1... | collective-permute-start | bytes 393224 | tf_op jit(solution)/shard_map/ppermute | solution.py:27
  133.1 8.8 %collective-permute-start.2 = (bf16[2,4,64,128]{3,0,2,1:T(2,128)(2,1)S(1)}, bf16[2,4,64,128]{3,0,2,1:T(2,128)(2,1)S(1)}, u32[]{:S(2)}, u32[]{:S(2)}) collective-permute-start(bf16[2,4,64,128]{3,0,2,1:T(2,128)(2,1)S(1)} %get-tuple-element.20), channel_id=1, source_target_pairs={{31,0},{0,1},{1,2},{2,3},{3,4},{4,5},{5,6},{6,7},{7,8},{8,9},{9,10... | collective-permute-start | bytes 393224 | tf_op jit(solution)/shard_map/ppermute | solution.py:27
  194.7 3.6 copy-start.2
  194.7 3.6 copy-start.5
  194.7 3.6 copy-start.6
  206.1 11.6 %copy-start.14 = (f32[1,2]{1,0:T(1,128)S(1)}, f32[1,2]{1,0:T(1,128)}, u32[]{:S(2)}) copy-start(f32[1,2]{1,0:T(1,128)} %param.7) | copy-start | bytes 28
  206.1 67.7 %all-to-all-start.1 = ((bf16[2,6,192,256]{3,0,1,2:T(2,128)(2,1)}), bf16[2,6,192,256]{3,0,1,2:T(2,128)(2,1)S(1)}, u32[]{:S(2)}, u32[]{:S(2)}) async-start(bf16[2,6,192,256]{3,0,1,2:T(2,128)(2,1)} %copy.106), calls=%async_computation.1 | async-start | bytes 2359296 | tf_op jit(solution)/shard_map/all_to_all | solution.py:130
  217.6 139.1 %all-reduce.2.cloned.1.call-start = ((), (), s32[]{:S(2)}) async-start(), calls=%async_computation.2 | async-start | bytes 1179648 | tf_op jit(solution)/shard_map/psum | solution.py:82
  273.8 1.3 copy-start.4
Sparse Core Ops, SparseCore 0:
  221.9 134.7 all-reduce.1

commit v2 on v1

--- a/solution.py
+++ b/solution.py
@@ -82,16 +82,27 @@
     density = lax.psum(partial_density.astype(jnp.bfloat16), "band")
     strength = 3.0 * math.sqrt(block_cells * projectors.shape[2]) / nproj_count
     coupled = (coupling + coupling.T) * (0.5 * strength)
-    own_blocks = wave_field.reshape(2, slab_planes * plane_blocks, block_cells)
     slab_blocks = slab_planes * plane_blocks
+    slab_rows = slab_planes * size_y
     around = [(slab_index + shift) % pieces for shift in (-1, 0, 1)]
     atom_rows = jnp.stack(
         [lax.dynamic_slice_in_dim(sphere_blocks, d * atom_dev, atom_dev, 0) for d in around]
-    )
+    ).reshape(-1)
     local_index = atom_rows - slab_index * slab_blocks
     is_mine = (atom_rows // slab_blocks) == slab_index
-    safe_index = jnp.where(is_mine, local_index, 0)
-    picked = jnp.where(is_mine[None, ..., None], own_blocks[:, safe_index], 0).astype(jnp.bfloat16)
+    row_of = local_index // zblocks
+    half_of = (local_index % zblocks)[None, :, None]
+    selector = (
+        (row_of[:, None] == jnp.arange(slab_rows, dtype=jnp.int32)[None, :]) & is_mine[:, None]
+    ).astype(jnp.bfloat16)
+    field_rows = wave_field.reshape(2, slab_rows, size_z)
+    picked_rows = jnp.einsum(
+        "er,crz->cez", selector, field_rows, preferred_element_type=jnp.float32
+    ).reshape(2, -1, zblocks, block_cells)
+    picked = jnp.zeros_like(picked_rows[:, :, 0])
+    for q in range(zblocks):
+        picked = jnp.where(half_of == q, picked_rows[:, :, q], picked)
+    picked = picked.astype(jnp.bfloat16).reshape(2, 3, atom_dev, -1, block_cells)
     from_right = passed_along(picked[:, 0], "fft", -1)
     from_left = passed_along(picked[:, 2], "fft", 1)
     gathered = picked[:, 1] + from_right + from_left
@@ -105,13 +116,23 @@
     spread_sent = spread.astype(jnp.bfloat16)
     spread_left = passed_along(spread_sent, "fft", 1).astype(jnp.float32)
     spread_right = passed_along(spread_sent, "fft", -1).astype(jnp.float32)
-    spread_all = jnp.stack([spread_left, spread, spread_right], axis=1)
-    drop_index = jnp.where(is_mine, local_index, slab_blocks)
-    nonlocal_term = (
-        jnp.zeros((2, slab_blocks, block_cells), jnp.float32)
-        .at[:, drop_index]
-        .add(spread_all, mode="drop")
-    ).reshape(2, slab_planes, size_y, size_z)
+    spread_all = jnp.stack([spread_left, spread, spread_right], axis=1).reshape(
+        2, -1, 1, block_cells
+    )
+    placed_halves = jnp.concatenate(
+        [jnp.where(half_of[..., None] == q, spread_all, 0.0) for q in range(zblocks)], axis=2
+    ).reshape(2, -1, size_z)
+    upper = placed_halves.astype(jnp.bfloat16)
+    lower = (placed_halves - upper.astype(jnp.float32)).astype(jnp.bfloat16)
+    nonlocal_parts = jnp.einsum(
+        "er,cez->crz",
+        selector,
+        jnp.concatenate([upper, lower]),
+        preferred_element_type=jnp.float32,
+    )
+    nonlocal_term = (nonlocal_parts[:2] + nonlocal_parts[2:]).reshape(
+        2, slab_planes, size_y, size_z
+    )
     total_field = (
         potential.astype(jnp.float32)[None] * wave_field.astype(jnp.float32) + nonlocal_term
     ).astype(jnp.bfloat16)

time: 370 us -> 308 us (0.83)
  the two profiles are of different devices: /device:TPU:4 before, /device:TPU:6 now
where the time goes in v2:
time: 308 us; the launch traced here: 304 us
  waiting for transfers between devices  190 us (62%)
  starting transfers between devices  45.4 us (15%)
  other arithmetic  19.9 us (6%)
  local copies, waits for them, and re-layouts  19.6 us (6%)
  matrix products  14.8 us (5%)
  between operations  14.5 us (5%)
    psum x1, waiting for transfers between devices, per_device(): density = lax.psum(partial_density.astype(jnp.bfloat16), 'band')  75.6 us
    all_to_all x1, waiting for transfers between devices, per_device(): lax.all_to_all(along_x, 'fft', split_axis=1, concat_axis=2, tiled=True)  54.2 us
    all_to_all x1, waiting for transfers between devices, per_device(): lax.all_to_all(back_y, 'fft', split_axis=2, concat_axis=1, tiled=True)  53.5 us
    all_to_all x1, starting transfers between devices, per_device(): lax.all_to_all(along_x, 'fft', split_axis=1, concat_axis=2, tiled=True)  18.3 us
    ppermute x4, starting transfers between devices, passed_along(): return lax.ppermute(block, axis, route)  16.7 us
    all_to_all x1, starting transfers between devices, per_device(): lax.all_to_all(back_y, 'fft', split_axis=2, concat_axis=1, tiled=True)  10.3 us
    ppermute x4, waiting for transfers between devices, passed_along(): return lax.ppermute(block, axis, route)  6.61 us
  transfers between devices with their start and end apart: 7, of which 6 were waited for; matrix products, arithmetic and copies ran while one was open for 4% of the time, Pallas kernels for 0%

profile of v2, /device:TPU:6, one launch (start us, length us, event | category | flops | bytes accessed | tf_op | source)
XLA Modules:
  0.0 304.1 jit_solution(13707943867304292632)
XLA Ops:
  14.4 2.2 copy.90
  16.7 18.3 %all-to-all-start = ((bf16[2,192,6,256]{3,0,2,1:T(2,128)(2,1)}), bf16[2,192,6,256]{3,0,2,1:T(2,128)(2,1)S(1)}, u32[]{:S(2)}, u32[]{:S(2)}) async-start(bf16[2,192,6,256]{3,0,2,1:T(2,128)(2,1)} %copy.90), calls=%async_computation | async-start | bytes 2359296 | tf_op jit(solution)/shard_map/all_to_all | solution.py:72
  35.7 1.0 multiply_convert_fusion.2
  36.7 1.0 negate_convert_fusion
  37.7 1.1 multiply_convert_fusion
  38.8 1.0 fusion.51
  39.9 54.2 %all-to-all-done = bf16[2,192,6,256]{3,0,2,1:T(2,128)(2,1)S(1)} async-done(((bf16[2,192,6,256]{3,0,2,1:T(2,128)(2,1)}), bf16[2,192,6,256]{3,0,2,1:T(2,128)(2,1)S(1)}, u32[]{:S(2)}, u32[]{:S(2)}) %all-to-all-start) | async-done | bytes 1179680 | tf_op jit(solution)/shard_map/all_to_all | solution.py:72
  95.0 2.5 fusion.17
  97.7 0.9 copy-done.1
  98.6 1.6 fusion.3
  101.1 2.3 select_convert_fusion
  103.6 2.3 collective-permute-start
  105.9 6.0 %collective-permute-start.1 = (bf16[2,4,64,128]{3,0,2,1:T(2,128)(2,1)S(1)}, bf16[2,4,64,128]{3,0,2,1:T(2,128)(2,1)S(1)}, u32[]{:S(2)}, u32[]{:S(2)}) collective-permute-start(bf16[2,4,64,128]{3,0,2,1:T(2,128)(2,1)S(1)} %get-tuple-element.13), channel_id=1, source_target_pairs={{31,0},{0,1},{1,2},{2,3},{3,4},{4,5},{5,6},{6,7},{7,8},{8,9},{9,10... | collective-permute-start | bytes 393224 | tf_op jit(solution)/shard_map/ppermute | solution.py:27
  112.0 1.1 convert_element_type.192
  113.1 2.7 collective-permute-done.1
  117.4 2.5 collective-permute-start.3
  120.0 6.0 %collective-permute-start.2 = (bf16[2,4,64,128]{3,0,2,1:T(2,128)(2,1)S(1)}, bf16[2,4,64,128]{3,0,2,1:T(2,128)(2,1)S(1)}, u32[]{:S(2)}, u32[]{:S(2)}) collective-permute-start(bf16[2,4,64,128]{3,0,2,1:T(2,128)(2,1)S(1)} %get-tuple-element.30), channel_id=1, source_target_pairs={{31,0},{0,1},{1,2},{2,3},{3,4},{4,5},{5,6},{6,7},{7,8},{8,9},{9,10... | collective-permute-start | bytes 393224 | tf_op jit(solution)/shard_map/ppermute | solution.py:27
  125.9 1.3 collective-permute-done.3
  127.3 2.6 collective-permute-done.2
  130.4 3.5 %broadcast_select_fusion.1 = (f32[2,768,1,128]{3,0,1,2:T(2,128)S(1)}, f32[2,768,1,128]{3,0,1,2:T(2,128)S(1)}) fusion(f32[2,768,1,128]{3,0,1,2:T(2,128)S(1)} %bitcast.205, pred[768]{0:T(1024)(128)(4,1)S(1)} %get-tuple-element.26, pred[768]{0:T(1024)(128)(4,1)S(1)} %get-tuple-element.27), kind=kLoop, calls=%fused_computation.45 | loop fusion | flops 393216 | bytes 2360832 | tf_op jit(solution)/shard_map/jit(_where)/select_n | solution.py:123
  134.0 1.9 pad_maximum_fusion
  135.9 2.5 copy.103
  138.6 2.5 convolution_bitcast_fusion
  141.3 2.0 copy.104
  143.3 3.9 %fusion.19 = bf16[2,6,192,256]{3,2,0,1:T(8,128)(2,1)S(1)} fusion(f32[2,6,192,256]{3,2,1,0:T(8,128)} %bitcast.206, bf16[2,6,192,256]{3,2,0,1:T(8,128)(2,1)} %copy-done.1, f32[6,192,256]{2,1,0:T(8,128)} %convert_element_type.192, bf16[1,2,256,256]{3,2,1,0:T(8,128)(2,1)} %get-tuple-element.15, bf16[1,2,256,256]{3,2,1,0:T(8,128)(2,1)} %get-tuple-element.14, ...), kind=kOutput, calls=%fused_computation.32 | convolution fusion | flops 1062141952 | bytes 6717440 | tf_op jit(solution)/shard_map/abyk,bxkz->axyz/dot_general | solution.py:145
  147.2 2.3 copy.106
  149.4 10.3 %all-to-all-start.1 = ((bf16[2,6,192,256]{3,0,1,2:T(2,128)(2,1)}), bf16[2,6,192,256]{3,0,1,2:T(2,128)(2,1)S(1)}, u32[]{:S(2)}, u32[]{:S(2)}) async-start(bf16[2,6,192,256]{3,0,1,2:T(2,128)(2,1)} %copy.106), calls=%async_computation.1 | async-start | bytes 2359296 | tf_op jit(solution)/shard_map/all_to_all | solution.py:151
  160.5 2.4 fusion.22
  163.1 53.5 %all-to-all-done.1 = bf16[2,6,192,256]{3,0,1,2:T(2,128)(2,1)S(1)} async-done(((bf16[2,6,192,256]{3,0,1,2:T(2,128)(2,1)}), bf16[2,6,192,256]{3,0,1,2:T(2,128)(2,1)S(1)}, u32[]{:S(2)}, u32[]{:S(2)}) %all-to-all-start.1) | async-done | bytes 1179680 | tf_op jit(solution)/shard_map/all_to_all | solution.py:151
  217.9 1.9 fusion.20
  219.7 75.6 %all-reduce.2.cloned.1.call-done = bf16[6,192,256]{2,1,0:T(8,128)(2,1)} async-done(((bf16[6,192,256]{2,1,0:T(8,128)(2,1)}), bf16[6,192,256]{2,1,0:T(8,128)(2,1)}) %all-reduce.2.cloned.1.call-update) | async-done | bytes 589840 | tf_op jit(solution)/shard_map/psum | solution.py:82
  295.3 1.9 copy.154
  (76 shorter events, 14.9 us)
Async XLA Ops:
  7.2 108.6 %copy-start = (bf16[4,8,64,128]{3,2,1,0:T(8,128)(2,1)S(1)}, bf16[4,8,64,128]{3,2,1,0:T(8,128)(2,1)}, u32[]{:S(2)}) copy-start(bf16[4,8,64,128]{3,2,1,0:T(8,128)(2,1)} %param.9) | copy-start | bytes 1572868
  10.3 0.7 copy-start.6
  10.3 0.8 copy-start.8
  10.3 1.5 copy-start.3
  16.7 18.4 %copy-start.10 = (s32[128,64]{0,1:T(8,128)S(1)}, s32[128,64]{0,1:T(8,128)}, u32[]{:S(2)}) copy-start(s32[128,64]{0,1:T(8,128)} %param.11) | copy-start | bytes 98308
  16.7 77.4 %all-to-all-start = ((bf16[2,192,6,256]{3,0,2,1:T(2,128)(2,1)}), bf16[2,192,6,256]{3,0,2,1:T(2,128)(2,1)S(1)}, u32[]{:S(2)}, u32[]{:S(2)}) async-start(bf16[2,192,6,256]{3,0,2,1:T(2,128)(2,1)} %copy.90), calls=%async_computation | async-start | bytes 2359296 | tf_op jit(solution)/shard_map/all_to_all | solution.py:72
  94.1 0.9 copy-start.7
  97.6 1.0 copy-start.1
  100.6 11.2 %copy-start.11 = (f32[8,8]{1,0:T(8,128)S(1)}, f32[8,8]{1,0:T(8,128)}, u32[]{:S(2)}) copy-start(f32[8,8]{1,0:T(8,128)} %param.10) | copy-start | bytes 772
  100.7 11.3 %copy-start.9 = (bf16[6,192,256]{2,1,0:T(8,128)(2,1)S(1)}, bf16[6,192,256]{2,1,0:T(8,128)(2,1)}, u32[]{:S(2)}) copy-start(bf16[6,192,256]{2,1,0:T(8,128)(2,1)} %param.8) | copy-start | bytes 1769476
  103.6 9.5 %collective-permute-start = (bf16[2,4,64,128]{3,0,2,1:T(2,128)(2,1)S(1)}, bf16[2,4,64,128]{3,0,2,1:T(2,128)(2,1)S(1)}, u32[]{:S(2)}, u32[]{:S(2)}) collective-permute-start(bf16[2,4,64,128]{3,0,2,1:T(2,128)(2,1)S(1)} %get-tuple-element.12), channel_id=1, source_target_pairs={{1,0},{2,1},{3,2},{4,3},{5,4},{6,5},{7,6},{8,7},{9,8},{10,9},{11,1... | collective-permute-start | bytes 393224 | tf_op jit(solution)/shard_map/ppermute | solution.py:27
  105.9 9.9 %collective-permute-start.1 = (bf16[2,4,64,128]{3,0,2,1:T(2,128)(2,1)S(1)}, bf16[2,4,64,128]{3,0,2,1:T(2,128)(2,1)S(1)}, u32[]{:S(2)}, u32[]{:S(2)}) collective-permute-start(bf16[2,4,64,128]{3,0,2,1:T(2,128)(2,1)S(1)} %get-tuple-element.13), channel_id=1, source_target_pairs={{31,0},{0,1},{1,2},{2,3},{3,4},{4,5},{5,6},{6,7},{7,8},{8,9},{9,10... | collective-permute-start | bytes 393224 | tf_op jit(solution)/shard_map/ppermute | solution.py:27
  116.5 13.9 %copy-start.12 = (f32[4,2,8,1]{2,1,3,0:T(2,128)}, f32[4,2,8,1]{2,1,3,0:T(2,128)S(1)}, u32[]{:S(2)}) copy-start(f32[4,2,8,1]{2,1,3,0:T(2,128)S(1)} %fusion.41) | copy-start | bytes 772
  117.4 9.8 %collective-permute-start.3 = (bf16[2,4,64,128]{3,0,2,1:T(2,128)(2,1)S(1)}, bf16[2,4,64,128]{3,0,2,1:T(2,128)(2,1)S(1)}, u32[]{:S(2)}, u32[]{:S(2)}) collective-permute-start(bf16[2,4,64,128]{3,0,2,1:T(2,128)(2,1)S(1)} %get-tuple-element.30), channel_id=1, source_target_pairs={{1,0},{2,1},{3,2},{4,3},{5,4},{6,5},{7,6},{8,7},{9,8},{10,9},{11,1... | collective-permute-start | bytes 393224 | tf_op jit(solution)/shard_map/ppermute | solution.py:27
  120.0 10.0 %collective-permute-start.2 = (bf16[2,4,64,128]{3,0,2,1:T(2,128)(2,1)S(1)}, bf16[2,4,64,128]{3,0,2,1:T(2,128)(2,1)S(1)}, u32[]{:S(2)}, u32[]{:S(2)}) collective-permute-start(bf16[2,4,64,128]{3,0,2,1:T(2,128)(2,1)S(1)} %get-tuple-element.30), channel_id=1, source_target_pairs={{31,0},{0,1},{1,2},{2,3},{3,4},{4,5},{5,6},{6,7},{7,8},{8,9},{9,10... | collective-permute-start | bytes 393224 | tf_op jit(solution)/shard_map/ppermute | solution.py:27
  141.3 2.0 copy-start.5
  149.4 10.4 %copy-start.13 = (f32[1,2]{1,0:T(1,128)S(1)}, f32[1,2]{1,0:T(1,128)}, u32[]{:S(2)}) copy-start(f32[1,2]{1,0:T(1,128)} %param.7) | copy-start | bytes 28
  149.4 11.1 %copy-start.2 = (bf16[2,6,192,256]{3,2,0,1:T(8,128)(2,1)S(1)}, bf16[2,6,192,256]{3,2,0,1:T(8,128)(2,1)}, u32[]{:S(2)}) copy-start(bf16[2,6,192,256]{3,2,0,1:T(8,128)(2,1)} %copy-done.1) | copy-start | bytes 3538948
  149.4 67.2 %all-to-all-start.1 = ((bf16[2,6,192,256]{3,0,1,2:T(2,128)(2,1)}), bf16[2,6,192,256]{3,0,1,2:T(2,128)(2,1)S(1)}, u32[]{:S(2)}, u32[]{:S(2)}) async-start(bf16[2,6,192,256]{3,0,1,2:T(2,128)(2,1)} %copy.106), calls=%async_computation.1 | async-start | bytes 2359296 | tf_op jit(solution)/shard_map/all_to_all | solution.py:151
  159.7 135.6 %all-reduce.2.cloned.1.call-start = ((), (), s32[]{:S(2)}) async-start(), calls=%async_computation.2 | async-start | bytes 1179648 | tf_op jit(solution)/shard_map/psum | solution.py:82
  216.6 1.3 copy-start.4
Sparse Core Ops, SparseCore 0:
  164.0 131.2 all-reduce.1

commit v3 on v2

--- a/solution.py
+++ b/solution.py
@@ -3,9 +3,88 @@
 import jax
 import jax.numpy as jnp
 from jax import lax
+from jax.experimental import pallas as pl
+from jax.experimental.pallas import tpu as pltpu
 from jax.sharding import PartitionSpec as P
 
 HALO = 6
+
+
+MESH = pl.DeviceIdType.MESH
+
+
+def band_sum_kernel(part_ref, out_ref, received, reduced, sems):
+    count = part_ref.shape[0]
+    me = lax.axis_index("band")
+    column = lax.axis_index("fft")
+    barrier = pltpu.get_barrier_semaphore()
+    for k in range(1, count):
+        pl.semaphore_signal(
+            barrier, inc=1, device_id=((me + k) % count, column), device_id_type=MESH
+        )
+    pl.semaphore_wait(barrier, count - 1)
+    scatter = []
+    for k in range(1, count):
+        target = (me + k) % count
+        scatter.append(
+            pltpu.make_async_remote_copy(
+                src_ref=part_ref.at[target],
+                dst_ref=received.at[me],
+                send_sem=sems.at[0, k],
+                recv_sem=sems.at[1, k],
+                device_id=(target, column),
+                device_id_type=MESH,
+            )
+        )
+    for copy in scatter:
+        copy.start()
+    for copy in scatter:
+        copy.wait()
+    total = part_ref[me].astype(jnp.float32)
+    for k in range(1, count):
+        total = total + received[(me + count - k) % count].astype(jnp.float32)
+    reduced[me] = total.astype(reduced.dtype)
+    spread_out = []
+    for k in range(1, count):
+        target = (me + k) % count
+        spread_out.append(
+            pltpu.make_async_remote_copy(
+                src_ref=reduced.at[me],
+                dst_ref=reduced.at[me],
+                send_sem=sems.at[2, k],
+                recv_sem=sems.at[3, k],
+                device_id=(target, column),
+                device_id_type=MESH,
+            )
+        )
+    for copy in spread_out:
+        copy.start()
+    for copy in spread_out:
+        copy.wait()
+    out_ref[...] = reduced[...]
+
+
+def band_sum(values):
+    count = lax.axis_size("band")
+    shape = values.shape
+    rows = values.size // (count * 128)
+    chunks = values.reshape(count, rows, 128)
+    summed = pl.pallas_call(
+        band_sum_kernel,
+        out_shape=jax.ShapeDtypeStruct(chunks.shape, chunks.dtype),
+        in_specs=[pl.BlockSpec(memory_space=pltpu.VMEM)],
+        out_specs=pl.BlockSpec(memory_space=pltpu.VMEM),
+        scratch_shapes=[
+            pltpu.VMEM(chunks.shape, chunks.dtype),
+            pltpu.VMEM(chunks.shape, chunks.dtype),
+            pltpu.SemaphoreType.DMA((4, count)),
+        ],
+        compiler_params=pltpu.CompilerParams(collective_id=0, has_side_effects=True),
+        cost_estimate=pl.CostEstimate(
+            flops=values.size, bytes_accessed=6 * values.size, transcendentals=0
+        ),
+    )(chunks)
+    return summed.reshape(shape)
 
 
 def extended_2(shard, sides, width):
@@ -79,7 +158,7 @@
     real_part = wave_field[0].astype(jnp.float32)
     imag_part = wave_field[1].astype(jnp.float32)
     partial_density = weights[0] * real_part * real_part + weights[1] * imag_part * imag_part
-    density = lax.psum(partial_density.astype(jnp.bfloat16), "band")
+    density = band_sum(partial_density.astype(jnp.bfloat16))
     strength = 3.0 * math.sqrt(block_cells * projectors.shape[2]) / nproj_count
     coupled = (coupling + coupling.T) * (0.5 * strength)
     slab_blocks = slab_planes * plane_blocks

time: 308 us -> 215 us (0.70); the launches traced: 304 us -> 214 us
  waiting for transfers between devices: 190 us -> 81.7 us
  Pallas kernels: 0 us -> 25.9 us
  between operations: 14.5 us -> 1.13 us
  local copies, waits for them, and re-layouts: 19.6 us -> 23 us
    psum x1 -> x0, waiting for transfers between devices: 75.6 us -> none  [per_device(): density = lax.psum(partial_density.astype(jnp.bfloat16), 'band')]
    all_to_all x1, waiting for transfers between devices: 53.5 us -> 20.9 us  [per_device(): lax.all_to_all(back_y, 'fft', split_axis=2, concat_axis=1, tiled=True)]
    pallas_call x0 -> x1, Pallas kernels: none -> 25.9 us  [band_sum(): pl.pallas_call(band_sum_kernel, out_shape=jax.ShapeDtypeStruct(chunks.sha...]
  transfers between devices with their start and end apart: 7 -> 6, of which waited for: 6 -> 5; matrix products, arithmetic and copies ran while one was open for 4% -> 8% of each run, Pallas kernels for 0% -> 12%
where the time goes in v3:
time: 215 us; the launch traced here: 214 us
  waiting for transfers between devices  81.7 us (38%)
  starting transfers between devices  45.4 us (21%)
  Pallas kernels  25.9 us (12%)
  local copies, waits for them, and re-layouts  23 us (11%)
  other arithmetic  22.3 us (10%)
  matrix products  14.8 us (7%)
    all_to_all x1, waiting for transfers between devices, per_device(): lax.all_to_all(along_x, 'fft', split_axis=1, concat_axis=2, tiled=True)  54.2 us
    pallas_call x1, Pallas kernels, band_sum(): pl.pallas_call(band_sum_kernel, out_shape=jax.ShapeDtypeStruct(chunks.sha...  25.9 us
    all_to_all x1, waiting for transfers between devices, per_device(): lax.all_to_all(back_y, 'fft', split_axis=2, concat_axis=1, tiled=True)  20.9 us
    all_to_all x1, starting transfers between devices, per_device(): lax.all_to_all(along_x, 'fft', split_axis=1, concat_axis=2, tiled=True)  18.3 us
    ppermute x4, starting transfers between devices, passed_along(): return lax.ppermute(block, axis, route)  16.7 us
    all_to_all x1, starting transfers between devices, per_device(): lax.all_to_all(back_y, 'fft', split_axis=2, concat_axis=1, tiled=True)  10.3 us
    ppermute x4, waiting for transfers between devices, passed_along(): return lax.ppermute(block, axis, route)  6.6 us
    another operation x6, other arithmetic  5.49 us
  transfers between devices with their start and end apart: 6, of which 5 were waited for; matrix products, arithmetic and copies ran while one was open for 8% of the time, Pallas kernels for 12%

profile of v3, /device:TPU:6, one launch (start us, length us, event | category | flops | bytes accessed | tf_op | source)
XLA Modules:
  0.0 214.2 jit_solution(8669574414960131834)
XLA Ops:
  7.9 2.2 %copy.86 = bf16[2,192,6,256]{3,0,2,1:T(2,128)(2,1)} copy(bf16[2,192,6,256]{3,1,2,0:T(8,128)(2,1)S(1)} %convolution_convert_fusion) | data formatting | bytes 2359296 | tf_op jit(solution)/shard_map/convert_element_type | solution.py:147
  10.1 18.3 %all-to-all-start = ((bf16[2,192,6,256]{3,0,2,1:T(2,128)(2,1)}), bf16[2,192,6,256]{3,0,2,1:T(2,128)(2,1)S(1)}, u32[]{:S(2)}, u32[]{:S(2)}) async-start(bf16[2,192,6,256]{3,0,2,1:T(2,128)(2,1)} %copy.86), calls=%async_computation | async-start | bytes 2359296 | tf_op jit(solution)/shard_map/all_to_all | solution.py:151
  31.2 1.1 multiply_convert_fusion
  33.3 54.2 %all-to-all-done = bf16[2,192,6,256]{3,0,2,1:T(2,128)(2,1)S(1)} async-done(((bf16[2,192,6,256]{3,0,2,1:T(2,128)(2,1)}), bf16[2,192,6,256]{3,0,2,1:T(2,128)(2,1)S(1)}, u32[]{:S(2)}, u32[]{:S(2)}) %all-to-all-start) | async-done | bytes 1179680 | tf_op jit(solution)/shard_map/all_to_all | solution.py:151
  88.5 2.5 %fusion.17 = bf16[2,6,192,256]{3,2,0,1:T(8,128)(2,1)S(1)} fusion(bf16[2,6,192,256,1]{3,0,2,1,4:T(2,128)(2,1)S(1)} %bitcast.206, bf16[1,2,256,256]{3,2,1,0:T(8,128)(2,1)} %get-tuple-element.18, bf16[1,2,256,256]{3,2,1,0:T(8,128)(2,1)} %get-tuple-element.19, bf16[1,2,192,192]{3,2,1,0:T(8,128)(2,1)S(1)} %copy-done.7, bf16[1,2,192,192]{3,2,1,0:T(8,128)(2,1)} %copy-done.8), kind=kOutput, calls=%fused_computation.30 | convolution fusion | flops 1059782656 | bytes 3178496 | tf_op jit(solution)/shard_map/abzk,bxyk->axyz/dot_general | solution.py:154
  92.0 1.6 fusion.3
  94.6 2.3 %select_convert_fusion = bf16[2,3,4,64,128]{4,0,3,2,1:T(2,128)(2,1)S(1)} fusion(bf16[2,3,4,64,128]{4,0,3,2,1:T(2,128)(2,1)S(1)} %bitcast.204, bf16[2,3,4,64,128]{4,0,3,2,1:T(2,128)(2,1)S(1)} %bitcast.205, pred[3,4,64]{2,1,0:T(4,128)(4,1)S(1)} %broadcast_compare_fusion.1, pred[3,4,64]{2,1,0:T(4,128)(4,1)S(1)} %get-tuple-element.5), kind=kLoop, calls=%fused_computation.43 | loop fusion | flops 393216 | bytes 1181184 | tf_op jit(solution)/shard_map/convert_element_type | solution.py:184
  97.1 2.3 %collective-permute-start = (bf16[2,4,64,128]{3,0,2,1:T(2,128)(2,1)S(1)}, bf16[2,4,64,128]{3,0,2,1:T(2,128)(2,1)S(1)}, u32[]{:S(2)}, u32[]{:S(2)}) collective-permute-start(bf16[2,4,64,128]{3,0,2,1:T(2,128)(2,1)S(1)} %get-tuple-element.14), channel_id=1, source_target_pairs={{1,0},{2,1},{3,2},{4,3},{5,4},{6,5},{7,6},{8,7},{9,8},{10,9},{11,1... | collective-permute-start | bytes 393224 | tf_op jit(solution)/shard_map/ppermute | solution.py:106
  99.3 6.0 %collective-permute-start.1 = (bf16[2,4,64,128]{3,0,2,1:T(2,128)(2,1)S(1)}, bf16[2,4,64,128]{3,0,2,1:T(2,128)(2,1)S(1)}, u32[]{:S(2)}, u32[]{:S(2)}) collective-permute-start(bf16[2,4,64,128]{3,0,2,1:T(2,128)(2,1)S(1)} %get-tuple-element.15), channel_id=1, source_target_pairs={{31,0},{0,1},{1,2},{2,3},{3,4},{4,5},{5,6},{6,7},{7,8},{8,9},{9,10... | collective-permute-start | bytes 393224 | tf_op jit(solution)/shard_map/ppermute | solution.py:106
  105.4 1.1 convert_element_type.195
  106.6 2.7 %collective-permute-done.1 = bf16[2,4,64,128]{3,0,2,1:T(2,128)(2,1)S(1)} collective-permute-done((bf16[2,4,64,128]{3,0,2,1:T(2,128)(2,1)S(1)}, bf16[2,4,64,128]{3,0,2,1:T(2,128)(2,1)S(1)}, u32[]{:S(2)}, u32[]{:S(2)}) %collective-permute-start.1) | collective-permute-done | bytes 131104 | tf_op jit(solution)/shard_map/ppermute | solution.py:106
  110.9 2.5 %collective-permute-start.3 = (bf16[2,4,64,128]{3,0,2,1:T(2,128)(2,1)S(1)}, bf16[2,4,64,128]{3,0,2,1:T(2,128)(2,1)S(1)}, u32[]{:S(2)}, u32[]{:S(2)}) collective-permute-start(bf16[2,4,64,128]{3,0,2,1:T(2,128)(2,1)S(1)} %get-tuple-element.32), channel_id=1, source_target_pairs={{1,0},{2,1},{3,2},{4,3},{5,4},{6,5},{7,6},{8,7},{9,8},{10,9},{11,1... | collective-permute-start | bytes 393224 | tf_op jit(solution)/shard_map/ppermute | solution.py:106
  113.4 5.9 %collective-permute-start.2 = (bf16[2,4,64,128]{3,0,2,1:T(2,128)(2,1)S(1)}, bf16[2,4,64,128]{3,0,2,1:T(2,128)(2,1)S(1)}, u32[]{:S(2)}, u32[]{:S(2)}) collective-permute-start(bf16[2,4,64,128]{3,0,2,1:T(2,128)(2,1)S(1)} %get-tuple-element.32), channel_id=1, source_target_pairs={{31,0},{0,1},{1,2},{2,3},{3,4},{4,5},{5,6},{6,7},{7,8},{8,9},{9,10... | collective-permute-start | bytes 393224 | tf_op jit(solution)/shard_map/ppermute | solution.py:106
  119.4 1.3 collective-permute-done.3
  120.8 2.6 %collective-permute-done.2 = bf16[2,4,64,128]{3,0,2,1:T(2,128)(2,1)S(1)} collective-permute-done((bf16[2,4,64,128]{3,0,2,1:T(2,128)(2,1)S(1)}, bf16[2,4,64,128]{3,0,2,1:T(2,128)(2,1)S(1)}, u32[]{:S(2)}, u32[]{:S(2)}) %collective-permute-start.2) | collective-permute-done | bytes 131104 | tf_op jit(solution)/shard_map/ppermute | solution.py:106
  123.9 3.5 %broadcast_select_fusion.1 = (f32[2,768,1,128]{3,0,1,2:T(2,128)S(1)}, f32[2,768,1,128]{3,0,1,2:T(2,128)S(1)}) fusion(f32[2,768,1,128]{3,0,1,2:T(2,128)S(1)} %bitcast.202, pred[768]{0:T(1024)(128)(4,1)S(1)} %get-tuple-element.28, pred[768]{0:T(1024)(128)(4,1)S(1)} %get-tuple-element.29), kind=kLoop, calls=%fused_computation.45 | loop fusion | flops 393216 | bytes 2360832 | tf_op jit(solution)/shard_map/jit(_where)/select_n | solution.py:202
  127.5 1.9 pad_maximum_fusion
  129.4 2.5 %copy.99 = f32[2,768,2,128]{1,3,2,0:T(8,128)S(1)} copy(f32[2,768,2,128]{3,0,1,2:T(2,128)} %pad_maximum_fusion) | data formatting | bytes 3145728 | tf_op jit(solution)/shard_map/concatenate | solution.py:201
  132.0 2.5 %convolution_bitcast_fusion = f32[4,1152,256]{1,2,0:T(8,128)S(1)} fusion(s32[768]{0:T(1024)S(1)} %add_select_fusion.4, pred[768]{0:T(1024)(128)(4,1)S(1)} %fusion.79, bf16[2,768,256]{1,2,0:T(8,128)(2,1)S(1)} %get-tuple-element.3, bf16[2,768,256]{1,2,0:T(8,128)(2,1)S(1)} %get-tuple-element.4), kind=kOutput, calls=%fused_computation | convolution fusion | flops 1814495232 | bytes 6295296 | tf_op jit(solution)/shard_map/er,cez->crz/dot_general | solution.py:206
  134.8 2.0 copy.100
  136.7 3.9 %fusion.19 = bf16[2,6,192,256]{3,2,0,1:T(8,128)(2,1)S(1)} fusion(f32[2,6,192,256]{3,2,1,0:T(8,128)} %bitcast.203, bf16[2,6,192,256]{3,2,0,1:T(8,128)(2,1)} %copy-done.1, f32[6,192,256]{2,1,0:T(8,128)} %convert_element_type.195, bf16[1,2,256,256]{3,2,1,0:T(8,128)(2,1)} %get-tuple-element.17, bf16[1,2,256,256]{3,2,1,0:T(8,128)(2,1)} %get-tuple-element.16, ...), kind=kOutput, calls=%fused_computation.32 | convolution fusion | flops 1062141952 | bytes 6717440 | tf_op jit(solution)/shard_map/abyk,bxkz->axyz/dot_general | solution.py:224
  140.6 2.2 %copy.102 = bf16[2,6,192,256]{3,0,1,2:T(2,128)(2,1)} copy(bf16[2,6,192,256]{3,2,0,1:T(8,128)(2,1)S(1)} %fusion.19) | data formatting | bytes 2359296 | tf_op jit(solution)/shard_map/convert_element_type | solution.py:226
  142.9 10.3 %all-to-all-start.1 = ((bf16[2,6,192,256]{3,0,1,2:T(2,128)(2,1)}), bf16[2,6,192,256]{3,0,1,2:T(2,128)(2,1)}, u32[]{:S(2)}, u32[]{:S(2)}) async-start(bf16[2,6,192,256]{3,0,1,2:T(2,128)(2,1)} %copy.102), calls=%async_computation.1 | async-start | bytes 2359296 | tf_op jit(solution)/shard_map/all_to_all | solution.py:230
  153.9 1.2 slice_convert_fusion
  155.2 1.3 reshape.444
  156.5 1.1 reshape.445
  157.6 3.5 %fusion.22.part_ref = bf16[16,144,128]{2,1,0:T(8,128)(2,1)} fusion(f32[16,144,128]{2,1,0:T(8,128)S(1)} %reshape.444, f32[16,144,128]{2,1,0:T(8,128)} %reshape.445, f32[]{:T(128)} %bitcast.77, f32[]{:T(128)} %bitcast.76), kind=kLoop, calls=%fused_computation.35 | loop fusion | flops 1769472 | bytes 2949128 | tf_op jit(solution)/shard_map/convert_element_type | solution.py:161
  161.3 25.9 %shard_map.85 = bf16[16,144,128]{2,1,0:T(8,128)(2,1)} custom-call(bf16[16,144,128]{2,1,0:T(8,128)(2,1)} %fusion.22.part_ref), custom_call_target="tpu_custom_call" | custom-call | flops 294912 | bytes 1769472 | tf_op jit(solution)/shard_map/pallas_call | solution.py:72
  187.2 2.0 reshape.440
  189.3 20.9 %all-to-all-done.1 = bf16[2,6,192,256]{3,0,1,2:T(2,128)(2,1)} async-done(((bf16[2,6,192,256]{3,0,1,2:T(2,128)(2,1)}), bf16[2,6,192,256]{3,0,1,2:T(2,128)(2,1)}, u32[]{:S(2)}, u32[]{:S(2)}) %all-to-all-start.1) | async-done | bytes 1179680 | tf_op jit(solution)/shard_map/all_to_all | solution.py:230
  210.2 2.2 %copy.104 = bf16[2,32,6,6,256]{4,0,3,2,1:T(2,128)(2,1)S(1)} copy(bf16[2,32,6,6,256]{4,0,2,3,1:T(2,128)(2,1)} %bitcast.69) | data formatting | bytes 2359296 | tf_op jit(solution)/shard_map/all_to_all | solution.py:230
  212.3 1.9 fusion.20
  (77 shorter events, 17.4 us)
Async XLA Ops:
  0.6 108.6 %copy-start = (bf16[4,8,64,128]{3,2,1,0:T(8,128)(2,1)S(1)}, bf16[4,8,64,128]{3,2,1,0:T(8,128)(2,1)}, u32[]{:S(2)}) copy-start(bf16[4,8,64,128]{3,2,1,0:T(8,128)(2,1)} %param.9) | copy-start | bytes 1572868
  3.8 0.7 copy-start.6
  3.8 0.8 copy-start.8
  3.8 1.5 copy-start.3
  10.1 18.4 %copy-start.10 = (s32[128,64]{0,1:T(8,128)S(1)}, s32[128,64]{0,1:T(8,128)}, u32[]{:S(2)}) copy-start(s32[128,64]{0,1:T(8,128)} %param.11) | copy-start | bytes 98308
  10.1 77.4 %all-to-all-start = ((bf16[2,192,6,256]{3,0,2,1:T(2,128)(2,1)}), bf16[2,192,6,256]{3,0,2,1:T(2,128)(2,1)S(1)}, u32[]{:S(2)}, u32[]{:S(2)}) async-start(bf16[2,192,6,256]{3,0,2,1:T(2,128)(2,1)} %copy.86), calls=%async_computation | async-start | bytes 2359296 | tf_op jit(solution)/shard_map/all_to_all | solution.py:151
  87.5 0.9 copy-start.7
  91.0 1.0 copy-start.1
  94.1 11.2 %copy-start.11 = (f32[8,8]{1,0:T(8,128)S(1)}, f32[8,8]{1,0:T(8,128)}, u32[]{:S(2)}) copy-start(f32[8,8]{1,0:T(8,128)} %param.10) | copy-start | bytes 772
  94.1 11.3 %copy-start.9 = (bf16[6,192,256]{2,1,0:T(8,128)(2,1)S(1)}, bf16[6,192,256]{2,1,0:T(8,128)(2,1)}, u32[]{:S(2)}) copy-start(bf16[6,192,256]{2,1,0:T(8,128)(2,1)} %param.8) | copy-start | bytes 1769476
  97.1 9.5 %collective-permute-start = (bf16[2,4,64,128]{3,0,2,1:T(2,128)(2,1)S(1)}, bf16[2,4,64,128]{3,0,2,1:T(2,128)(2,1)S(1)}, u32[]{:S(2)}, u32[]{:S(2)}) collective-permute-start(bf16[2,4,64,128]{3,0,2,1:T(2,128)(2,1)S(1)} %get-tuple-element.14), channel_id=1, source_target_pairs={{1,0},{2,1},{3,2},{4,3},{5,4},{6,5},{7,6},{8,7},{9,8},{10,9},{11,1... | collective-permute-start | bytes 393224 | tf_op jit(solution)/shard_map/ppermute | solution.py:106
  99.3 9.9 %collective-permute-start.1 = (bf16[2,4,64,128]{3,0,2,1:T(2,128)(2,1)S(1)}, bf16[2,4,64,128]{3,0,2,1:T(2,128)(2,1)S(1)}, u32[]{:S(2)}, u32[]{:S(2)}) collective-permute-start(bf16[2,4,64,128]{3,0,2,1:T(2,128)(2,1)S(1)} %get-tuple-element.15), channel_id=1, source_target_pairs={{31,0},{0,1},{1,2},{2,3},{3,4},{4,5},{5,6},{6,7},{7,8},{8,9},{9,10... | collective-permute-start | bytes 393224 | tf_op jit(solution)/shard_map/ppermute | solution.py:106
  110.0 13.9 %copy-start.12 = (f32[4,2,8,1]{2,1,3,0:T(2,128)}, f32[4,2,8,1]{2,1,3,0:T(2,128)S(1)}, u32[]{:S(2)}) copy-start(f32[4,2,8,1]{2,1,3,0:T(2,128)S(1)} %fusion.41) | copy-start | bytes 772
  110.9 9.8 %collective-permute-start.3 = (bf16[2,4,64,128]{3,0,2,1:T(2,128)(2,1)S(1)}, bf16[2,4,64,128]{3,0,2,1:T(2,128)(2,1)S(1)}, u32[]{:S(2)}, u32[]{:S(2)}) collective-permute-start(bf16[2,4,64,128]{3,0,2,1:T(2,128)(2,1)S(1)} %get-tuple-element.32), channel_id=1, source_target_pairs={{1,0},{2,1},{3,2},{4,3},{5,4},{6,5},{7,6},{8,7},{9,8},{10,9},{11,1... | collective-permute-start | bytes 393224 | tf_op jit(solution)/shard_map/ppermute | solution.py:106
  113.4 10.0 %collective-permute-start.2 = (bf16[2,4,64,128]{3,0,2,1:T(2,128)(2,1)S(1)}, bf16[2,4,64,128]{3,0,2,1:T(2,128)(2,1)S(1)}, u32[]{:S(2)}, u32[]{:S(2)}) collective-permute-start(bf16[2,4,64,128]{3,0,2,1:T(2,128)(2,1)S(1)} %get-tuple-element.32), channel_id=1, source_target_pairs={{31,0},{0,1},{1,2},{2,3},{3,4},{4,5},{5,6},{6,7},{7,8},{8,9},{9,10... | collective-permute-start | bytes 393224 | tf_op jit(solution)/shard_map/ppermute | solution.py:106
  134.8 2.0 copy-start.5
  142.9 10.4 %copy-start.13 = (f32[1,2]{1,0:T(1,128)S(1)}, f32[1,2]{1,0:T(1,128)}, u32[]{:S(2)}) copy-start(f32[1,2]{1,0:T(1,128)} %param.7) | copy-start | bytes 28
  142.9 11.1 %copy-start.2 = (bf16[2,6,192,256]{3,2,0,1:T(8,128)(2,1)S(1)}, bf16[2,6,192,256]{3,2,0,1:T(8,128)(2,1)}, u32[]{:S(2)}) copy-start(bf16[2,6,192,256]{3,2,0,1:T(8,128)(2,1)} %copy-done.1) | copy-start | bytes 3538948
  142.9 67.3 %all-to-all-start.1 = ((bf16[2,6,192,256]{3,0,1,2:T(2,128)(2,1)}), bf16[2,6,192,256]{3,0,1,2:T(2,128)(2,1)}, u32[]{:S(2)}, u32[]{:S(2)}) async-start(bf16[2,6,192,256]{3,0,1,2:T(2,128)(2,1)} %copy.102), calls=%async_computation.1 | async-start | bytes 2359296 | tf_op jit(solution)/shard_map/all_to_all | solution.py:230
  210.2 2.2 %copy-start.4 = (bf16[1,2,192,6,256]{4,2,3,1,0:T(8,128)(2,1)S(1)}, bf16[1,2,192,6,256]{4,2,3,1,0:T(8,128)(2,1)}, u32[]{:S(2)}) copy-start(bf16[1,2,192,6,256]{4,2,3,1,0:T(8,128)(2,1)} %param.6) | copy-start | bytes 3538948

commit v4 on v3

--- a/solution.py
+++ b/solution.py
@@ -1,3 +1,4 @@
+import functools
 import math
 
 import jax
@@ -87,6 +88,57 @@
     return summed.reshape(shape)
 
 
+def exchange_kernel(axis, chunks_ref, out_ref, received, sems):
+    count = chunks_ref.shape[0]
+    me = lax.axis_index(axis)
+    if axis == "fft":
+        place = lambda t: (lax.axis_index("band"), t)
+    else:
+        place = lambda t: (t, lax.axis_index("fft"))
+    barrier = pltpu.get_barrier_semaphore()
+    for k in range(1, count):
+        pl.semaphore_signal(
+            barrier, inc=1, device_id=place((me + k) % count), device_id_type=MESH
+        )
+    pl.semaphore_wait(barrier, count - 1)
+    copies = []
+    for k in range(1, count):
+        target = (me + k) % count
+        copies.append(
+            pltpu.make_async_remote_copy(
+                src_ref=chunks_ref.at[target],
+                dst_ref=received.at[me],
+                send_sem=sems.at[0, k],
+                recv_sem=sems.at[1, k],
+                device_id=place(target),
+                device_id_type=MESH,
+            )
+        )
+    for copy in copies:
+        copy.start()
+    received[me] = chunks_ref[me]
+    for copy in copies:
+        copy.wait()
+    out_ref[...] = received[...]
+
+
+def exchange(chunks, axis, tag):
+    return pl.pallas_call(
+        functools.partial(exchange_kernel, axis),
+        out_shape=jax.ShapeDtypeStruct(chunks.shape, chunks.dtype),
+        in_specs=[pl.BlockSpec(memory_space=pltpu.VMEM)],
+        out_specs=pl.BlockSpec(memory_space=pltpu.VMEM),
+        scratch_shapes=[
+            pltpu.VMEM(chunks.shape, chunks.dtype),
+            pltpu.SemaphoreType.DMA((2, chunks.shape[0])),
+        ],
+        compiler_params=pltpu.CompilerParams(collective_id=tag, has_side_effects=True),
+        cost_estimate=pl.CostEstimate(
+            flops=0, bytes_accessed=4 * chunks.size, transcendentals=0
+        ),
+    )(chunks)
+
+
 def extended_2(shard, sides, width):
     for axis, dim in sides:
         count, length = (lax.axis_size(axis), shard.shape[dim])
@@ -145,10 +197,17 @@
     flattened = coeffs.reshape(2 * size_x, columns * size_z)
     along_x = jnp.dot(table_x, flattened, preferred_element_type=jnp.float32)
     along_x = along_x.reshape(2, size_x, columns, size_z).astype(jnp.bfloat16)
+    outgoing = along_x.reshape(2, pieces, slab_planes, columns, size_z).transpose(1, 0, 2, 3, 4)
+    arrived = exchange(outgoing.reshape(pieces, -1, 128), "fft", 1)
+    arrived = (
+        arrived.reshape(pieces, 2, slab_planes, columns, size_z)
+        .transpose(1, 2, 0, 3, 4)
+        .reshape(2, slab_planes, pieces * columns, size_z)
+    )
     along_y = jnp.einsum(
         "abyk,bxkz->axyz",
         inverse_y,
-        lax.all_to_all(along_x, "fft", split_axis=1, concat_axis=2, tiled=True),
+        arrived,
         preferred_element_type=jnp.float32,
     ).astype(jnp.bfloat16)
     wave_field = jnp.einsum(

time: 215 us -> 223 us (1.037)
  Pallas kernels: 25.9 us -> 98.1 us
  waiting for transfers between devices: 81.7 us -> 29.7 us
  starting transfers between devices: 45.4 us -> 27.1 us
  local copies, waits for them, and re-layouts: 23 us -> 26.6 us
    pallas_call x0 -> x1, Pallas kernels: none -> 72.1 us  [exchange(): pl.pallas_call(functools.partial(exchange_kernel, axis), out_shape=jax.Sh...]
    all_to_all x1 -> x0, waiting for transfers between devices: 54.2 us -> none  [per_device(): lax.all_to_all(along_x, 'fft', split_axis=1, concat_axis=2, tiled=True)]
    all_to_all x1 -> x0, starting transfers between devices: 18.3 us -> none  [per_device(): lax.all_to_all(along_x, 'fft', split_axis=1, concat_axis=2, tiled=True)]
    reshape x0 -> x2, local copies, waits for them, and re-layouts: none -> 3.68 us  [the longest x1 2.32 us: per_device(): arrived.reshape(pieces, 2, slab_planes, columns, size_z)]
    ppermute x4, waiting for transfers between devices: 6.6 us -> 8.94 us  [passed_along(): return lax.ppermute(block, axis, route)]
  transfers between devices with their start and end apart: 6 -> 5, of which waited for: 5 -> 4; matrix products, arithmetic and copies ran while one was open for 8% -> 5% of each run, Pallas kernels for 12% -> 12%
where the time goes in v4:
time: 223 us; the launch traced here: 222 us
  Pallas kernels  98.1 us (44%)
  waiting for transfers between devices  29.7 us (13%)
  starting transfers between devices  27.1 us (12%)
  local copies, waits for them, and re-layouts  26.6 us (12%)
  other arithmetic  24.3 us (11%)
  matrix products  14.7 us (7%)
    pallas_call x1, Pallas kernels, exchange(): pl.pallas_call(functools.partial(exchange_kernel, axis), out_shape=jax.Sh...  72.1 us
    pallas_call x1, Pallas kernels, band_sum(): pl.pallas_call(band_sum_kernel, out_shape=jax.ShapeDtypeStruct(chunks.sha...  26 us
    all_to_all x1, waiting for transfers between devices, per_device(): lax.all_to_all(back_y, 'fft', split_axis=2, concat_axis=1, tiled=True)  20.7 us
    ppermute x4, starting transfers between devices, passed_along(): return lax.ppermute(block, axis, route)  17.5 us
    all_to_all x1, starting transfers between devices, per_device(): lax.all_to_all(back_y, 'fft', split_axis=2, concat_axis=1, tiled=True)  9.57 us
    ppermute x4, waiting for transfers between devices, passed_along(): return lax.ppermute(block, axis, route)  8.94 us
    another operation x6, other arithmetic  7.5 us
  transfers between devices with their start and end apart: 5, of which 4 were waited for; matrix products, arithmetic and copies ran while one was open for 5% of the time, Pallas kernels for 12%

profile of v4, /device:TPU:6, one launch (start us, length us, event | category | flops | bytes accessed | tf_op | source)
XLA Modules:
  0.0 221.8 jit_solution(16944749843644453096)
XLA Ops:
  3.1 1.7 negate_convert_fusion
  4.8 1.8 multiply_convert_fusion
  6.6 1.6 multiply_convert_fusion.2
  13.7 1.2 copy.65
  15.2 1.4 reshape.448.chunks_ref
  16.6 72.1 %shard_map.85 = bf16[32,144,128]{2,1,0:T(8,128)(2,1)} custom-call(bf16[32,144,128]{2,1,0:T(8,128)(2,1)} %reshape.448.chunks_ref), custom_call_target="tpu_custom_call" | custom-call | bytes 2359296 | tf_op jit(solution)/shard_map/pallas_call | solution.py:126
  88.6 2.3 %reshape.449 = bf16[32,2,6,6,256]{4,3,2,1,0:T(8,128)(2,1)S(1)} reshape(bf16[32,144,128]{2,1,0:T(8,128)(2,1)} %shard_map.85) | data formatting | bytes 2359296 | tf_op jit(solution)/shard_map/reshape | solution.py:203
  93.4 2.5 %fusion.17 = bf16[2,6,192,256]{3,2,0,1:T(8,128)(2,1)S(1)} fusion(bf16[2,6,192,256,1]{3,0,2,1,4:T(2,128)(2,1)S(1)} %bitcast.209, bf16[1,2,256,256]{3,2,1,0:T(8,128)(2,1)} %get-tuple-element.18, bf16[1,2,256,256]{3,2,1,0:T(8,128)(2,1)} %get-tuple-element.19, bf16[1,2,192,192]{3,2,1,0:T(8,128)(2,1)S(1)} %copy-done.7, bf16[1,2,192,192]{3,2,1,0:T(8,128)(2,1)S(1)} %copy-done.9), kind=kOutput, calls=%fused_computation.30 | convolution fusion | flops 1059782656 | bytes 3178496 | tf_op jit(solution)/shard_map/abzk,bxyk->axyz/dot_general | solution.py:213
  96.9 1.6 fusion.3
  99.7 2.3 %select_convert_fusion = bf16[2,3,4,64,128]{4,0,3,2,1:T(2,128)(2,1)S(1)} fusion(bf16[2,3,4,64,128]{4,0,3,2,1:T(2,128)(2,1)S(1)} %bitcast.206, bf16[2,3,4,64,128]{4,0,3,2,1:T(2,128)(2,1)S(1)} %bitcast.207, pred[3,4,64]{2,1,0:T(4,128)(4,1)S(1)} %broadcast_compare_fusion.1, pred[3,4,64]{2,1,0:T(4,128)(4,1)S(1)} %get-tuple-element.5), kind=kLoop, calls=%fused_computation.43 | loop fusion | flops 393216 | bytes 1181184 | tf_op jit(solution)/shard_map/convert_element_type | solution.py:243
  102.2 2.9 %collective-permute-start = (bf16[2,4,64,128]{3,0,2,1:T(2,128)(2,1)S(1)}, bf16[2,4,64,128]{3,0,2,1:T(2,128)(2,1)S(1)}, u32[]{:S(2)}, u32[]{:S(2)}) collective-permute-start(bf16[2,4,64,128]{3,0,2,1:T(2,128)(2,1)S(1)} %get-tuple-element.14), channel_id=1, source_target_pairs={{1,0},{2,1},{3,2},{4,3},{5,4},{6,5},{7,6},{8,7},{9,8},{10,9},{11,1... | collective-permute-start | bytes 393224 | tf_op jit(solution)/shard_map/ppermute | solution.py:158
  105.1 5.3 %collective-permute-start.1 = (bf16[2,4,64,128]{3,0,2,1:T(2,128)(2,1)S(1)}, bf16[2,4,64,128]{3,0,2,1:T(2,128)(2,1)S(1)}, u32[]{:S(2)}, u32[]{:S(2)}) collective-permute-start(bf16[2,4,64,128]{3,0,2,1:T(2,128)(2,1)S(1)} %get-tuple-element.15), channel_id=1, source_target_pairs={{31,0},{0,1},{1,2},{2,3},{3,4},{4,5},{5,6},{6,7},{7,8},{8,9},{9,10... | collective-permute-start | bytes 393224 | tf_op jit(solution)/shard_map/ppermute | solution.py:158
  111.6 2.6 %collective-permute-done.1 = bf16[2,4,64,128]{3,0,2,1:T(2,128)(2,1)S(1)} collective-permute-done((bf16[2,4,64,128]{3,0,2,1:T(2,128)(2,1)S(1)}, bf16[2,4,64,128]{3,0,2,1:T(2,128)(2,1)S(1)}, u32[]{:S(2)}, u32[]{:S(2)}) %collective-permute-start.1) | collective-permute-done | bytes 131104 | tf_op jit(solution)/shard_map/ppermute | solution.py:158
  115.9 7.4 %collective-permute-start.3 = (bf16[2,4,64,128]{3,0,2,1:T(2,128)(2,1)S(1)}, bf16[2,4,64,128]{3,0,2,1:T(2,128)(2,1)S(1)}, u32[]{:S(2)}, u32[]{:S(2)}) collective-permute-start(bf16[2,4,64,128]{3,0,2,1:T(2,128)(2,1)S(1)} %get-tuple-element.32), channel_id=1, source_target_pairs={{1,0},{2,1},{3,2},{4,3},{5,4},{6,5},{7,6},{8,7},{9,8},{10,9},{11,1... | collective-permute-start | bytes 393224 | tf_op jit(solution)/shard_map/ppermute | solution.py:158
  123.3 1.9 collective-permute-start.2
  125.9 5.8 %collective-permute-done.2 = bf16[2,4,64,128]{3,0,2,1:T(2,128)(2,1)S(1)} collective-permute-done((bf16[2,4,64,128]{3,0,2,1:T(2,128)(2,1)S(1)}, bf16[2,4,64,128]{3,0,2,1:T(2,128)(2,1)S(1)}, u32[]{:S(2)}, u32[]{:S(2)}) %collective-permute-start.2) | collective-permute-done | bytes 131104 | tf_op jit(solution)/shard_map/ppermute | solution.py:158
  132.2 3.5 %broadcast_select_fusion.1 = (f32[2,768,1,128]{3,0,1,2:T(2,128)S(1)}, f32[2,768,1,128]{3,0,1,2:T(2,128)S(1)}) fusion(f32[2,768,1,128]{3,0,1,2:T(2,128)S(1)} %bitcast.204, pred[768]{0:T(1024)(128)(4,1)S(1)} %get-tuple-element.28, pred[768]{0:T(1024)(128)(4,1)S(1)} %get-tuple-element.29), kind=kLoop, calls=%fused_computation.45 | loop fusion | flops 393216 | bytes 2360832 | tf_op jit(solution)/shard_map/jit(_where)/select_n | solution.py:261
  135.7 1.9 pad_maximum_fusion
  137.6 2.5 %copy.79 = f32[2,768,2,128]{1,3,2,0:T(8,128)S(1)} copy(f32[2,768,2,128]{3,0,1,2:T(2,128)} %pad_maximum_fusion) | data formatting | bytes 3145728 | tf_op jit(solution)/shard_map/concatenate | solution.py:260
  140.3 2.5 %convolution_bitcast_fusion = f32[4,1152,256]{1,2,0:T(8,128)S(1)} fusion(s32[768]{0:T(1024)S(1)} %add_select_fusion.4, pred[768]{0:T(1024)(128)(4,1)S(1)} %fusion.79, bf16[2,768,256]{1,2,0:T(8,128)(2,1)S(1)} %get-tuple-element.3, bf16[2,768,256]{1,2,0:T(8,128)(2,1)S(1)} %get-tuple-element.4), kind=kOutput, calls=%fused_computation | convolution fusion | flops 1814495232 | bytes 6295296 | tf_op jit(solution)/shard_map/er,cez->crz/dot_general | solution.py:265
  143.0 2.0 copy.80
  145.0 3.9 %fusion.19 = bf16[2,6,192,256]{3,2,0,1:T(8,128)(2,1)S(1)} fusion(f32[2,6,192,256]{3,2,1,0:T(8,128)} %bitcast.205, bf16[2,6,192,256]{3,2,0,1:T(8,128)(2,1)} %copy-done.1, f32[6,192,256]{2,1,0:T(8,128)} %convert_element_type.195, bf16[1,2,256,256]{3,2,1,0:T(8,128)(2,1)} %get-tuple-element.17, bf16[1,2,256,256]{3,2,1,0:T(8,128)(2,1)} %get-tuple-element.16, ...), kind=kOutput, calls=%fused_computation.32 | convolution fusion | flops 1062141952 | bytes 6717440 | tf_op jit(solution)/shard_map/abyk,bxkz->axyz/dot_general | solution.py:283
  148.9 2.2 %copy.82 = bf16[2,6,192,256]{3,0,1,2:T(2,128)(2,1)} copy(bf16[2,6,192,256]{3,2,0,1:T(8,128)(2,1)S(1)} %fusion.19) | data formatting | bytes 2359296 | tf_op jit(solution)/shard_map/convert_element_type | solution.py:285
  151.1 9.6 %all-to-all-start = ((bf16[2,6,192,256]{3,0,1,2:T(2,128)(2,1)}), bf16[2,6,192,256]{3,0,1,2:T(2,128)(2,1)}, u32[]{:S(2)}, u32[]{:S(2)}) async-start(bf16[2,6,192,256]{3,0,1,2:T(2,128)(2,1)} %copy.82), calls=%async_computation | async-start | bytes 2359296 | tf_op jit(solution)/shard_map/all_to_all | solution.py:289
  160.7 1.2 slice_convert_fusion
  162.0 1.3 reshape.460
  165.1 3.6 %fusion.22.part_ref = bf16[16,144,128]{2,1,0:T(8,128)(2,1)} fusion(f32[16,144,128]{2,1,0:T(8,128)S(1)} %reshape.460, f32[16,144,128]{2,1,0:T(8,128)} %reshape.461, f32[]{:T(128)} %bitcast.78, f32[]{:T(128)} %bitcast.77), kind=kLoop, calls=%fused_computation.35 | loop fusion | flops 1769472 | bytes 2949128 | tf_op jit(solution)/shard_map/convert_element_type | solution.py:220
  168.6 26.0 %shard_map.86 = bf16[16,144,128]{2,1,0:T(8,128)(2,1)} custom-call(bf16[16,144,128]{2,1,0:T(8,128)(2,1)} %fusion.22.part_ref), custom_call_target="tpu_custom_call" | custom-call | flops 294912 | bytes 1769472 | tf_op jit(solution)/shard_map/pallas_call | solution.py:73
  194.6 2.0 reshape.456
  197.0 20.7 %all-to-all-done = bf16[2,6,192,256]{3,0,1,2:T(2,128)(2,1)} async-done(((bf16[2,6,192,256]{3,0,1,2:T(2,128)(2,1)}), bf16[2,6,192,256]{3,0,1,2:T(2,128)(2,1)}, u32[]{:S(2)}, u32[]{:S(2)}) %all-to-all-start) | async-done | bytes 1179680 | tf_op jit(solution)/shard_map/all_to_all | solution.py:289
  217.7 2.2 copy.84
  219.9 1.9 fusion.20
  (91 shorter events, 19.2 us)
Async XLA Ops:
  0.6 113.6 %copy-start = (bf16[4,8,64,128]{3,2,1,0:T(8,128)(2,1)S(1)}, bf16[4,8,64,128]{3,2,1,0:T(8,128)(2,1)}, u32[]{:S(2)}) copy-start(bf16[4,8,64,128]{3,2,1,0:T(8,128)(2,1)} %param.9) | copy-start | bytes 1572868
  0.6 7.6 %copy-start.16 = (s32[128,64]{0,1:T(8,128)S(1)}, s32[128,64]{0,1:T(8,128)}, u32[]{:S(2)}) copy-start(s32[128,64]{0,1:T(8,128)} %param.11) | copy-start | bytes 98308
  9.6 0.7 copy-start.6
  9.6 0.7 copy-start.8
  9.6 1.5 copy-start.3
  91.0 1.3 copy-start.11
  91.0 1.3 copy-start.12
  91.0 1.3 copy-start.13
  91.0 1.3 copy-start.14
  91.0 1.3 copy-start.15
  92.2 1.1 copy-start.7
  92.3 1.2 copy-start.9
  95.9 1.0 copy-start.1
  99.0 11.5 %copy-start.17 = (f32[8,8]{1,0:T(8,128)S(1)}, f32[8,8]{1,0:T(8,128)}, u32[]{:S(2)}) copy-start(f32[8,8]{1,0:T(8,128)} %param.10) | copy-start | bytes 772
  99.0 11.5 %copy-start.10 = (bf16[6,192,256]{2,1,0:T(8,128)(2,1)S(1)}, bf16[6,192,256]{2,1,0:T(8,128)(2,1)}, u32[]{:S(2)}) copy-start(bf16[6,192,256]{2,1,0:T(8,128)(2,1)} %param.8) | copy-start | bytes 1769476
  102.2 9.5 %collective-permute-start = (bf16[2,4,64,128]{3,0,2,1:T(2,128)(2,1)S(1)}, bf16[2,4,64,128]{3,0,2,1:T(2,128)(2,1)S(1)}, u32[]{:S(2)}, u32[]{:S(2)}) collective-permute-start(bf16[2,4,64,128]{3,0,2,1:T(2,128)(2,1)S(1)} %get-tuple-element.14), channel_id=1, source_target_pairs={{1,0},{2,1},{3,2},{4,3},{5,4},{6,5},{7,6},{8,7},{9,8},{10,9},{11,1... | collective-permute-start | bytes 393224 | tf_op jit(solution)/shard_map/ppermute | solution.py:158
  105.1 9.1 %collective-permute-start.1 = (bf16[2,4,64,128]{3,0,2,1:T(2,128)(2,1)S(1)}, bf16[2,4,64,128]{3,0,2,1:T(2,128)(2,1)S(1)}, u32[]{:S(2)}, u32[]{:S(2)}) collective-permute-start(bf16[2,4,64,128]{3,0,2,1:T(2,128)(2,1)S(1)} %get-tuple-element.15), channel_id=1, source_target_pairs={{31,0},{0,1},{1,2},{2,3},{3,4},{4,5},{5,6},{6,7},{7,8},{8,9},{9,10... | collective-permute-start | bytes 393224 | tf_op jit(solution)/shard_map/ppermute | solution.py:158
  115.0 17.1 %copy-start.18 = (f32[4,2,8,1]{2,1,3,0:T(2,128)}, f32[4,2,8,1]{2,1,3,0:T(2,128)S(1)}, u32[]{:S(2)}) copy-start(f32[4,2,8,1]{2,1,3,0:T(2,128)S(1)} %fusion.41) | copy-start | bytes 772
  115.9 9.9 %collective-permute-start.3 = (bf16[2,4,64,128]{3,0,2,1:T(2,128)(2,1)S(1)}, bf16[2,4,64,128]{3,0,2,1:T(2,128)(2,1)S(1)}, u32[]{:S(2)}, u32[]{:S(2)}) collective-permute-start(bf16[2,4,64,128]{3,0,2,1:T(2,128)(2,1)S(1)} %get-tuple-element.32), channel_id=1, source_target_pairs={{1,0},{2,1},{3,2},{4,3},{5,4},{6,5},{7,6},{8,7},{9,8},{10,9},{11,1... | collective-permute-start | bytes 393224 | tf_op jit(solution)/shard_map/ppermute | solution.py:158
  123.3 8.4 %collective-permute-start.2 = (bf16[2,4,64,128]{3,0,2,1:T(2,128)(2,1)S(1)}, bf16[2,4,64,128]{3,0,2,1:T(2,128)(2,1)S(1)}, u32[]{:S(2)}, u32[]{:S(2)}) collective-permute-start(bf16[2,4,64,128]{3,0,2,1:T(2,128)(2,1)S(1)} %get-tuple-element.32), channel_id=1, source_target_pairs={{31,0},{0,1},{1,2},{2,3},{3,4},{4,5},{5,6},{6,7},{7,8},{8,9},{9,10... | collective-permute-start | bytes 393224 | tf_op jit(solution)/shard_map/ppermute | solution.py:158
  143.0 2.0 copy-start.5
  151.1 9.6 %copy-start.2 = (bf16[2,6,192,256]{3,2,0,1:T(8,128)(2,1)S(1)}, bf16[2,6,192,256]{3,2,0,1:T(8,128)(2,1)}, u32[]{:S(2)}) copy-start(bf16[2,6,192,256]{3,2,0,1:T(8,128)(2,1)} %copy-done.1) | copy-start | bytes 3538948
  151.1 66.6 %all-to-all-start = ((bf16[2,6,192,256]{3,0,1,2:T(2,128)(2,1)}), bf16[2,6,192,256]{3,0,1,2:T(2,128)(2,1)}, u32[]{:S(2)}, u32[]{:S(2)}) async-start(bf16[2,6,192,256]{3,0,1,2:T(2,128)(2,1)} %copy.82), calls=%async_computation | async-start | bytes 2359296 | tf_op jit(solution)/shard_map/all_to_all | solution.py:289
  163.3 1.1 copy-start.19
  217.7 2.2 copy-start.4

commit v5 on v3

--- a/solution.py
+++ b/solution.py
@@ -87,6 +87,60 @@
     return summed.reshape(shape)
 
 
+def swap_kernel(to_left_ref, to_right_ref, from_right_ref, from_left_ref, landed, sems):
+    count = lax.axis_size("fft")
+    me = lax.axis_index("fft")
+    band = lax.axis_index("band")
+    left = (me + count - 1) % count
+    right = (me + 1) % count
+    barrier = pltpu.get_barrier_semaphore()
+    for neighbour in (left, right):
+        pl.semaphore_signal(barrier, inc=1, device_id=(band, neighbour), device_id_type=MESH)
+    pl.semaphore_wait(barrier, 2)
+    copies = [
+        pltpu.make_async_remote_copy(
+            src_ref=to_left_ref,
+            dst_ref=landed.at[0],
+            send_sem=sems.at[0],
+            recv_sem=sems.at[1],
+            device_id=(band, left),
+            device_id_type=MESH,
+        ),
+        pltpu.make_async_remote_copy(
+            src_ref=to_right_ref,
+            dst_ref=landed.at[1],
+            send_sem=sems.at[2],
+            recv_sem=sems.at[3],
+            device_id=(band, right),
+            device_id_type=MESH,
+        ),
+    ]
+    for copy in copies:
+        copy.start()
+    for copy in copies:
+        copy.wait()
+    from_right_ref[...] = landed[0]
+    from_left_ref[...] = landed[1]
+
+
+def neighbour_swap(to_left, to_right, tag):
+    shape = jax.ShapeDtypeStruct(to_left.shape, to_left.dtype)
+    return pl.pallas_call(
+        swap_kernel,
+        out_shape=(shape, shape),
+        in_specs=[pl.BlockSpec(memory_space=pltpu.VMEM)] * 2,
+        out_specs=(pl.BlockSpec(memory_space=pltpu.VMEM),) * 2,
+        scratch_shapes=[
+            pltpu.VMEM((2,) + to_left.shape, to_left.dtype),
+            pltpu.SemaphoreType.DMA((4,)),
+        ],
+        compiler_params=pltpu.CompilerParams(collective_id=tag, has_side_effects=True),
+        cost_estimate=pl.CostEstimate(
+            flops=0, bytes_accessed=4 * to_left.size, transcendentals=0
+        ),
+    )(to_left, to_right)
+
+
 def extended_2(shard, sides, width):
     for axis, dim in sides:
         count, length = (lax.axis_size(axis), shard.shape[dim])
@@ -182,8 +236,7 @@
     for q in range(zblocks):
         picked = jnp.where(half_of == q, picked_rows[:, :, q], picked)
     picked = picked.astype(jnp.bfloat16).reshape(2, 3, atom_dev, -1, block_cells)
-    from_right = passed_along(picked[:, 0], "fft", -1)
-    from_left = passed_along(picked[:, 2], "fft", 1)
+    from_right, from_left = neighbour_swap(picked[:, 0], picked[:, 2], 2)
     gathered = picked[:, 1] + from_right + from_left
     projections_own = jnp.einsum(
         "ajsk,bask->abj", projectors, gathered, preferred_element_type=jnp.float32
@@ -193,8 +246,9 @@
         "ajsk,abj->bask", projectors.astype(jnp.float32), energy, precision=lax.Precision.HIGHEST
     )
     spread_sent = spread.astype(jnp.bfloat16)
-    spread_left = passed_along(spread_sent, "fft", 1).astype(jnp.float32)
-    spread_right = passed_along(spread_sent, "fft", -1).astype(jnp.float32)
+    spread_right, spread_left = neighbour_swap(spread_sent, spread_sent, 3)
+    spread_right = spread_right.astype(jnp.float32)
+    spread_left = spread_left.astype(jnp.float32)
     spread_all = jnp.stack([spread_left, spread, spread_right], axis=1).reshape(
         2, -1, 1, block_cells
     )

time: 215 us -> 211 us (0.981)
  Pallas kernels: 25.9 us -> 49.5 us
  starting transfers between devices: 45.4 us -> 26.5 us
  waiting for transfers between devices: 81.7 us -> 76 us
  other arithmetic: 22.3 us -> 18.9 us
    pallas_call x0 -> x2, Pallas kernels: none -> 23 us  [neighbour_swap(): pl.pallas_call(swap_kernel, out_shape=(shape, shape), in_specs=[pl.BlockS...]
    ppermute x4 -> x0, starting transfers between devices: 16.7 us -> none  [passed_along(): return lax.ppermute(block, axis, route)]
    ppermute x4 -> x0, waiting for transfers between devices: 6.6 us -> none  [passed_along(): return lax.ppermute(block, axis, route)]
    select_n x1, other arithmetic: 3.54 us -> 0.27 us  [per_device(): jnp.where(half_of[..., None] == q, spread_all, 0.0)]
    all_to_all x1, waiting for transfers between devices: 20.9 us -> 23.2 us  [per_device(): lax.all_to_all(back_y, 'fft', split_axis=2, concat_axis=1, tiled=True)]
    all_to_all x1, starting transfers between devices: 10.3 us -> 8.17 us  [per_device(): lax.all_to_all(back_y, 'fft', split_axis=2, concat_axis=1, tiled=True)]
  transfers between devices with their start and end apart: 6 -> 2, of which waited for: 5 -> 2; matrix products, arithmetic and copies ran while one was open for 8% -> 8% of each run, Pallas kernels for 12% -> 13%
where the time goes in v5:
time: 211 us; the launch traced here: 210 us
  waiting for transfers between devices  76 us (36%)
  Pallas kernels  49.5 us (23%)
  starting transfers between devices  26.5 us (13%)
  local copies, waits for them, and re-layouts  23.2 us (11%)
  other arithmetic  18.9 us (9%)
  matrix products  14.7 us (7%)
    all_to_all x1, waiting for transfers between devices, per_device(): lax.all_to_all(along_x, 'fft', split_axis=1, concat_axis=2, tiled=True)  52.8 us
    pallas_call x1, Pallas kernels, band_sum(): pl.pallas_call(band_sum_kernel, out_shape=jax.ShapeDtypeStruct(chunks.sha...  26.6 us
    all_to_all x1, waiting for transfers between devices, per_device(): lax.all_to_all(back_y, 'fft', split_axis=2, concat_axis=1, tiled=True)  23.2 us
    pallas_call x2, Pallas kernels, neighbour_swap(): pl.pallas_call(swap_kernel, out_shape=(shape, shape), in_specs=[pl.BlockS...  23 us
    all_to_all x1, starting transfers between devices, per_device(): lax.all_to_all(along_x, 'fft', split_axis=1, concat_axis=2, tiled=True)  18.3 us
    all_to_all x1, starting transfers between devices, per_device(): lax.all_to_all(back_y, 'fft', split_axis=2, concat_axis=1, tiled=True)  8.17 us
    another operation x6, other arithmetic  5.67 us
  transfers between devices with their start and end apart: 2, of which 2 were waited for; matrix products, arithmetic and copies ran while one was open for 8% of the time, Pallas kernels for 13%

profile of v5, /device:TPU:6, one launch (start us, length us, event | category | flops | bytes accessed | tf_op | source)
XLA Modules:
  0.0 209.9 jit_solution(9172567726897597456)
XLA Ops:
  7.9 2.2 %copy.101 = bf16[2,192,6,256]{3,0,2,1:T(2,128)(2,1)} copy(bf16[2,192,6,256]{3,1,2,0:T(8,128)(2,1)S(1)} %convolution_convert_fusion) | data formatting | bytes 2359296 | tf_op jit(solution)/shard_map/convert_element_type | solution.py:201
  10.1 18.3 %all-to-all-start = ((bf16[2,192,6,256]{3,0,2,1:T(2,128)(2,1)}), bf16[2,192,6,256]{3,0,2,1:T(2,128)(2,1)S(1)}, u32[]{:S(2)}, u32[]{:S(2)}) async-start(bf16[2,192,6,256]{3,0,2,1:T(2,128)(2,1)} %copy.101), calls=%async_computation | async-start | bytes 2359296 | tf_op jit(solution)/shard_map/all_to_all | solution.py:205
  29.2 1.1 convert_element_type.195
  30.4 1.0 multiply_convert_fusion.2
  31.4 1.0 negate_convert_fusion
  32.4 1.3 multiply_convert_fusion
  33.7 1.0 fusion.52
  34.7 52.8 %all-to-all-done = bf16[2,192,6,256]{3,0,2,1:T(2,128)(2,1)S(1)} async-done(((bf16[2,192,6,256]{3,0,2,1:T(2,128)(2,1)}), bf16[2,192,6,256]{3,0,2,1:T(2,128)(2,1)S(1)}, u32[]{:S(2)}, u32[]{:S(2)}) %all-to-all-start) | async-done | bytes 1179680 | tf_op jit(solution)/shard_map/all_to_all | solution.py:205
  88.5 2.5 %fusion.17 = bf16[2,6,192,256]{3,2,0,1:T(8,128)(2,1)S(1)} fusion(bf16[2,6,192,256,1]{3,0,2,1,4:T(2,128)(2,1)S(1)} %bitcast.210, bf16[1,2,256,256]{3,2,1,0:T(8,128)(2,1)} %get-tuple-element.26, bf16[1,2,256,256]{3,2,1,0:T(8,128)(2,1)} %get-tuple-element.27, bf16[1,2,192,192]{3,2,1,0:T(8,128)(2,1)S(1)} %copy-done.7, bf16[1,2,192,192]{3,2,1,0:T(8,128)(2,1)} %copy-done.8), kind=kOutput, calls=%fused_computation.30 | convolution fusion | flops 1059782656 | bytes 3178496 | tf_op jit(solution)/shard_map/abzk,bxyk->axyz/dot_general | solution.py:208
  91.1 0.9 copy-done.1
  92.0 1.6 fusion.3
  95.1 11.8 %shard_map.85 = (bf16[2,4,64,128]{3,2,1,0:T(8,128)(2,1)}, bf16[2,4,64,128]{3,2,1,0:T(8,128)(2,1)}) custom-call(bf16[2,4,64,128]{3,2,1,0:T(8,128)(2,1)} %get-tuple-element.23.to_left_ref, bf16[2,4,64,128]{3,2,1,0:T(8,128)(2,1)} %get-tuple-element.22.to_right_ref), custom_call_target="tpu_custom_call" | custom-call | bytes 262144 | tf_op jit(solution)/shard_map/pallas_call | solution.py:128
  106.9 1.0 fusion.75
  110.1 11.2 %shard_map.86 = (bf16[2,4,64,128]{3,2,1,0:T(8,128)(2,1)}, bf16[2,4,64,128]{3,2,1,0:T(8,128)(2,1)}) custom-call(bf16[2,4,64,128]{3,2,1,0:T(8,128)(2,1)} %bitcast.208, bf16[2,4,64,128]{3,2,1,0:T(8,128)(2,1)} %bitcast.209), custom_call_target="tpu_custom_call" | custom-call | bytes 262144 | tf_op jit(solution)/shard_map/pallas_call | solution.py:128
  121.3 0.9 bitcast_convert_fusion.6
  122.3 0.9 bitcast_convert_fusion.7
  123.6 1.3 pad_maximum_fusion
  124.9 1.9 copy.119
  126.9 2.5 %convolution_bitcast_fusion = f32[4,1152,256]{1,2,0:T(8,128)S(1)} fusion(s32[768]{0:T(1024)S(1)} %add_select_fusion.4, pred[768]{0:T(1024)(128)(4,1)S(1)} %fusion.80, bf16[2,768,256]{1,2,0:T(8,128)(2,1)S(1)} %get-tuple-element.11, bf16[2,768,256]{1,2,0:T(8,128)(2,1)S(1)} %get-tuple-element.12), kind=kOutput, calls=%fused_computation | convolution fusion | flops 1814495232 | bytes 6295296 | tf_op jit(solution)/shard_map/er,cez->crz/dot_general | solution.py:260
  129.7 2.0 copy.120
  131.6 3.9 %fusion.19 = bf16[2,6,192,256]{3,2,0,1:T(8,128)(2,1)S(1)} fusion(f32[2,6,192,256]{3,2,1,0:T(8,128)} %bitcast.205, bf16[2,6,192,256]{3,2,0,1:T(8,128)(2,1)} %copy-done.1, f32[6,192,256]{2,1,0:T(8,128)} %convert_element_type.195, bf16[1,2,256,256]{3,2,1,0:T(8,128)(2,1)} %get-tuple-element.25, bf16[1,2,256,256]{3,2,1,0:T(8,128)(2,1)} %get-tuple-element.24, ...), kind=kOutput, calls=%fused_computation.32 | convolution fusion | flops 1062141952 | bytes 6717440 | tf_op jit(solution)/shard_map/abyk,bxkz->axyz/dot_general | solution.py:278
  135.5 2.2 %copy.122 = bf16[2,6,192,256]{3,0,1,2:T(2,128)(2,1)} copy(bf16[2,6,192,256]{3,2,0,1:T(8,128)(2,1)S(1)} %fusion.19) | data formatting | bytes 2359296 | tf_op jit(solution)/shard_map/convert_element_type | solution.py:280
  137.8 8.2 %all-to-all-start.1 = ((bf16[2,6,192,256]{3,0,1,2:T(2,128)(2,1)}), bf16[2,6,192,256]{3,0,1,2:T(2,128)(2,1)}, u32[]{:S(2)}, u32[]{:S(2)}) async-start(bf16[2,6,192,256]{3,0,1,2:T(2,128)(2,1)} %copy.122), calls=%async_computation.1 | async-start | bytes 2359296 | tf_op jit(solution)/shard_map/all_to_all | solution.py:284
  146.7 1.2 slice_convert_fusion
  147.9 1.3 reshape.444
  149.3 1.1 reshape.445
  150.4 3.5 %fusion.22.part_ref = bf16[16,144,128]{2,1,0:T(8,128)(2,1)} fusion(f32[16,144,128]{2,1,0:T(8,128)S(1)} %reshape.444, f32[16,144,128]{2,1,0:T(8,128)} %reshape.445, f32[]{:T(128)} %bitcast.77, f32[]{:T(128)} %bitcast.76), kind=kLoop, calls=%fused_computation.35 | loop fusion | flops 1769472 | bytes 2949128 | tf_op jit(solution)/shard_map/convert_element_type | solution.py:215
  154.1 26.6 %shard_map.87 = bf16[16,144,128]{2,1,0:T(8,128)(2,1)} custom-call(bf16[16,144,128]{2,1,0:T(8,128)(2,1)} %fusion.22.part_ref), custom_call_target="tpu_custom_call" | custom-call | flops 294912 | bytes 1769472 | tf_op jit(solution)/shard_map/pallas_call | solution.py:72
  180.7 2.0 reshape.440
  182.7 23.2 %all-to-all-done.1 = bf16[2,6,192,256]{3,0,1,2:T(2,128)(2,1)} async-done(((bf16[2,6,192,256]{3,0,1,2:T(2,128)(2,1)}), bf16[2,6,192,256]{3,0,1,2:T(2,128)(2,1)}, u32[]{:S(2)}, u32[]{:S(2)}) %all-to-all-start.1) | async-done | bytes 1179680 | tf_op jit(solution)/shard_map/all_to_all | solution.py:284
  205.9 2.2 %copy.124 = bf16[2,32,6,6,256]{4,0,3,2,1:T(2,128)(2,1)S(1)} copy(bf16[2,32,6,6,256]{4,0,2,3,1:T(2,128)(2,1)} %bitcast.69) | data formatting | bytes 2359296 | tf_op jit(solution)/shard_map/all_to_all | solution.py:284
  208.1 1.9 fusion.20
  (75 shorter events, 14.3 us)
Async XLA Ops:
  0.6 107.3 %copy-start = (bf16[4,8,64,128]{3,2,1,0:T(8,128)(2,1)S(1)}, bf16[4,8,64,128]{3,2,1,0:T(8,128)(2,1)}, u32[]{:S(2)}) copy-start(bf16[4,8,64,128]{3,2,1,0:T(8,128)(2,1)} %param.9) | copy-start | bytes 1572868
  3.8 0.7 copy-start.6
  3.8 0.8 copy-start.8
  3.8 1.5 copy-start.3
  10.1 18.4 %copy-start.10 = (s32[128,64]{0,1:T(8,128)S(1)}, s32[128,64]{0,1:T(8,128)}, u32[]{:S(2)}) copy-start(s32[128,64]{0,1:T(8,128)} %param.11) | copy-start | bytes 98308
  10.1 19.0 %copy-start.11 = (f32[8,8]{1,0:T(8,128)S(1)}, f32[8,8]{1,0:T(8,128)}, u32[]{:S(2)}) copy-start(f32[8,8]{1,0:T(8,128)} %param.10) | copy-start | bytes 772
  10.1 19.1 %copy-start.9 = (bf16[6,192,256]{2,1,0:T(8,128)(2,1)S(1)}, bf16[6,192,256]{2,1,0:T(8,128)(2,1)}, u32[]{:S(2)}) copy-start(bf16[6,192,256]{2,1,0:T(8,128)(2,1)} %param.8) | copy-start | bytes 1769476
  10.1 77.4 %all-to-all-start = ((bf16[2,192,6,256]{3,0,2,1:T(2,128)(2,1)}), bf16[2,192,6,256]{3,0,2,1:T(2,128)(2,1)S(1)}, u32[]{:S(2)}, u32[]{:S(2)}) async-start(bf16[2,192,6,256]{3,0,2,1:T(2,128)(2,1)} %copy.101), calls=%async_computation | async-start | bytes 2359296 | tf_op jit(solution)/shard_map/all_to_all | solution.py:205
  87.5 0.9 copy-start.7
  91.0 1.0 copy-start.1
  108.5 13.7 %copy-start.12 = (f32[4,2,8,1]{2,1,3,0:T(2,128)}, f32[4,2,8,1]{2,1,3,0:T(2,128)S(1)}, u32[]{:S(2)}) copy-start(f32[4,2,8,1]{2,1,3,0:T(2,128)S(1)} %fusion.42) | copy-start | bytes 772
  129.7 2.0 copy-start.5
  137.8 8.2 %copy-start.13 = (f32[1,2]{1,0:T(1,128)S(1)}, f32[1,2]{1,0:T(1,128)}, u32[]{:S(2)}) copy-start(f32[1,2]{1,0:T(1,128)} %param.7) | copy-start | bytes 28
  137.8 8.9 %copy-start.2 = (bf16[2,6,192,256]{3,2,0,1:T(8,128)(2,1)S(1)}, bf16[2,6,192,256]{3,2,0,1:T(8,128)(2,1)}, u32[]{:S(2)}) copy-start(bf16[2,6,192,256]{3,2,0,1:T(8,128)(2,1)} %copy-done.1) | copy-start | bytes 3538948
  137.8 68.1 %all-to-all-start.1 = ((bf16[2,6,192,256]{3,0,1,2:T(2,128)(2,1)}), bf16[2,6,192,256]{3,0,1,2:T(2,128)(2,1)}, u32[]{:S(2)}, u32[]{:S(2)}) async-start(bf16[2,6,192,256]{3,0,1,2:T(2,128)(2,1)} %copy.122), calls=%async_computation.1 | async-start | bytes 2359296 | tf_op jit(solution)/shard_map/all_to_all | solution.py:284
  205.9 2.2 %copy-start.4 = (bf16[1,2,192,6,256]{4,2,3,1,0:T(8,128)(2,1)S(1)}, bf16[1,2,192,6,256]{4,2,3,1,0:T(8,128)(2,1)}, u32[]{:S(2)}) copy-start(bf16[1,2,192,6,256]{4,2,3,1,0:T(8,128)(2,1)} %param.6) | copy-start | bytes 3538948

commit v6 on v5

--- a/solution.py
+++ b/solution.py
@@ -141,6 +141,102 @@
     )(to_left, to_right)
 
 
+def halo_kernel(
+    to_left_ref, own_ref, to_right_ref, beta_ref, coupled_ref,
+    proj_ref, spread_ref, spread_right_ref, spread_left_ref,
+    landed, outgoing, landed_spread, sems,
+):
+    count = lax.axis_size("fft")
+    me = lax.axis_index("fft")
+    band = lax.axis_index("band")
+    left = (me + count - 1) % count
+    right = (me + 1) % count
+    barrier = pltpu.get_barrier_semaphore()
+    for neighbour in (left, right):
+        pl.semaphore_signal(barrier, inc=1, device_id=(band, neighbour), device_id_type=MESH)
+    pl.semaphore_wait(barrier, 2)
+
+    def swap(first, second, into, base):
+        copies = [
+            pltpu.make_async_remote_copy(
+                src_ref=first,
+                dst_ref=into.at[0],
+                send_sem=sems.at[base],
+                recv_sem=sems.at[base + 1],
+                device_id=(band, left),
+                device_id_type=MESH,
+            ),
+            pltpu.make_async_remote_copy(
+                src_ref=second,
+                dst_ref=into.at[1],
+                send_sem=sems.at[base + 2],
+                recv_sem=sems.at[base + 3],
+                device_id=(band, right),
+                device_id_type=MESH,
+            ),
+        ]
+        for copy in copies:
+            copy.start()
+        for copy in copies:
+            copy.wait()
+
+    swap(to_left_ref, to_right_ref, landed, 0)
+    atoms, nproj = beta_ref.shape[0], beta_ref.shape[1]
+    lane = lax.broadcasted_iota(jnp.int32, (1, 128), 1)
+    for c in range(2):
+        for a in range(atoms):
+            block = (
+                own_ref[c, a].astype(jnp.float32)
+                + landed[0, c, a].astype(jnp.float32)
+                + landed[1, c, a].astype(jnp.float32)
+            )
+            sums = []
+            row = jnp.zeros((1, 128), jnp.float32)
+            for j in range(nproj):
+                value = jnp.sum(beta_ref[a, j].astype(jnp.float32) * block, keepdims=True)
+                sums.append(value)
+                row = row + jnp.where(lane == j, value, 0.0)
+            proj_ref[pl.ds(a * 2 + c, 1), :] = row
+            spread = jnp.zeros(block.shape, jnp.float32)
+            for i in range(nproj):
+                energy = sums[0] * coupled_ref[i, 0]
+                for j in range(1, nproj):
+                    energy = energy + sums[j] * coupled_ref[i, j]
+                spread = spread + beta_ref[a, i].astype(jnp.float32) * energy
+            spread_ref[c, a] = spread
+            outgoing[c, a] = spread.astype(outgoing.dtype)
+    swap(outgoing, outgoing, landed_spread, 4)
+    spread_right_ref[...] = landed_spread[0]
+    spread_left_ref[...] = landed_spread[1]
+
+
+def halo_exchange(to_left, own, to_right, projectors, coupled):
+    atoms = projectors.shape[0]
+    half = jax.ShapeDtypeStruct(own.shape, jnp.bfloat16)
+    vmem = pl.BlockSpec(memory_space=pltpu.VMEM)
+    return pl.pallas_call(
+        halo_kernel,
+        out_shape=(
+            jax.ShapeDtypeStruct((2 * atoms, 128), jnp.float32),
+            jax.ShapeDtypeStruct(own.shape, jnp.float32),
+            half,
+            half,
+        ),
+        in_specs=[vmem, vmem, vmem, vmem, pl.BlockSpec(memory_space=pltpu.SMEM)],
+        out_specs=(vmem, vmem, vmem, vmem),
+        scratch_shapes=[
+            pltpu.VMEM((2,) + own.shape, jnp.bfloat16),
+            pltpu.VMEM(own.shape, jnp.bfloat16),
+            pltpu.VMEM((2,) + own.shape, jnp.bfloat16),
+            pltpu.SemaphoreType.DMA((8,)),
+        ],
+        compiler_params=pltpu.CompilerParams(collective_id=2, has_side_effects=True),
+        cost_estimate=pl.CostEstimate(
+            flops=8 * projectors.size, bytes_accessed=16 * own.size, transcendentals=0
+        ),
+    )(to_left, own, to_right, projectors, coupled)
+
+
 def extended_2(shard, sides, width):
     for axis, dim in sides:
         count, length = (lax.axis_size(axis), shard.shape[dim])
@@ -236,17 +332,10 @@
     for q in range(zblocks):
         picked = jnp.where(half_of == q, picked_rows[:, :, q], picked)
     picked = picked.astype(jnp.bfloat16).reshape(2, 3, atom_dev, -1, block_cells)
-    from_right, from_left = neighbour_swap(picked[:, 0], picked[:, 2], 2)
-    gathered = picked[:, 1] + from_right + from_left
-    projections_own = jnp.einsum(
-        "ajsk,bask->abj", projectors, gathered, preferred_element_type=jnp.float32
-    )
-    energy = jnp.einsum("ij,abj->abi", coupled, projections_own, precision=lax.Precision.HIGHEST)
-    spread = jnp.einsum(
-        "ajsk,abj->bask", projectors.astype(jnp.float32), energy, precision=lax.Precision.HIGHEST
-    )
-    spread_sent = spread.astype(jnp.bfloat16)
-    spread_right, spread_left = neighbour_swap(spread_sent, spread_sent, 3)
+    proj_rows, spread, spread_right, spread_left = halo_exchange(
+        picked[:, 0], picked[:, 1], picked[:, 2], projectors, coupled
+    )
+    projections_own = proj_rows[:, :nproj_count].reshape(atom_dev, 2, nproj_count)
     spread_right = spread_right.astype(jnp.float32)
     spread_left = spread_left.astype(jnp.float32)
     spread_all = jnp.stack([spread_left, spread, spread_right], axis=1).reshape(

time: 211 us -> 201 us (0.953)
  waiting for transfers between devices: 76 us -> 80.3 us
  Pallas kernels: 49.5 us -> 45.3 us
  local copies, waits for them, and re-layouts: 23.2 us -> 19.3 us
  other arithmetic: 18.9 us -> 15.8 us
  matrix products: 14.7 us -> 11.8 us
    all_to_all x1, waiting for transfers between devices: 23.2 us -> 27.7 us  [per_device(): lax.all_to_all(back_y, 'fft', split_axis=2, concat_axis=1, tiled=True)]
    pallas_call x2 -> x1, Pallas kernels: 23 us -> 18.6 us  [halo_exchange(): pl.pallas_call(halo_kernel, out_shape=(jax.ShapeDtypeStruct((2 * atoms, 1...]
  transfers between devices with their start and end apart: 2 -> 2, of which waited for: 2 -> 2; matrix products, arithmetic and copies ran while one was open for 8% -> 6% of each run, Pallas kernels for 13% -> 13%
where the time goes in v6:
time: 201 us; the launch traced here: 200 us
  waiting for transfers between devices  80.3 us (40%)
  Pallas kernels  45.3 us (23%)
  starting transfers between devices  26.7 us (13%)
  local copies, waits for them, and re-layouts  19.3 us (10%)
  other arithmetic  15.8 us (8%)
  matrix products  11.8 us (6%)
    all_to_all x1, waiting for transfers between devices, per_device(): lax.all_to_all(along_x, 'fft', split_axis=1, concat_axis=2, tiled=True)  52.6 us
    all_to_all x1, waiting for transfers between devices, per_device(): lax.all_to_all(back_y, 'fft', split_axis=2, concat_axis=1, tiled=True)  27.7 us
    pallas_call x1, Pallas kernels, band_sum(): pl.pallas_call(band_sum_kernel, out_shape=jax.ShapeDtypeStruct(chunks.sha...  26.7 us
    pallas_call x1, Pallas kernels, halo_exchange(): pl.pallas_call(halo_kernel, out_shape=(jax.ShapeDtypeStruct((2 * atoms, 1...  18.6 us
    all_to_all x1, starting transfers between devices, per_device(): lax.all_to_all(along_x, 'fft', split_axis=1, concat_axis=2, tiled=True)  18.4 us
    all_to_all x1, starting transfers between devices, per_device(): lax.all_to_all(back_y, 'fft', split_axis=2, concat_axis=1, tiled=True)  8.35 us
    another operation x6, other arithmetic  5.49 us
  transfers between devices with their start and end apart: 2, of which 2 were waited for; matrix products, arithmetic and copies ran while one was open for 6% of the time, Pallas kernels for 13%

profile of v6, /device:TPU:6, one launch (start us, length us, event | category | flops | bytes accessed | tf_op | source)
XLA Modules:
  0.0 200.3 jit_solution(14089255601299940317)
XLA Ops:
  0.6 0.8 negate_convert_fusion.2
  1.4 0.8 multiply_convert_fusion.3
  2.2 0.8 fusion.69
  3.0 0.8 fusion.58
  6.9 0.8 convolution_convert_fusion
  7.7 2.2 %copy.85 = bf16[2,192,6,256]{3,0,2,1:T(2,128)(2,1)} copy(bf16[2,192,6,256]{3,1,2,0:T(8,128)(2,1)S(1)} %convolution_convert_fusion) | data formatting | bytes 2359296 | tf_op jit(solution)/shard_map/convert_element_type | solution.py:297
  10.0 18.4 %all-to-all-start = ((bf16[2,192,6,256]{3,0,2,1:T(2,128)(2,1)}), bf16[2,192,6,256]{3,0,2,1:T(2,128)(2,1)S(1)}, u32[]{:S(2)}, u32[]{:S(2)}) async-start(bf16[2,192,6,256]{3,0,2,1:T(2,128)(2,1)} %copy.85), calls=%async_computation | async-start | bytes 2359296 | tf_op jit(solution)/shard_map/all_to_all | solution.py:301
  29.1 1.1 convert_element_type.191
  30.2 1.0 multiply_convert_fusion.2
  31.2 1.0 negate_convert_fusion
  32.2 1.1 multiply_convert_fusion
  33.3 0.9 fusion.48
  34.8 52.6 %all-to-all-done = bf16[2,192,6,256]{3,0,2,1:T(2,128)(2,1)S(1)} async-done(((bf16[2,192,6,256]{3,0,2,1:T(2,128)(2,1)}), bf16[2,192,6,256]{3,0,2,1:T(2,128)(2,1)S(1)}, u32[]{:S(2)}, u32[]{:S(2)}) %all-to-all-start) | async-done | bytes 1179680 | tf_op jit(solution)/shard_map/all_to_all | solution.py:301
  87.4 0.8 copy.86
  88.2 1.4 fusion.17
  89.8 0.9 copy-done
  90.7 1.6 fusion.3
  93.8 18.6 %shard_map.85 = (f32[8,128]{1,0:T(8,128)}, f32[2,4,64,128]{3,2,1,0:T(8,128)}, bf16[2,4,64,128]{3,2,1,0:T(8,128)(2,1)}, bf16[2,4,64,128]{3,2,1,0:T(8,128)(2,1)}) custom-call(bf16[2,4,64,128]{3,2,1,0:T(8,128)(2,1)} %get-tuple-element.24.to_left_ref, bf16[2,4,64,128]{3,2,1,0:T(8,128)(2,1)} %get-tuple-element.23.own_ref, ...), custom_call_target="tpu_custom_call" | custom-call | flops 2097152 | bytes 1048576 | tf_op jit(solution)/shard_map/pallas_call | solution.py:217
  112.4 0.9 bitcast_convert_fusion.5
  113.4 0.9 bitcast_convert_fusion.6
  114.3 1.0 pad_maximum_fusion.1
  116.4 2.5 %convolution_bitcast_fusion = f32[4,1152,256]{1,2,0:T(8,128)S(1)} fusion(s32[768]{0:T(1024)S(1)} %add_select_fusion.4, pred[768]{0:T(1024)(128)(4,1)S(1)} %fusion.73, bf16[2,768,256]{1,2,0:T(8,128)(2,1)S(1)} %get-tuple-element.11, bf16[2,768,256]{1,2,0:T(8,128)(2,1)S(1)} %get-tuple-element.12), kind=kOutput, calls=%fused_computation | convolution fusion | flops 1814495232 | bytes 6295296 | tf_op jit(solution)/shard_map/er,cez->crz/dot_general | solution.py:349
  119.1 2.0 copy.100
  121.1 3.7 %fusion.19 = bf16[2,6,192,256]{3,2,0,1:T(8,128)(2,1)S(1)} fusion(f32[2,6,192,256]{3,2,1,0:T(8,128)} %bitcast.181, bf16[2,6,192,256]{3,2,0,1:T(8,128)(2,1)S(1)} %copy-done.1, f32[6,192,256]{2,1,0:T(8,128)} %convert_element_type.191, bf16[1,2,256,256]{3,2,1,0:T(8,128)(2,1)} %get-tuple-element.26, bf16[1,2,256,256]{3,2,1,0:T(8,128)(2,1)} %get-tuple-element.25, ...), kind=kOutput, calls=%fused_computation.32 | convolution fusion | flops 1062141952 | bytes 6717440 | tf_op jit(solution)/shard_map/abyk,bxkz->axyz/dot_general | solution.py:367
  124.8 2.2 %copy.102 = bf16[2,6,192,256]{3,0,1,2:T(2,128)(2,1)} copy(bf16[2,6,192,256]{3,2,0,1:T(8,128)(2,1)S(1)} %fusion.19) | data formatting | bytes 2359296 | tf_op jit(solution)/shard_map/convert_element_type | solution.py:369
  127.0 8.4 %all-to-all-start.1 = ((bf16[2,6,192,256]{3,0,1,2:T(2,128)(2,1)}), bf16[2,6,192,256]{3,0,1,2:T(2,128)(2,1)}, u32[]{:S(2)}, u32[]{:S(2)}) async-start(bf16[2,6,192,256]{3,0,1,2:T(2,128)(2,1)} %copy.102), calls=%async_computation.1 | async-start | bytes 2359296 | tf_op jit(solution)/shard_map/all_to_all | solution.py:373
  136.5 2.3 %fusion.22.part_ref = bf16[16,144,128]{2,1,0:T(8,128)(2,1)} fusion(f32[16,144,128]{2,1,0:T(8,128)S(1)} %reshape.444, f32[16,144,128]{2,1,0:T(8,128)S(1)} %reshape.445, f32[]{:T(128)} %bitcast.71, f32[]{:T(128)} %bitcast.70), kind=kLoop, calls=%fused_computation.35 | loop fusion | flops 1769472 | bytes 2949128 | tf_op jit(solution)/shard_map/convert_element_type | solution.py:311
  139.1 26.7 %shard_map.86 = bf16[16,144,128]{2,1,0:T(8,128)(2,1)} custom-call(bf16[16,144,128]{2,1,0:T(8,128)(2,1)} %fusion.22.part_ref), custom_call_target="tpu_custom_call" | custom-call | flops 294912 | bytes 1769472 | tf_op jit(solution)/shard_map/pallas_call | solution.py:72
  165.8 2.0 %reshape.440 = bf16[6,192,256]{2,1,0:T(8,128)(2,1)} reshape(bf16[16,144,128]{2,1,0:T(8,128)(2,1)} %shard_map.86) | data formatting | bytes 1179648 | tf_op jit(solution)/shard_map/reshape | solution.py:87
  167.9 27.7 %all-to-all-done.1 = bf16[2,6,192,256]{3,0,1,2:T(2,128)(2,1)} async-done(((bf16[2,6,192,256]{3,0,1,2:T(2,128)(2,1)}), bf16[2,6,192,256]{3,0,1,2:T(2,128)(2,1)}, u32[]{:S(2)}, u32[]{:S(2)}) %all-to-all-start.1) | async-done | bytes 1179680 | tf_op jit(solution)/shard_map/all_to_all | solution.py:373
  195.6 2.2 %copy.104 = bf16[2,32,6,6,256]{4,0,3,2,1:T(2,128)(2,1)S(1)} copy(bf16[2,32,6,6,256]{4,0,2,3,1:T(2,128)(2,1)} %bitcast.63) | data formatting | bytes 2359296 | tf_op jit(solution)/shard_map/all_to_all | solution.py:373
  197.8 1.9 fusion.20
  (64 shorter events, 9.2 us)
Async XLA Ops:
  3.9 1.3 copy-start.2
  10.0 18.4 %copy-start.7 = (s32[128,64]{0,1:T(8,128)S(1)}, s32[128,64]{0,1:T(8,128)}, u32[]{:S(2)}) copy-start(s32[128,64]{0,1:T(8,128)} %param.11) | copy-start | bytes 98308
  10.0 19.1 %copy-start.8 = (f32[8,8]{1,0:T(8,128)S(1)}, f32[8,8]{1,0:T(8,128)}, u32[]{:S(2)}) copy-start(f32[8,8]{1,0:T(8,128)} %param.10) | copy-start | bytes 772
  10.0 19.1 %copy-start.6 = (bf16[6,192,256]{2,1,0:T(8,128)(2,1)S(1)}, bf16[6,192,256]{2,1,0:T(8,128)(2,1)}, u32[]{:S(2)}) copy-start(bf16[6,192,256]{2,1,0:T(8,128)(2,1)} %param.8) | copy-start | bytes 1769476
  10.0 77.4 %all-to-all-start = ((bf16[2,192,6,256]{3,0,2,1:T(2,128)(2,1)}), bf16[2,192,6,256]{3,0,2,1:T(2,128)(2,1)S(1)}, u32[]{:S(2)}, u32[]{:S(2)}) async-start(bf16[2,192,6,256]{3,0,2,1:T(2,128)(2,1)} %copy.85), calls=%async_computation | async-start | bytes 2359296 | tf_op jit(solution)/shard_map/all_to_all | solution.py:301
  89.7 1.0 copy-start
  119.1 2.0 copy-start.1
  127.0 8.4 %copy-start.10 = (f32[1,2]{1,0:T(1,128)S(1)}, f32[1,2]{1,0:T(1,128)}, u32[]{:S(2)}) copy-start(f32[1,2]{1,0:T(1,128)} %param.7) | copy-start | bytes 28
  127.0 68.6 %all-to-all-start.1 = ((bf16[2,6,192,256]{3,0,1,2:T(2,128)(2,1)}), bf16[2,6,192,256]{3,0,1,2:T(2,128)(2,1)}, u32[]{:S(2)}, u32[]{:S(2)}) async-start(bf16[2,6,192,256]{3,0,1,2:T(2,128)(2,1)} %copy.102), calls=%async_computation.1 | async-start | bytes 2359296 | tf_op jit(solution)/shard_map/all_to_all | solution.py:373
  195.6 2.2 %copy-start.3 = (bf16[1,2,192,6,256]{4,2,3,1,0:T(8,128)(2,1)S(1)}, bf16[1,2,192,6,256]{4,2,3,1,0:T(8,128)(2,1)}, u32[]{:S(2)}) copy-start(bf16[1,2,192,6,256]{4,2,3,1,0:T(8,128)(2,1)} %param.6) | copy-start | bytes 3538948
  195.6 2.2 %copy-start.4 = (bf16[1,2,192,192]{3,2,1,0:T(8,128)(2,1)S(1)}, bf16[1,2,192,192]{3,2,1,0:T(8,128)(2,1)}, u32[]{:S(2)}) copy-start(bf16[1,2,192,192]{3,2,1,0:T(8,128)(2,1)} %get-tuple-element.29) | copy-start | bytes 442372
  195.6 2.2 %copy-start.5 = (bf16[1,2,192,192]{3,2,1,0:T(8,128)(2,1)S(1)}, bf16[1,2,192,192]{3,2,1,0:T(8,128)(2,1)}, u32[]{:S(2)}) copy-start(bf16[1,2,192,192]{3,2,1,0:T(8,128)(2,1)} %get-tuple-element.32) | copy-start | bytes 442372
  197.8 1.9 copy-start.9

commit v7 on v6

--- a/solution.py
+++ b/solution.py
@@ -1,6 +1,8 @@
 import math
 
 import jax
+import ml_dtypes
+import numpy as np
 import jax.numpy as jnp
 from jax import lax
 from jax.experimental import pallas as pl
@@ -268,6 +270,17 @@
     return jnp.stack([upper_rows, bottom]).astype(jnp.bfloat16)
 
 
+def dft_table_constant(length, sign_value):
+    indices = np.arange(length, dtype=np.int64)
+    phases = indices[:, None] * indices[None, :] % length
+    angles = np.float32(2.0 * math.pi / length) * phases.astype(np.float32)
+    factor = np.float32(1.0 / math.sqrt(length))
+    cosine = np.cos(angles).astype(np.float32) * factor
+    sine_part = np.sin(angles).astype(np.float32) * np.float32(sign_value) * factor
+    table = np.stack([np.stack([cosine, -sine_part]), np.stack([sine_part, cosine])])
+    return table.astype(ml_dtypes.bfloat16)
+
+
 def wave_squares(indices, length):
     frequency = (
         jnp.where(2 * indices < length, indices, indices - length).astype(jnp.float32) / length
@@ -289,16 +302,22 @@
     block_cells = projectors.shape[3]
     zblocks = size_z // block_cells
     plane_blocks = size_y * zblocks
-    table_x = dft_table(size_x, 1.0).transpose(0, 2, 1, 3).reshape(2 * size_x, 2 * size_x)
+    table_x = (
+        dft_table_constant(size_x, 1.0)
+        .reshape(2, 2, pieces, slab_planes, size_x)
+        .transpose(2, 0, 3, 1, 4)
+        .reshape(2 * size_x, 2 * size_x)
+    )
     inverse_y = dft_table(size_y, 1.0)
     inverse_z = dft_table(size_z, 1.0)
     flattened = coeffs.reshape(2 * size_x, columns * size_z)
-    along_x = jnp.dot(table_x, flattened, preferred_element_type=jnp.float32)
-    along_x = along_x.reshape(2, size_x, columns, size_z).astype(jnp.bfloat16)
+    along_x = jnp.dot(jnp.asarray(table_x), flattened, preferred_element_type=jnp.float32)
+    along_x = along_x.reshape(pieces, 2, slab_planes, columns, size_z).astype(jnp.bfloat16)
+    arrived = lax.all_to_all(along_x, "fft", split_axis=0, concat_axis=0, tiled=True)
     along_y = jnp.einsum(
-        "abyk,bxkz->axyz",
-        inverse_y,
-        lax.all_to_all(along_x, "fft", split_axis=1, concat_axis=2, tiled=True),
+        "abysu,sbxuz->axyz",
+        inverse_y.reshape(2, 2, size_y, pieces, columns),
+        arrived,
         preferred_element_type=jnp.float32,
     ).astype(jnp.bfloat16)
     wave_field = jnp.einsum(

time: 201 us -> 197 us (0.980)
  waiting for transfers between devices: 80.3 us -> 76.3 us
    all_to_all x1, waiting for transfers between devices: 52.6 us -> 49 us  [per_device(): lax.all_to_all(along_x, 'fft', split_axis=0, concat_axis=0, tiled=True)]
  transfers between devices with their start and end apart: 2 -> 2, of which waited for: 2 -> 2; matrix products, arithmetic and copies ran while one was open for 6% -> 8% of each run, Pallas kernels for 13% -> 14%
where the time goes in v7:
time: 197 us; the launch traced here: 196 us
  waiting for transfers between devices  76.3 us (39%)
  Pallas kernels  45.6 us (23%)
  starting transfers between devices  26.5 us (13%)
  local copies, waits for them, and re-layouts  18.8 us (10%)
  other arithmetic  16 us (8%)
  matrix products  11.8 us (6%)
    all_to_all x1, waiting for transfers between devices, per_device(): lax.all_to_all(along_x, 'fft', split_axis=0, concat_axis=0, tiled=True)  49 us
    all_to_all x1, waiting for transfers between devices, per_device(): lax.all_to_all(back_y, 'fft', split_axis=2, concat_axis=1, tiled=True)  27.3 us
    pallas_call x1, Pallas kernels, band_sum(): pl.pallas_call(band_sum_kernel, out_shape=jax.ShapeDtypeStruct(chunks.sha...  27 us
    pallas_call x1, Pallas kernels, halo_exchange(): pl.pallas_call(halo_kernel, out_shape=(jax.ShapeDtypeStruct((2 * atoms, 1...  18.6 us
    all_to_all x1, starting transfers between devices, per_device(): lax.all_to_all(along_x, 'fft', split_axis=0, concat_axis=0, tiled=True)  18.3 us
    all_to_all x1, starting transfers between devices, per_device(): lax.all_to_all(back_y, 'fft', split_axis=2, concat_axis=1, tiled=True)  8.18 us
    another operation x6, other arithmetic  5.81 us
    unnamed x28, local copies, waits for them, and re-layouts  4.57 us
  transfers between devices with their start and end apart: 2, of which 2 were waited for; matrix products, arithmetic and copies ran while one was open for 8% of the time, Pallas kernels for 14%

profile of v7, /device:TPU:6, one launch (start us, length us, event | category | flops | bytes accessed | tf_op | source)
XLA Modules:
  0.0 196.1 jit_solution(12269237060839940378)
XLA Ops:
  0.6 2.0 %copy.31 = bf16[1,2,192,6,256]{4,3,2,1,0:T(8,128)(2,1)S(1)} copy(bf16[1,2,192,6,256]{4,2,3,1,0:T(8,128)(2,1)} %param.7) | data formatting | bytes 2359296 | tf_op args[0]
  3.9 0.8 convolution_convert_fusion
  4.7 2.2 %copy.33 = bf16[32,2,6,6,256]{4,1,3,2,0:T(2,128)(2,1)} copy(bf16[32,2,6,6,256]{4,0,3,2,1:T(8,128)(2,1)S(1)} %convolution_convert_fusion) | data formatting | bytes 2359296 | tf_op jit(solution)/shard_map/convert_element_type | solution.py:315
  6.9 18.3 %all-to-all-start = ((bf16[32,2,6,6,256]{4,1,3,2,0:T(2,128)(2,1)}), bf16[32,2,6,6,256]{4,1,3,2,0:T(2,128)(2,1)S(1)}, u32[]{:S(2)}, u32[]{:S(2)}) async-start(bf16[32,2,6,6,256]{4,1,3,2,0:T(2,128)(2,1)} %copy.33), calls=%async_computation | async-start | bytes 2359296 | tf_op jit(solution)/shard_map/all_to_all | solution.py:316
  26.1 1.1 convert_element_type.198
  27.2 0.8 fusion.74
  28.0 1.0 multiply_convert_fusion.2
  28.9 0.8 negate_convert_fusion.3
  29.8 1.0 negate_convert_fusion
  30.8 1.3 multiply_convert_fusion
  32.1 0.8 maximum_bitcast_fusion.8
  32.9 0.9 fusion.57
  34.4 0.9 negate_convert_fusion.2
  35.4 49.0 %all-to-all-done = bf16[32,2,6,6,256]{4,1,3,2,0:T(2,128)(2,1)S(1)} async-done(((bf16[32,2,6,6,256]{4,1,3,2,0:T(2,128)(2,1)}), bf16[32,2,6,6,256]{4,1,3,2,0:T(2,128)(2,1)S(1)}, u32[]{:S(2)}, u32[]{:S(2)}) %all-to-all-start) | async-done | bytes 1179680 | tf_op jit(solution)/shard_map/all_to_all | solution.py:316
  84.4 1.5 fusion.16
  85.9 0.9 copy-done
  86.9 1.6 fusion.3
  90.0 18.6 %shard_map.94 = (f32[8,128]{1,0:T(8,128)}, f32[2,4,64,128]{3,2,1,0:T(8,128)}, bf16[2,4,64,128]{3,2,1,0:T(8,128)(2,1)}, bf16[2,4,64,128]{3,2,1,0:T(8,128)(2,1)}) custom-call(bf16[2,4,64,128]{3,2,1,0:T(8,128)(2,1)} %get-tuple-element.24.to_left_ref, bf16[2,4,64,128]{3,2,1,0:T(8,128)(2,1)} %get-tuple-element.23.own_ref, ...), custom_call_target="tpu_custom_call" | custom-call | flops 2097152 | bytes 1048576 | tf_op jit(solution)/shard_map/pallas_call | solution.py:219
  108.6 0.9 bitcast_convert_fusion.5
  109.6 0.9 bitcast_convert_fusion.6
  110.5 1.0 pad_maximum_fusion.1
  112.6 2.5 %convolution_bitcast_fusion = f32[4,1152,256]{1,2,0:T(8,128)S(1)} fusion(s32[768]{0:T(1024)S(1)} %add_select_fusion.5, pred[768]{0:T(1024)(128)(4,1)S(1)} %fusion.79, bf16[2,768,256]{1,2,0:T(8,128)(2,1)S(1)} %get-tuple-element.11, bf16[2,768,256]{1,2,0:T(8,128)(2,1)S(1)} %get-tuple-element.12), kind=kOutput, calls=%fused_computation | convolution fusion | flops 1814495232 | bytes 6295296 | tf_op jit(solution)/shard_map/er,cez->crz/dot_general | solution.py:368
  115.3 2.0 %copy.47 = f32[2,1152,256]{2,1,0:T(8,128)} copy(f32[2,1152,256]{1,2,0:T(8,128)S(1)} %slice_add_fusion) | data formatting | bytes 4718592 | tf_op jit(solution)/shard_map/add | solution.py:374
  117.3 3.7 %fusion.18 = bf16[2,6,192,256]{3,2,0,1:T(8,128)(2,1)S(1)} fusion(f32[2,6,192,256]{3,2,1,0:T(8,128)} %bitcast.173, bf16[2,6,192,256]{3,2,0,1:T(8,128)(2,1)S(1)} %copy-done.1, f32[6,192,256]{2,1,0:T(8,128)} %convert_element_type.198, bf16[1,2,256,256]{3,2,1,0:T(8,128)(2,1)} %get-tuple-element.26, bf16[1,2,256,256]{3,2,1,0:T(8,128)(2,1)} %get-tuple-element.25, ...), kind=kOutput, calls=%fused_computation.31 | convolution fusion | flops 1062141952 | bytes 6717440 | tf_op jit(solution)/shard_map/abyk,bxkz->axyz/dot_general | solution.py:386
  121.0 2.2 %copy.49 = bf16[2,6,192,256]{3,0,1,2:T(2,128)(2,1)} copy(bf16[2,6,192,256]{3,2,0,1:T(8,128)(2,1)S(1)} %fusion.18) | data formatting | bytes 2359296 | tf_op jit(solution)/shard_map/convert_element_type | solution.py:388
  123.2 8.2 %all-to-all-start.1 = ((bf16[2,6,192,256]{3,0,1,2:T(2,128)(2,1)}), bf16[2,6,192,256]{3,0,1,2:T(2,128)(2,1)}, u32[]{:S(2)}, u32[]{:S(2)}) async-start(bf16[2,6,192,256]{3,0,1,2:T(2,128)(2,1)} %copy.49), calls=%async_computation.1 | async-start | bytes 2359296 | tf_op jit(solution)/shard_map/all_to_all | solution.py:392
  132.6 2.3 %fusion.22.part_ref = bf16[16,144,128]{2,1,0:T(8,128)(2,1)} fusion(f32[16,144,128]{2,1,0:T(8,128)S(1)} %reshape.485, f32[16,144,128]{2,1,0:T(8,128)S(1)} %reshape.486, f32[]{:T(128)} %bitcast.67, f32[]{:T(128)} %bitcast.66), kind=kLoop, calls=%fused_computation.35 | loop fusion | flops 1769472 | bytes 2949128 | tf_op jit(solution)/shard_map/convert_element_type | solution.py:330
  135.1 27.0 %shard_map.95 = bf16[16,144,128]{2,1,0:T(8,128)(2,1)} custom-call(bf16[16,144,128]{2,1,0:T(8,128)(2,1)} %fusion.22.part_ref), custom_call_target="tpu_custom_call" | custom-call | flops 294912 | bytes 1769472 | tf_op jit(solution)/shard_map/pallas_call | solution.py:74
  162.1 2.0 %reshape.481 = bf16[6,192,256]{2,1,0:T(8,128)(2,1)} reshape(bf16[16,144,128]{2,1,0:T(8,128)(2,1)} %shard_map.95) | data formatting | bytes 1179648 | tf_op jit(solution)/shard_map/reshape | solution.py:89
  164.1 27.3 %all-to-all-done.1 = bf16[2,6,192,256]{3,0,1,2:T(2,128)(2,1)} async-done(((bf16[2,6,192,256]{3,0,1,2:T(2,128)(2,1)}), bf16[2,6,192,256]{3,0,1,2:T(2,128)(2,1)}, u32[]{:S(2)}, u32[]{:S(2)}) %all-to-all-start.1) | async-done | bytes 1179680 | tf_op jit(solution)/shard_map/all_to_all | solution.py:392
  191.4 2.2 %copy.51 = bf16[2,32,6,6,256]{4,0,3,2,1:T(2,128)(2,1)S(1)} copy(bf16[2,32,6,6,256]{4,0,2,3,1:T(2,128)(2,1)} %bitcast.59) | data formatting | bytes 2359296 | tf_op jit(solution)/shard_map/all_to_all | solution.py:392
  193.7 1.9 fusion.20
  (61 shorter events, 7.5 us)
Async XLA Ops:
  2.9 1.0 copy-start.7
  6.9 18.4 %copy-start.6 = (s32[128,64]{0,1:T(8,128)S(1)}, s32[128,64]{0,1:T(8,128)}, u32[]{:S(2)}) copy-start(s32[128,64]{0,1:T(8,128)} %param.12) | copy-start | bytes 98308
  6.9 19.0 %copy-start.8 = (f32[8,8]{1,0:T(8,128)S(1)}, f32[8,8]{1,0:T(8,128)}, u32[]{:S(2)}) copy-start(f32[8,8]{1,0:T(8,128)} %param.11) | copy-start | bytes 772
  6.9 19.1 %copy-start.5 = (bf16[6,192,256]{2,1,0:T(8,128)(2,1)S(1)}, bf16[6,192,256]{2,1,0:T(8,128)(2,1)}, u32[]{:S(2)}) copy-start(bf16[6,192,256]{2,1,0:T(8,128)(2,1)} %param.9) | copy-start | bytes 1769476
  6.9 77.4 %all-to-all-start = ((bf16[32,2,6,6,256]{4,1,3,2,0:T(2,128)(2,1)}), bf16[32,2,6,6,256]{4,1,3,2,0:T(2,128)(2,1)S(1)}, u32[]{:S(2)}, u32[]{:S(2)}) async-start(bf16[32,2,6,6,256]{4,1,3,2,0:T(2,128)(2,1)} %copy.33), calls=%async_computation | async-start | bytes 2359296 | tf_op jit(solution)/shard_map/all_to_all | solution.py:316
  85.8 1.0 copy-start
  115.3 2.0 %copy-start.1 = (bf16[2,6,192,256]{3,2,0,1:T(8,128)(2,1)S(1)}, bf16[2,6,192,256]{3,2,0,1:T(8,128)(2,1)}, u32[]{:S(2)}) copy-start(bf16[2,6,192,256]{3,2,0,1:T(8,128)(2,1)} %copy-done) | copy-start | bytes 3538948
  123.2 8.2 %copy-start.10 = (f32[1,2]{1,0:T(1,128)S(1)}, f32[1,2]{1,0:T(1,128)}, u32[]{:S(2)}) copy-start(f32[1,2]{1,0:T(1,128)} %param.8) | copy-start | bytes 28
  123.2 68.2 %all-to-all-start.1 = ((bf16[2,6,192,256]{3,0,1,2:T(2,128)(2,1)}), bf16[2,6,192,256]{3,0,1,2:T(2,128)(2,1)}, u32[]{:S(2)}, u32[]{:S(2)}) async-start(bf16[2,6,192,256]{3,0,1,2:T(2,128)(2,1)} %copy.49), calls=%async_computation.1 | async-start | bytes 2359296 | tf_op jit(solution)/shard_map/all_to_all | solution.py:392
  191.4 2.2 %copy-start.2 = (bf16[1,2,192,6,256]{4,2,3,1,0:T(8,128)(2,1)S(1)}, bf16[1,2,192,6,256]{4,2,3,1,0:T(8,128)(2,1)}, u32[]{:S(2)}) copy-start(bf16[1,2,192,6,256]{4,2,3,1,0:T(8,128)(2,1)} %param.7) | copy-start | bytes 3538948
  191.4 2.2 %copy-start.3 = (bf16[1,2,192,192]{3,2,1,0:T(8,128)(2,1)S(1)}, bf16[1,2,192,192]{3,2,1,0:T(8,128)(2,1)}, u32[]{:S(2)}) copy-start(bf16[1,2,192,192]{3,2,1,0:T(8,128)(2,1)} %get-tuple-element.29) | copy-start | bytes 442372
  191.4 2.2 %copy-start.4 = (bf16[1,2,192,192]{3,2,1,0:T(8,128)(2,1)S(1)}, bf16[1,2,192,192]{3,2,1,0:T(8,128)(2,1)}, u32[]{:S(2)}) copy-start(bf16[1,2,192,192]{3,2,1,0:T(8,128)(2,1)} %get-tuple-element.30) | copy-start | bytes 442372
  193.7 1.9 copy-start.9

commit v8 on v7

--- a/solution.py
+++ b/solution.py
@@ -379,19 +379,27 @@
     ).astype(jnp.bfloat16)
     forward_z = dft_table(size_z, -1.0)
     forward_y = dft_table(size_y, -1.0)
-    forward_x = dft_table(size_x, -1.0)
     back_z = jnp.einsum(
         "abzk,bxyk->axyz", forward_z, total_field, preferred_element_type=jnp.float32
     ).astype(jnp.bfloat16)
     back_y = jnp.einsum(
-        "abyk,bxkz->axyz", forward_y, back_z, preferred_element_type=jnp.float32
-    ).astype(jnp.bfloat16)
-    transformed = jnp.einsum(
-        "abxk,bkyz->axyz",
-        forward_x,
-        lax.all_to_all(back_y, "fft", split_axis=2, concat_axis=1, tiled=True),
+        "abtuk,bxkz->taxuz",
+        forward_y.reshape(2, 2, pieces, columns, size_y),
+        back_z,
         preferred_element_type=jnp.float32,
-    )
+    ).astype(jnp.bfloat16)
+    returned = lax.all_to_all(back_y, "fft", split_axis=0, concat_axis=0, tiled=True)
+    table_back = (
+        dft_table_constant(size_x, -1.0)
+        .reshape(2, 2, size_x, pieces, slab_planes)
+        .transpose(0, 2, 3, 1, 4)
+        .reshape(2 * size_x, 2 * size_x)
+    )
+    transformed = jnp.dot(
+        jnp.asarray(table_back),
+        returned.reshape(2 * size_x, columns * size_z),
+        preferred_element_type=jnp.float32,
+    ).reshape(2, size_x, columns, size_z)
     index_x = jnp.arange(size_x, dtype=jnp.int32)
     index_y = slab_index * columns + jnp.arange(columns, dtype=jnp.int32)
     index_z = jnp.arange(size_z, dtype=jnp.int32)

time: 197 us -> 204 us (1.036)
  local copies, waits for them, and re-layouts: 18.8 us -> 22.9 us
  other arithmetic: 16 us -> 19.8 us
    convert_element_type x0 -> x1, other arithmetic: none -> 2.68 us  [per_device(): (transformed + kinetic[None] * coeffs.astype(jnp.float32)).astype(jnp.bfl...]
    reshape x0 -> x1, local copies, waits for them, and re-layouts: none -> 2.65 us  [per_device(): transformed = jnp.dot(jnp.asarray(table_back), returned.reshape(2 * size_...]
    unnamed x28, local copies, waits for them, and re-layouts: 4.57 us -> 6.79 us
    another operation x6 -> x5, other arithmetic: 5.81 us -> 5.83 us
  transfers between devices with their start and end apart: 2 -> 2, of which waited for: 2 -> 2; matrix products, arithmetic and copies ran while one was open for 8% -> 8% of each run, Pallas kernels for 14% -> 13%
where the time goes in v8:
time: 204 us; the launch traced here: 203 us
  waiting for transfers between devices  75.2 us (37%)
  Pallas kernels  45.8 us (22%)
  starting transfers between devices  26.5 us (13%)
  local copies, waits for them, and re-layouts  22.9 us (11%)
  other arithmetic  19.8 us (10%)
  matrix products  12.2 us (6%)
    all_to_all x1, waiting for transfers between devices, per_device(): lax.all_to_all(along_x, 'fft', split_axis=0, concat_axis=0, tiled=True)  49.8 us
    pallas_call x1, Pallas kernels, band_sum(): pl.pallas_call(band_sum_kernel, out_shape=jax.ShapeDtypeStruct(chunks.sha...  27.2 us
    all_to_all x1, waiting for transfers between devices, per_device(): lax.all_to_all(back_y, 'fft', split_axis=0, concat_axis=0, tiled=True)  25.3 us
    pallas_call x1, Pallas kernels, halo_exchange(): pl.pallas_call(halo_kernel, out_shape=(jax.ShapeDtypeStruct((2 * atoms, 1...  18.6 us
    all_to_all x1, starting transfers between devices, per_device(): lax.all_to_all(along_x, 'fft', split_axis=0, concat_axis=0, tiled=True)  18.3 us
    all_to_all x1, starting transfers between devices, per_device(): lax.all_to_all(back_y, 'fft', split_axis=0, concat_axis=0, tiled=True)  8.18 us
    unnamed x28, local copies, waits for them, and re-layouts  6.79 us
    another operation x5, other arithmetic  5.83 us
  transfers between devices with their start and end apart: 2, of which 2 were waited for; matrix products, arithmetic and copies ran while one was open for 8% of the time, Pallas kernels for 13%

profile of v8, /device:TPU:6, one launch (start us, length us, event | category | flops | bytes accessed | tf_op | source)
XLA Modules:
  0.0 203.3 jit_solution(17012038227037355154)
XLA Ops:
  0.6 2.0 copy.56
  4.7 2.2 %copy.58 = bf16[32,2,6,6,256]{4,1,3,2,0:T(2,128)(2,1)} copy(bf16[32,2,6,6,256]{4,0,3,2,1:T(8,128)(2,1)S(1)} %convolution_convert_fusion) | data formatting | bytes 2359296 | tf_op jit(solution)/shard_map/convert_element_type | solution.py:315
  6.9 18.3 %all-to-all-start = ((bf16[32,2,6,6,256]{4,1,3,2,0:T(2,128)(2,1)}), bf16[32,2,6,6,256]{4,1,3,2,0:T(2,128)(2,1)S(1)}, u32[]{:S(2)}, u32[]{:S(2)}) async-start(bf16[32,2,6,6,256]{4,1,3,2,0:T(2,128)(2,1)} %copy.58), calls=%async_computation | async-start | bytes 2359296 | tf_op jit(solution)/shard_map/all_to_all | solution.py:316
  26.1 1.1 convert_element_type.199
  27.2 1.0 multiply_convert_fusion.2
  28.2 1.0 negate_convert_fusion
  29.2 1.3 multiply_convert_fusion
  32.0 0.9 negate_convert_fusion.3
  32.9 1.6 negate_convert_fusion.2
  34.6 49.8 %all-to-all-done = bf16[32,2,6,6,256]{4,1,3,2,0:T(2,128)(2,1)S(1)} async-done(((bf16[32,2,6,6,256]{4,1,3,2,0:T(2,128)(2,1)}), bf16[32,2,6,6,256]{4,1,3,2,0:T(2,128)(2,1)S(1)}, u32[]{:S(2)}, u32[]{:S(2)}) %all-to-all-start) | async-done | bytes 1179680 | tf_op jit(solution)/shard_map/all_to_all | solution.py:316
  84.4 1.5 fusion.14
  85.9 0.9 copy-done
  86.9 1.6 fusion.3
  90.0 18.6 %shard_map.103 = (f32[8,128]{1,0:T(8,128)}, f32[2,4,64,128]{3,2,1,0:T(8,128)}, bf16[2,4,64,128]{3,2,1,0:T(8,128)(2,1)}, bf16[2,4,64,128]{3,2,1,0:T(8,128)(2,1)}) custom-call(bf16[2,4,64,128]{3,2,1,0:T(8,128)(2,1)} %get-tuple-element.33.to_left_ref, bf16[2,4,64,128]{3,2,1,0:T(8,128)(2,1)} %get-tuple-element.32.own_ref, ...), custom_call_target="tpu_custom_call" | custom-call | flops 2097152 | bytes 1048576 | tf_op jit(solution)/shard_map/pallas_call | solution.py:219
  108.6 0.9 bitcast_convert_fusion.5
  109.5 0.9 bitcast_convert_fusion.6
  110.5 1.0 pad_maximum_fusion.1
  112.6 2.5 %convolution_bitcast_fusion = f32[4,1152,256]{1,2,0:T(8,128)S(1)} fusion(s32[768]{0:T(1024)S(1)} %add_select_fusion.5, pred[768]{0:T(1024)(128)(4,1)S(1)} %fusion.78, bf16[2,768,256]{1,2,0:T(8,128)(2,1)S(1)} %get-tuple-element.20, bf16[2,768,256]{1,2,0:T(8,128)(2,1)S(1)} %get-tuple-element.21), kind=kOutput, calls=%fused_computation | convolution fusion | flops 1814495232 | bytes 6295296 | tf_op jit(solution)/shard_map/er,cez->crz/dot_general | solution.py:368
  115.3 2.0 copy.72
  117.3 3.7 %fusion.16 = bf16[32,2,6,6,256]{4,0,3,1,2:T(8,128)(2,1)S(1)} fusion(f32[2,6,192,256]{3,2,1,0:T(8,128)} %bitcast.154, bf16[2,6,192,256]{3,2,0,1:T(8,128)(2,1)S(1)} %copy-done.1, f32[6,192,256]{2,1,0:T(8,128)} %convert_element_type.199, bf16[1,2,256,256]{3,2,1,0:T(8,128)(2,1)} %get-tuple-element.35, bf16[1,2,256,256]{3,2,1,0:T(8,128)(2,1)} %get-tuple-element.34, ...), kind=kOutput, calls=%fused_computation.29 | convolution fusion | flops 1062731776 | bytes 6643712 | tf_op jit(solution)/shard_map/abtuk,bxkz->taxuz/dot_general | solution.py:385
  120.9 2.2 %copy.74 = bf16[32,2,6,6,256]{4,1,3,2,0:T(2,128)(2,1)} copy(bf16[32,2,6,6,256]{4,0,3,1,2:T(8,128)(2,1)S(1)} %fusion.16) | data formatting | bytes 2359296 | tf_op jit(solution)/shard_map/convert_element_type | solution.py:390
  123.2 8.2 %all-to-all-start.1 = ((bf16[32,2,6,6,256]{4,1,3,2,0:T(2,128)(2,1)}), bf16[32,2,6,6,256]{4,1,3,2,0:T(2,128)(2,1)}, u32[]{:S(2)}, u32[]{:S(2)}) async-start(bf16[32,2,6,6,256]{4,1,3,2,0:T(2,128)(2,1)} %copy.74), calls=%async_computation.1 | async-start | bytes 2359296 | tf_op jit(solution)/shard_map/all_to_all | solution.py:391
  133.1 2.3 %fusion.19.part_ref = bf16[16,144,128]{2,1,0:T(8,128)(2,1)} fusion(f32[16,144,128]{2,1,0:T(8,128)S(1)} %reshape.506, f32[16,144,128]{2,1,0:T(8,128)S(1)} %reshape.507, f32[]{:T(128)} %bitcast.55, f32[]{:T(128)} %bitcast.54), kind=kLoop, calls=%fused_computation.32 | loop fusion | flops 1769472 | bytes 2949128 | tf_op jit(solution)/shard_map/convert_element_type | solution.py:330
  135.4 1.4 broadcast_add_fusion
  136.8 27.2 %shard_map.104 = bf16[16,144,128]{2,1,0:T(8,128)(2,1)} custom-call(bf16[16,144,128]{2,1,0:T(8,128)(2,1)} %fusion.19.part_ref), custom_call_target="tpu_custom_call" | custom-call | flops 294912 | bytes 1769472 | tf_op jit(solution)/shard_map/pallas_call | solution.py:74
  164.0 2.0 reshape.503
  166.0 25.3 %all-to-all-done.1 = bf16[32,2,6,6,256]{4,1,3,2,0:T(2,128)(2,1)} async-done(((bf16[32,2,6,6,256]{4,1,3,2,0:T(2,128)(2,1)}), bf16[32,2,6,6,256]{4,1,3,2,0:T(2,128)(2,1)}, u32[]{:S(2)}, u32[]{:S(2)}) %all-to-all-start.1) | async-done | bytes 1179680 | tf_op jit(solution)/shard_map/all_to_all | solution.py:391
  191.4 1.5 copy.75
  193.9 2.2 %fusion.95 = f32[384,1536]{1,0:T(8,128)} fusion(bf16[384,384]{1,0:T(8,128)(2,1)S(1)} %copy-done.6, bf16[384,1536]{1,0:T(8,128)(2,1)S(1)} %bitcast.152), kind=kOutput, calls=%fused_computation.165 | convolution fusion | flops 452984832 | bytes 3833856 | tf_op jit(solution)/shard_map/dot_general | solution.py:398
  196.1 2.7 %reshape.502 = f32[1,2,192,6,256]{4,3,2,1,0:T(8,128)S(1)} reshape(f32[384,1536]{1,0:T(8,128)} %fusion.95) | data formatting | bytes 4718592 | tf_op jit(solution)/shard_map/reshape | solution.py:402
  198.8 2.7 %add_convert_fusion = bf16[1,2,192,6,256]{4,3,2,1,0:T(8,128)(2,1)S(1)} fusion(f32[1,2,192,6,256]{4,3,2,1,0:T(8,128)S(1)} %reshape.502, f32[192,6,256]{2,1,0:T(8,128)} %broadcast_add_fusion, bf16[1,2,192,6,256]{4,2,3,1,0:T(8,128)(2,1)} %param.8), kind=kLoop, calls=%fused_computation.4 | loop fusion | flops 2359296 | bytes 5898240 | tf_op jit(solution)/shard_map/convert_element_type | solution.py:411
  201.5 1.3 copy.77
  (61 shorter events, 10.4 us)
Async XLA Ops:
  2.9 1.0 copy-start.5
  6.9 18.4 %copy-start.4 = (s32[128,64]{0,1:T(8,128)S(1)}, s32[128,64]{0,1:T(8,128)}, u32[]{:S(2)}) copy-start(s32[128,64]{0,1:T(8,128)} %param.13) | copy-start | bytes 98308
  6.9 19.0 %copy-start.7 = (f32[8,8]{1,0:T(8,128)S(1)}, f32[8,8]{1,0:T(8,128)}, u32[]{:S(2)}) copy-start(f32[8,8]{1,0:T(8,128)} %param.12) | copy-start | bytes 772
  6.9 19.1 %copy-start.2 = (bf16[6,192,256]{2,1,0:T(8,128)(2,1)S(1)}, bf16[6,192,256]{2,1,0:T(8,128)(2,1)}, u32[]{:S(2)}) copy-start(bf16[6,192,256]{2,1,0:T(8,128)(2,1)} %param.10) | copy-start | bytes 1769476
  6.9 77.4 %all-to-all-start = ((bf16[32,2,6,6,256]{4,1,3,2,0:T(2,128)(2,1)}), bf16[32,2,6,6,256]{4,1,3,2,0:T(2,128)(2,1)S(1)}, u32[]{:S(2)}, u32[]{:S(2)}) async-start(bf16[32,2,6,6,256]{4,1,3,2,0:T(2,128)(2,1)} %copy.58), calls=%async_computation | async-start | bytes 2359296 | tf_op jit(solution)/shard_map/all_to_all | solution.py:316
  85.8 1.0 copy-start
  115.3 2.0 copy-start.1
  123.2 8.2 %copy-start.9 = (f32[1,2]{1,0:T(1,128)S(1)}, f32[1,2]{1,0:T(1,128)}, u32[]{:S(2)}) copy-start(f32[1,2]{1,0:T(1,128)} %param.9) | copy-start | bytes 28
  123.2 68.2 %all-to-all-start.1 = ((bf16[32,2,6,6,256]{4,1,3,2,0:T(2,128)(2,1)}), bf16[32,2,6,6,256]{4,1,3,2,0:T(2,128)(2,1)}, u32[]{:S(2)}, u32[]{:S(2)}) async-start(bf16[32,2,6,6,256]{4,1,3,2,0:T(2,128)(2,1)} %copy.74), calls=%async_computation.1 | async-start | bytes 2359296 | tf_op jit(solution)/shard_map/all_to_all | solution.py:391
  133.1 2.3 %copy-start.3 = (f32[192,6]{1,0:T(8,128)S(1)}, f32[192,6]{1,0:T(8,128)}, u32[]{:S(2)}) copy-start(f32[192,6]{1,0:T(8,128)} %broadcast_add_fusion.1) | copy-start | bytes 13828
  193.0 1.0 copy-start.6
  201.5 1.3 copy-start.8

commit v9 on v7

--- a/solution.py
+++ b/solution.py
@@ -145,7 +145,7 @@
 
 def halo_kernel(
     to_left_ref, own_ref, to_right_ref, beta_ref, coupled_ref,
-    proj_ref, spread_ref, spread_right_ref, spread_left_ref,
+    proj_ref, spread_ref,
     landed, outgoing, landed_spread, sems,
 ):
     count = lax.axis_size("fft")
@@ -205,27 +205,25 @@
                 for j in range(1, nproj):
                     energy = energy + sums[j] * coupled_ref[i, j]
                 spread = spread + beta_ref[a, i].astype(jnp.float32) * energy
-            spread_ref[c, a] = spread
+            spread_ref[c, 1, a] = spread
             outgoing[c, a] = spread.astype(outgoing.dtype)
     swap(outgoing, outgoing, landed_spread, 4)
-    spread_right_ref[...] = landed_spread[0]
-    spread_left_ref[...] = landed_spread[1]
+    for c in range(2):
+        spread_ref[c, 0] = landed_spread[1, c].astype(jnp.float32)
+        spread_ref[c, 2] = landed_spread[0, c].astype(jnp.float32)
 
 
 def halo_exchange(to_left, own, to_right, projectors, coupled):
     atoms = projectors.shape[0]
-    half = jax.ShapeDtypeStruct(own.shape, jnp.bfloat16)
     vmem = pl.BlockSpec(memory_space=pltpu.VMEM)
     return pl.pallas_call(
         halo_kernel,
         out_shape=(
             jax.ShapeDtypeStruct((2 * atoms, 128), jnp.float32),
-            jax.ShapeDtypeStruct(own.shape, jnp.float32),
-            half,
-            half,
+            jax.ShapeDtypeStruct((2, 3) + own.shape[1:], jnp.float32),
         ),
         in_specs=[vmem, vmem, vmem, vmem, pl.BlockSpec(memory_space=pltpu.SMEM)],
-        out_specs=(vmem, vmem, vmem, vmem),
+        out_specs=(vmem, vmem),
         scratch_shapes=[
             pltpu.VMEM((2,) + own.shape, jnp.bfloat16),
             pltpu.VMEM(own.shape, jnp.bfloat16),
@@ -351,15 +349,11 @@
     for q in range(zblocks):
         picked = jnp.where(half_of == q, picked_rows[:, :, q], picked)
     picked = picked.astype(jnp.bfloat16).reshape(2, 3, atom_dev, -1, block_cells)
-    proj_rows, spread, spread_right, spread_left = halo_exchange(
+    proj_rows, spread_all = halo_exchange(
         picked[:, 0], picked[:, 1], picked[:, 2], projectors, coupled
     )
     projections_own = proj_rows[:, :nproj_count].reshape(atom_dev, 2, nproj_count)
-    spread_right = spread_right.astype(jnp.float32)
-    spread_left = spread_left.astype(jnp.float32)
-    spread_all = jnp.stack([spread_left, spread, spread_right], axis=1).reshape(
-        2, -1, 1, block_cells
-    )
+    spread_all = spread_all.reshape(2, -1, 1, block_cells)
     placed_halves = jnp.concatenate(
         [jnp.where(half_of[..., None] == q, spread_all, 0.0) for q in range(zblocks)], axis=2
     ).reshape(2, -1, size_z)

time: 197 us -> 195 us (0.990)
    another operation x9 -> x6, other arithmetic: 8.67 us -> 5.81 us
where the time goes in v9:
time: 195 us; the launch traced here: 194 us
  waiting for transfers between devices  75.9 us (39%)
  Pallas kernels  46.1 us (24%)
  starting transfers between devices  26.5 us (14%)
  local copies, waits for them, and re-layouts  18.7 us (10%)
  other arithmetic  14.3 us (7%)
  matrix products  11.8 us (6%)
    all_to_all x1, waiting for transfers between devices, per_device(): lax.all_to_all(along_x, 'fft', split_axis=0, concat_axis=0, tiled=True)  49 us
    pallas_call x1, Pallas kernels, band_sum(): pl.pallas_call(band_sum_kernel, out_shape=jax.ShapeDtypeStruct(chunks.sha...  27.3 us
    all_to_all x1, waiting for transfers between devices, per_device(): lax.all_to_all(back_y, 'fft', split_axis=2, concat_axis=1, tiled=True)  26.9 us
    pallas_call x1, Pallas kernels, halo_exchange(): pl.pallas_call(halo_kernel, out_shape=(jax.ShapeDtypeStruct((2 * atoms, 1...  18.7 us
    all_to_all x1, starting transfers between devices, per_device(): lax.all_to_all(along_x, 'fft', split_axis=0, concat_axis=0, tiled=True)  18.3 us
    all_to_all x1, starting transfers between devices, per_device(): lax.all_to_all(back_y, 'fft', split_axis=2, concat_axis=1, tiled=True)  8.19 us
    another operation x6, other arithmetic  5.81 us
    unnamed x28, local copies, waits for them, and re-layouts  4.57 us
  transfers between devices with their start and end apart: 2, of which 2 were waited for; matrix products, arithmetic and copies ran while one was open for 8% of the time, Pallas kernels for 14%

profile of v9, /device:TPU:6, one launch (start us, length us, event | category | flops | bytes accessed | tf_op | source)
XLA Modules:
  0.0 194.4 jit_solution(14733093600449777346)
XLA Ops:
  0.6 2.0 %copy.31 = bf16[1,2,192,6,256]{4,3,2,1,0:T(8,128)(2,1)S(1)} copy(bf16[1,2,192,6,256]{4,2,3,1,0:T(8,128)(2,1)} %param.7) | data formatting | bytes 2359296 | tf_op args[0]
  2.9 0.7 copy.32
  3.9 0.8 convolution_convert_fusion
  4.7 2.2 %copy.33 = bf16[32,2,6,6,256]{4,1,3,2,0:T(2,128)(2,1)} copy(bf16[32,2,6,6,256]{4,0,3,2,1:T(8,128)(2,1)S(1)} %convolution_convert_fusion) | data formatting | bytes 2359296 | tf_op jit(solution)/shard_map/convert_element_type | solution.py:313
  6.9 18.3 %all-to-all-start = ((bf16[32,2,6,6,256]{4,1,3,2,0:T(2,128)(2,1)}), bf16[32,2,6,6,256]{4,1,3,2,0:T(2,128)(2,1)S(1)}, u32[]{:S(2)}, u32[]{:S(2)}) async-start(bf16[32,2,6,6,256]{4,1,3,2,0:T(2,128)(2,1)} %copy.33), calls=%async_computation | async-start | bytes 2359296 | tf_op jit(solution)/shard_map/all_to_all | solution.py:314
  26.1 1.1 convert_element_type.196
  27.2 0.8 fusion.74
  28.0 1.0 multiply_convert_fusion.2
  28.9 0.8 negate_convert_fusion.3
  29.8 1.0 negate_convert_fusion
  30.8 1.3 multiply_convert_fusion
  32.1 0.8 maximum_bitcast_fusion.8
  32.9 0.9 fusion.57
  34.4 0.9 negate_convert_fusion.2
  35.4 49.0 %all-to-all-done = bf16[32,2,6,6,256]{4,1,3,2,0:T(2,128)(2,1)S(1)} async-done(((bf16[32,2,6,6,256]{4,1,3,2,0:T(2,128)(2,1)}), bf16[32,2,6,6,256]{4,1,3,2,0:T(2,128)(2,1)S(1)}, u32[]{:S(2)}, u32[]{:S(2)}) %all-to-all-start) | async-done | bytes 1179680 | tf_op jit(solution)/shard_map/all_to_all | solution.py:314
  84.4 1.5 fusion.16
  85.9 0.9 copy-done
  86.9 1.6 fusion.3
  89.2 0.8 slice_bitcast_fusion
  90.0 18.7 %shard_map.94 = (f32[8,128]{1,0:T(8,128)}, f32[2,3,4,64,128]{4,3,2,1,0:T(8,128)}) custom-call(bf16[2,4,64,128]{3,2,1,0:T(8,128)(2,1)} %get-tuple-element.20.to_left_ref, bf16[2,4,64,128]{3,2,1,0:T(8,128)(2,1)} %get-tuple-element.19.own_ref, bf16[2,4,64,128]{3,2,1,0:T(8,128)(2,1)} %get-tuple-element.18.to_right_ref, bf16[4,8,64,128]{3,2,1,0:T(8,128)(2,1)} %beta_ref.1, ...), custom_call_target="tpu_custom_call" | custom-call | flops 2097152 | bytes 1048576 | tf_op jit(solution)/shard_map/pallas_call | solution.py:219
  108.7 1.4 broadcast_select_fusion.1
  110.9 2.5 %convolution_bitcast_fusion = f32[4,1152,256]{1,2,0:T(8,128)S(1)} fusion(s32[768]{0:T(1024)S(1)} %add_select_fusion.5, pred[768]{0:T(1024)(128)(4,1)S(1)} %fusion.79, bf16[2,768,256]{1,2,0:T(8,128)(2,1)S(1)} %get-tuple-element.7, bf16[2,768,256]{1,2,0:T(8,128)(2,1)S(1)} %get-tuple-element.8), kind=kOutput, calls=%fused_computation | convolution fusion | flops 1814495232 | bytes 6295296 | tf_op jit(solution)/shard_map/er,cez->crz/dot_general | solution.py:362
  113.6 2.0 %copy.46 = f32[2,1152,256]{2,1,0:T(8,128)} copy(f32[2,1152,256]{1,2,0:T(8,128)S(1)} %slice_add_fusion) | data formatting | bytes 4718592 | tf_op jit(solution)/shard_map/add | solution.py:368
  115.6 3.7 %fusion.18 = bf16[2,6,192,256]{3,2,0,1:T(8,128)(2,1)S(1)} fusion(f32[2,6,192,256]{3,2,1,0:T(8,128)} %bitcast.165, bf16[2,6,192,256]{3,2,0,1:T(8,128)(2,1)S(1)} %copy-done.1, f32[6,192,256]{2,1,0:T(8,128)} %convert_element_type.196, bf16[1,2,256,256]{3,2,1,0:T(8,128)(2,1)} %get-tuple-element.22, bf16[1,2,256,256]{3,2,1,0:T(8,128)(2,1)} %get-tuple-element.21, ...), kind=kOutput, calls=%fused_computation.31 | convolution fusion | flops 1062141952 | bytes 6717440 | tf_op jit(solution)/shard_map/abyk,bxkz->axyz/dot_general | solution.py:380
  119.3 2.2 %copy.48 = bf16[2,6,192,256]{3,0,1,2:T(2,128)(2,1)} copy(bf16[2,6,192,256]{3,2,0,1:T(8,128)(2,1)S(1)} %fusion.18) | data formatting | bytes 2359296 | tf_op jit(solution)/shard_map/convert_element_type | solution.py:382
  121.5 8.2 %all-to-all-start.1 = ((bf16[2,6,192,256]{3,0,1,2:T(2,128)(2,1)}), bf16[2,6,192,256]{3,0,1,2:T(2,128)(2,1)}, u32[]{:S(2)}, u32[]{:S(2)}) async-start(bf16[2,6,192,256]{3,0,1,2:T(2,128)(2,1)} %copy.48), calls=%async_computation.1 | async-start | bytes 2359296 | tf_op jit(solution)/shard_map/all_to_all | solution.py:386
  130.9 2.3 %fusion.22.part_ref = bf16[16,144,128]{2,1,0:T(8,128)(2,1)} fusion(f32[16,144,128]{2,1,0:T(8,128)S(1)} %reshape.483, f32[16,144,128]{2,1,0:T(8,128)S(1)} %reshape.484, f32[]{:T(128)} %bitcast.64, f32[]{:T(128)} %bitcast.63), kind=kLoop, calls=%fused_computation.35 | loop fusion | flops 1769472 | bytes 2949128 | tf_op jit(solution)/shard_map/convert_element_type | solution.py:328
  133.4 27.3 %shard_map.95 = bf16[16,144,128]{2,1,0:T(8,128)(2,1)} custom-call(bf16[16,144,128]{2,1,0:T(8,128)(2,1)} %fusion.22.part_ref), custom_call_target="tpu_custom_call" | custom-call | flops 294912 | bytes 1769472 | tf_op jit(solution)/shard_map/pallas_call | solution.py:74
  160.7 2.0 %reshape.481 = bf16[6,192,256]{2,1,0:T(8,128)(2,1)} reshape(bf16[16,144,128]{2,1,0:T(8,128)(2,1)} %shard_map.95) | data formatting | bytes 1179648 | tf_op jit(solution)/shard_map/reshape | solution.py:89
  162.8 26.9 %all-to-all-done.1 = bf16[2,6,192,256]{3,0,1,2:T(2,128)(2,1)} async-done(((bf16[2,6,192,256]{3,0,1,2:T(2,128)(2,1)}), bf16[2,6,192,256]{3,0,1,2:T(2,128)(2,1)}, u32[]{:S(2)}, u32[]{:S(2)}) %all-to-all-start.1) | async-done | bytes 1179680 | tf_op jit(solution)/shard_map/all_to_all | solution.py:386
  189.7 2.2 %copy.50 = bf16[2,32,6,6,256]{4,0,3,2,1:T(2,128)(2,1)S(1)} copy(bf16[2,32,6,6,256]{4,0,2,3,1:T(2,128)(2,1)} %bitcast.56) | data formatting | bytes 2359296 | tf_op jit(solution)/shard_map/all_to_all | solution.py:386
  192.0 1.9 fusion.20
  (57 shorter events, 5.6 us)
Async XLA Ops:
  2.9 1.0 copy-start.7
  6.9 18.4 %copy-start.6 = (s32[128,64]{0,1:T(8,128)S(1)}, s32[128,64]{0,1:T(8,128)}, u32[]{:S(2)}) copy-start(s32[128,64]{0,1:T(8,128)} %param.12) | copy-start | bytes 98308
  6.9 19.0 %copy-start.8 = (f32[8,8]{1,0:T(8,128)S(1)}, f32[8,8]{1,0:T(8,128)}, u32[]{:S(2)}) copy-start(f32[8,8]{1,0:T(8,128)} %param.11) | copy-start | bytes 772
  6.9 19.1 %copy-start.5 = (bf16[6,192,256]{2,1,0:T(8,128)(2,1)S(1)}, bf16[6,192,256]{2,1,0:T(8,128)(2,1)}, u32[]{:S(2)}) copy-start(bf16[6,192,256]{2,1,0:T(8,128)(2,1)} %param.9) | copy-start | bytes 1769476
  6.9 77.4 %all-to-all-start = ((bf16[32,2,6,6,256]{4,1,3,2,0:T(2,128)(2,1)}), bf16[32,2,6,6,256]{4,1,3,2,0:T(2,128)(2,1)S(1)}, u32[]{:S(2)}, u32[]{:S(2)}) async-start(bf16[32,2,6,6,256]{4,1,3,2,0:T(2,128)(2,1)} %copy.33), calls=%async_computation | async-start | bytes 2359296 | tf_op jit(solution)/shard_map/all_to_all | solution.py:314
  85.8 1.0 copy-start
  113.6 2.0 %copy-start.1 = (bf16[2,6,192,256]{3,2,0,1:T(8,128)(2,1)S(1)}, bf16[2,6,192,256]{3,2,0,1:T(8,128)(2,1)}, u32[]{:S(2)}) copy-start(bf16[2,6,192,256]{3,2,0,1:T(8,128)(2,1)} %copy-done) | copy-start | bytes 3538948
  121.5 8.3 %copy-start.10 = (f32[1,2]{1,0:T(1,128)S(1)}, f32[1,2]{1,0:T(1,128)}, u32[]{:S(2)}) copy-start(f32[1,2]{1,0:T(1,128)} %param.8) | copy-start | bytes 28
  121.5 68.2 %all-to-all-start.1 = ((bf16[2,6,192,256]{3,0,1,2:T(2,128)(2,1)}), bf16[2,6,192,256]{3,0,1,2:T(2,128)(2,1)}, u32[]{:S(2)}, u32[]{:S(2)}) async-start(bf16[2,6,192,256]{3,0,1,2:T(2,128)(2,1)} %copy.48), calls=%async_computation.1 | async-start | bytes 2359296 | tf_op jit(solution)/shard_map/all_to_all | solution.py:386
  189.7 2.2 %copy-start.2 = (bf16[1,2,192,6,256]{4,2,3,1,0:T(8,128)(2,1)S(1)}, bf16[1,2,192,6,256]{4,2,3,1,0:T(8,128)(2,1)}, u32[]{:S(2)}) copy-start(bf16[1,2,192,6,256]{4,2,3,1,0:T(8,128)(2,1)} %param.7) | copy-start | bytes 3538948
  189.7 2.2 %copy-start.3 = (bf16[1,2,192,192]{3,2,1,0:T(8,128)(2,1)S(1)}, bf16[1,2,192,192]{3,2,1,0:T(8,128)(2,1)}, u32[]{:S(2)}) copy-start(bf16[1,2,192,192]{3,2,1,0:T(8,128)(2,1)} %get-tuple-element.25) | copy-start | bytes 442372
  189.7 2.2 %copy-start.4 = (bf16[1,2,192,192]{3,2,1,0:T(8,128)(2,1)S(1)}, bf16[1,2,192,192]{3,2,1,0:T(8,128)(2,1)}, u32[]{:S(2)}) copy-start(bf16[1,2,192,192]{3,2,1,0:T(8,128)(2,1)} %get-tuple-element.26) | copy-start | bytes 442372
  191.9 1.9 copy-start.9

commit v10 on v9

--- a/solution.py
+++ b/solution.py
@@ -308,9 +308,14 @@
     )
     inverse_y = dft_table(size_y, 1.0)
     inverse_z = dft_table(size_z, 1.0)
-    flattened = coeffs.reshape(2 * size_x, columns * size_z)
-    along_x = jnp.dot(jnp.asarray(table_x), flattened, preferred_element_type=jnp.float32)
-    along_x = along_x.reshape(pieces, 2, slab_planes, columns, size_z).astype(jnp.bfloat16)
+    table_x = jnp.asarray(table_x).reshape(2 * size_x, 2, size_x)
+    along_x = jnp.einsum(
+        "ypcx,cxyz->ypz",
+        jnp.broadcast_to(table_x[None], (columns,) + table_x.shape),
+        coeffs,
+        preferred_element_type=jnp.float32,
+    ).astype(jnp.bfloat16)
+    along_x = along_x.reshape(columns, pieces, 2, slab_planes, size_z).transpose(1, 2, 3, 0, 4)
     arrived = lax.all_to_all(along_x, "fft", split_axis=0, concat_axis=0, tiled=True)
     along_y = jnp.einsum(
         "abysu,sbxuz->axyz",

time: 195 us -> 193 us (0.990)
  local copies, waits for them, and re-layouts: 18.7 us -> 15.5 us
    unnamed x28 -> x24, local copies, waits for them, and re-layouts: 4.57 us -> 2.06 us
    convert_element_type x1 -> x0, local copies, waits for them, and re-layouts: 2.23 us -> none  [per_device(): along_x.reshape(pieces, 2, slab_planes, columns, size_z)]
where the time goes in v10:
time: 193 us
  waiting for transfers between devices  76.4 us (40%)
  Pallas kernels  45.7 us (24%)
  starting transfers between devices  26.5 us (14%)
  local copies, waits for them, and re-layouts  15.5 us (8%)
  other arithmetic  14.3 us (7%)
  matrix products  13.2 us (7%)
    all_to_all x1, waiting for transfers between devices, per_device(): lax.all_to_all(along_x, 'fft', split_axis=0, concat_axis=0, tiled=True)  49 us
    all_to_all x1, waiting for transfers between devices, per_device(): lax.all_to_all(back_y, 'fft', split_axis=2, concat_axis=1, tiled=True)  27.3 us
    pallas_call x1, Pallas kernels, band_sum(): pl.pallas_call(band_sum_kernel, out_shape=jax.ShapeDtypeStruct(chunks.sha...  27 us
    pallas_call x1, Pallas kernels, halo_exchange(): pl.pallas_call(halo_kernel, out_shape=(jax.ShapeDtypeStruct((2 * atoms, 1...  18.7 us
    all_to_all x1, starting transfers between devices, per_device(): lax.all_to_all(along_x, 'fft', split_axis=0, concat_axis=0, tiled=True)  18.3 us
    all_to_all x1, starting transfers between devices, per_device(): lax.all_to_all(back_y, 'fft', split_axis=2, concat_axis=1, tiled=True)  8.19 us
    another operation x6, other arithmetic  5.81 us
  transfers between devices with their start and end apart: 2, of which 2 were waited for; matrix products, arithmetic and copies ran while one was open for 8% of the time, Pallas kernels for 14%

profile of v10, /device:TPU:6, one launch (start us, length us, event | category | flops | bytes accessed | tf_op | source)
XLA Modules:
  0.0 192.7 jit_solution(16131310628025947718)
XLA Ops:
  0.6 2.2 %bitcast_convert_fusion.4 = bf16[6,384,256]{2,1,0:T(8,128)(2,1)S(1)} fusion(bf16[384,2,192]{0,2,1:T(8,128)(2,1)} %constant.152, bf16[1,2,192,6,256]{4,2,3,1,0:T(8,128)(2,1)} %param.7), kind=kOutput, calls=%fused_computation.12 | convolution fusion | flops 453574656 | bytes 2654208 | tf_op jit(solution)/shard_map/ypcx,cxyz->ypz/dot_general | solution.py:312
  3.3 1.9 copy.32
  5.2 18.3 %all-to-all-start = ((bf16[32,2,6,6,256]{4,1,3,2,0:T(2,128)(2,1)}), bf16[32,2,6,6,256]{4,1,3,2,0:T(2,128)(2,1)S(1)}, u32[]{:S(2)}, u32[]{:S(2)}) async-start(bf16[32,2,6,6,256]{4,1,3,2,0:T(2,128)(2,1)} %copy.32), calls=%async_computation | async-start | bytes 2359296 | tf_op jit(solution)/shard_map/all_to_all | solution.py:319
  24.4 1.1 convert_element_type.193
  25.5 0.8 fusion.75
  26.3 1.0 multiply_convert_fusion.2
  27.2 0.8 negate_convert_fusion.3
  28.1 1.0 negate_convert_fusion
  29.1 1.3 multiply_convert_fusion
  30.4 0.8 maximum_bitcast_fusion.8
  31.2 0.9 fusion.58
  32.1 0.6 fusion.81.coupled_ref
  32.7 0.9 negate_convert_fusion.2
  33.6 49.0 %all-to-all-done = bf16[32,2,6,6,256]{4,1,3,2,0:T(2,128)(2,1)S(1)} async-done(((bf16[32,2,6,6,256]{4,1,3,2,0:T(2,128)(2,1)}), bf16[32,2,6,6,256]{4,1,3,2,0:T(2,128)(2,1)S(1)}, u32[]{:S(2)}, u32[]{:S(2)}) %all-to-all-start) | async-done | bytes 1179680 | tf_op jit(solution)/shard_map/all_to_all | solution.py:319
  82.7 1.5 fusion.15
  84.2 0.9 copy-done
  85.2 1.6 fusion.3
  87.5 0.8 slice_bitcast_fusion
  88.3 18.7 %shard_map.94 = (f32[8,128]{1,0:T(8,128)}, f32[2,3,4,64,128]{4,3,2,1,0:T(8,128)}) custom-call(bf16[2,4,64,128]{3,2,1,0:T(8,128)(2,1)} %get-tuple-element.20.to_left_ref, bf16[2,4,64,128]{3,2,1,0:T(8,128)(2,1)} %get-tuple-element.19.own_ref, bf16[2,4,64,128]{3,2,1,0:T(8,128)(2,1)} %get-tuple-element.18.to_right_ref, bf16[4,8,64,128]{3,2,1,0:T(8,128)(2,1)} %beta_ref.1, ...), custom_call_target="tpu_custom_call" | custom-call | flops 2097152 | bytes 1048576 | tf_op jit(solution)/shard_map/pallas_call | solution.py:219
  107.0 1.4 broadcast_select_fusion.1
  109.2 2.5 %convolution_bitcast_fusion = f32[4,1152,256]{1,2,0:T(8,128)S(1)} fusion(s32[768]{0:T(1024)S(1)} %add_select_fusion.5, pred[768]{0:T(1024)(128)(4,1)S(1)} %fusion.80, bf16[2,768,256]{1,2,0:T(8,128)(2,1)S(1)} %get-tuple-element.7, bf16[2,768,256]{1,2,0:T(8,128)(2,1)S(1)} %get-tuple-element.8), kind=kOutput, calls=%fused_computation | convolution fusion | flops 1814495232 | bytes 6295296 | tf_op jit(solution)/shard_map/er,cez->crz/dot_general | solution.py:367
  111.9 2.0 %copy.45 = f32[2,1152,256]{2,1,0:T(8,128)} copy(f32[2,1152,256]{1,2,0:T(8,128)S(1)} %slice_add_fusion) | data formatting | bytes 4718592 | tf_op jit(solution)/shard_map/add | solution.py:373
  113.9 3.7 %fusion.17 = bf16[2,6,192,256]{3,2,0,1:T(8,128)(2,1)S(1)} fusion(f32[2,6,192,256]{3,2,1,0:T(8,128)} %bitcast.156, bf16[2,6,192,256]{3,2,0,1:T(8,128)(2,1)S(1)} %copy-done.1, f32[6,192,256]{2,1,0:T(8,128)} %convert_element_type.193, bf16[1,2,256,256]{3,2,1,0:T(8,128)(2,1)} %get-tuple-element.22, bf16[1,2,256,256]{3,2,1,0:T(8,128)(2,1)} %get-tuple-element.21, ...), kind=kOutput, calls=%fused_computation.30 | convolution fusion | flops 1062141952 | bytes 6717440 | tf_op jit(solution)/shard_map/abyk,bxkz->axyz/dot_general | solution.py:385
  117.5 2.2 %copy.47 = bf16[2,6,192,256]{3,0,1,2:T(2,128)(2,1)} copy(bf16[2,6,192,256]{3,2,0,1:T(8,128)(2,1)S(1)} %fusion.17) | data formatting | bytes 2359296 | tf_op jit(solution)/shard_map/convert_element_type | solution.py:387
  119.8 8.2 %all-to-all-start.1 = ((bf16[2,6,192,256]{3,0,1,2:T(2,128)(2,1)}), bf16[2,6,192,256]{3,0,1,2:T(2,128)(2,1)}, u32[]{:S(2)}, u32[]{:S(2)}) async-start(bf16[2,6,192,256]{3,0,1,2:T(2,128)(2,1)} %copy.47), calls=%async_computation.1 | async-start | bytes 2359296 | tf_op jit(solution)/shard_map/all_to_all | solution.py:391
  128.0 0.6 fusion.97
  129.1 2.3 %fusion.21.part_ref = bf16[16,144,128]{2,1,0:T(8,128)(2,1)} fusion(f32[16,144,128]{2,1,0:T(8,128)S(1)} %reshape.482, f32[16,144,128]{2,1,0:T(8,128)S(1)} %reshape.483, f32[]{:T(128)} %bitcast.61, f32[]{:T(128)} %bitcast.60), kind=kLoop, calls=%fused_computation.34 | loop fusion | flops 1769472 | bytes 2949128 | tf_op jit(solution)/shard_map/convert_element_type | solution.py:333
  131.6 27.0 %shard_map.95 = bf16[16,144,128]{2,1,0:T(8,128)(2,1)} custom-call(bf16[16,144,128]{2,1,0:T(8,128)(2,1)} %fusion.21.part_ref), custom_call_target="tpu_custom_call" | custom-call | flops 294912 | bytes 1769472 | tf_op jit(solution)/shard_map/pallas_call | solution.py:74
  158.6 2.0 %reshape.481 = bf16[6,192,256]{2,1,0:T(8,128)(2,1)} reshape(bf16[16,144,128]{2,1,0:T(8,128)(2,1)} %shard_map.95) | data formatting | bytes 1179648 | tf_op jit(solution)/shard_map/reshape | solution.py:89
  160.7 27.3 %all-to-all-done.1 = bf16[2,6,192,256]{3,0,1,2:T(2,128)(2,1)} async-done(((bf16[2,6,192,256]{3,0,1,2:T(2,128)(2,1)}), bf16[2,6,192,256]{3,0,1,2:T(2,128)(2,1)}, u32[]{:S(2)}, u32[]{:S(2)}) %all-to-all-start.1) | async-done | bytes 1179680 | tf_op jit(solution)/shard_map/all_to_all | solution.py:391
  188.0 2.2 %copy.49 = bf16[2,32,6,6,256]{4,0,3,2,1:T(2,128)(2,1)S(1)} copy(bf16[2,32,6,6,256]{4,0,2,3,1:T(2,128)(2,1)} %bitcast.54) | data formatting | bytes 2359296 | tf_op jit(solution)/shard_map/all_to_all | solution.py:391
  190.2 1.9 fusion.19
  (53 shorter events, 4.3 us)
Async XLA Ops:
  5.2 18.4 %copy-start.6 = (s32[128,64]{0,1:T(8,128)S(1)}, s32[128,64]{0,1:T(8,128)}, u32[]{:S(2)}) copy-start(s32[128,64]{0,1:T(8,128)} %param.12) | copy-start | bytes 98308
  5.2 19.0 %copy-start.7 = (f32[8,8]{1,0:T(8,128)S(1)}, f32[8,8]{1,0:T(8,128)}, u32[]{:S(2)}) copy-start(f32[8,8]{1,0:T(8,128)} %param.11) | copy-start | bytes 772
  5.2 19.1 %copy-start.5 = (bf16[6,192,256]{2,1,0:T(8,128)(2,1)S(1)}, bf16[6,192,256]{2,1,0:T(8,128)(2,1)}, u32[]{:S(2)}) copy-start(bf16[6,192,256]{2,1,0:T(8,128)(2,1)} %param.9) | copy-start | bytes 1769476
  5.2 77.4 %all-to-all-start = ((bf16[32,2,6,6,256]{4,1,3,2,0:T(2,128)(2,1)}), bf16[32,2,6,6,256]{4,1,3,2,0:T(2,128)(2,1)S(1)}, u32[]{:S(2)}, u32[]{:S(2)}) async-start(bf16[32,2,6,6,256]{4,1,3,2,0:T(2,128)(2,1)} %copy.32), calls=%async_computation | async-start | bytes 2359296 | tf_op jit(solution)/shard_map/all_to_all | solution.py:319
  84.1 1.0 copy-start
  111.9 2.0 %copy-start.1 = (bf16[2,6,192,256]{3,2,0,1:T(8,128)(2,1)S(1)}, bf16[2,6,192,256]{3,2,0,1:T(8,128)(2,1)}, u32[]{:S(2)}) copy-start(bf16[2,6,192,256]{3,2,0,1:T(8,128)(2,1)} %copy-done) | copy-start | bytes 3538948
  119.8 8.2 %copy-start.9 = (f32[1,2]{1,0:T(1,128)S(1)}, f32[1,2]{1,0:T(1,128)}, u32[]{:S(2)}) copy-start(f32[1,2]{1,0:T(1,128)} %param.8) | copy-start | bytes 28
  119.8 68.2 %all-to-all-start.1 = ((bf16[2,6,192,256]{3,0,1,2:T(2,128)(2,1)}), bf16[2,6,192,256]{3,0,1,2:T(2,128)(2,1)}, u32[]{:S(2)}, u32[]{:S(2)}) async-start(bf16[2,6,192,256]{3,0,1,2:T(2,128)(2,1)} %copy.47), calls=%async_computation.1 | async-start | bytes 2359296 | tf_op jit(solution)/shard_map/all_to_all | solution.py:391
  188.0 2.2 %copy-start.2 = (bf16[1,2,192,6,256]{4,2,3,1,0:T(8,128)(2,1)S(1)}, bf16[1,2,192,6,256]{4,2,3,1,0:T(8,128)(2,1)}, u32[]{:S(2)}) copy-start(bf16[1,2,192,6,256]{4,2,3,1,0:T(8,128)(2,1)} %param.7) | copy-start | bytes 3538948
  188.0 2.2 %copy-start.3 = (bf16[1,2,192,192]{3,2,1,0:T(8,128)(2,1)S(1)}, bf16[1,2,192,192]{3,2,1,0:T(8,128)(2,1)}, u32[]{:S(2)}) copy-start(bf16[1,2,192,192]{3,2,1,0:T(8,128)(2,1)} %get-tuple-element.25) | copy-start | bytes 442372
  188.0 2.2 %copy-start.4 = (bf16[1,2,192,192]{3,2,1,0:T(8,128)(2,1)S(1)}, bf16[1,2,192,192]{3,2,1,0:T(8,128)(2,1)}, u32[]{:S(2)}) copy-start(bf16[1,2,192,192]{3,2,1,0:T(8,128)(2,1)} %get-tuple-element.26) | copy-start | bytes 442372
  190.2 1.9 copy-start.8

commit v11 on v10

--- a/solution.py
+++ b/solution.py
@@ -364,15 +364,16 @@
     ).reshape(2, -1, size_z)
     upper = placed_halves.astype(jnp.bfloat16)
     lower = (placed_halves - upper.astype(jnp.float32)).astype(jnp.bfloat16)
-    nonlocal_parts = jnp.einsum(
-        "er,cez->crz",
-        selector,
-        jnp.concatenate([upper, lower]),
-        preferred_element_type=jnp.float32,
-    )
-    nonlocal_term = (nonlocal_parts[:2] + nonlocal_parts[2:]).reshape(
-        2, slab_planes, size_y, size_z
-    )
+    scatter_selector = (
+        (jnp.arange(slab_rows, dtype=jnp.int32)[:, None] == row_of[None, :]) & is_mine[None, :]
+    ).astype(jnp.bfloat16)
+    nonlocal_term = jnp.stack(
+        [
+            jnp.dot(scatter_selector, upper[c], preferred_element_type=jnp.float32)
+            + jnp.dot(scatter_selector, lower[c], preferred_element_type=jnp.float32)
+            for c in range(2)
+        ]
+    ).reshape(2, slab_planes, size_y, size_z)
     total_field = (
         potential.astype(jnp.float32)[None] * wave_field.astype(jnp.float32) + nonlocal_term
     ).astype(jnp.bfloat16)

time: 193 us -> 195 us (1.010)
  matrix products: 13.2 us -> 17.1 us
    dot_general x1 -> x4, matrix products: 2.47 us -> 5.47 us  [the longest x2 3.79 us: per_device(): jnp.dot(scatter_selector, upper[c], preferred_element_type=jnp.float32)]
    add x1 -> x0, local copies, waits for them, and re-layouts: 1.98 us -> none  [per_device(): nonlocal_parts[:2] + nonlocal_parts[2:]]
  transfers between devices with their start and end apart: 2 -> 2, of which waited for: 2 -> 2; matrix products, arithmetic and copies ran while one was open for 8% -> 9% of each run, Pallas kernels for 14% -> 14%
where the time goes in v11:
time: 195 us; the launch traced here: 194 us
  waiting for transfers between devices  75.3 us (39%)
  Pallas kernels  45.7 us (23%)
  starting transfers between devices  26.5 us (14%)
  matrix products  17.1 us (9%)
  local copies, waits for them, and re-layouts  14.9 us (8%)
  other arithmetic  13.8 us (7%)
    all_to_all x1, waiting for transfers between devices, per_device(): lax.all_to_all(along_x, 'fft', split_axis=0, concat_axis=0, tiled=True)  48 us
    all_to_all x1, waiting for transfers between devices, per_device(): lax.all_to_all(back_y, 'fft', split_axis=2, concat_axis=1, tiled=True)  27.3 us
    pallas_call x1, Pallas kernels, band_sum(): pl.pallas_call(band_sum_kernel, out_shape=jax.ShapeDtypeStruct(chunks.sha...  27 us
    pallas_call x1, Pallas kernels, halo_exchange(): pl.pallas_call(halo_kernel, out_shape=(jax.ShapeDtypeStruct((2 * atoms, 1...  18.7 us
    all_to_all x1, starting transfers between devices, per_device(): lax.all_to_all(along_x, 'fft', split_axis=0, concat_axis=0, tiled=True)  18.3 us
    all_to_all x1, starting transfers between devices, per_device(): lax.all_to_all(back_y, 'fft', split_axis=2, concat_axis=1, tiled=True)  8.2 us
    another operation x6, other arithmetic  6.52 us
  transfers between devices with their start and end apart: 2, of which 2 were waited for; matrix products, arithmetic and copies ran while one was open for 9% of the time, Pallas kernels for 14%

profile of v11, /device:TPU:6, one launch (start us, length us, event | category | flops | bytes accessed | tf_op | source)
XLA Modules:
  0.0 194.4 jit_solution(6637937340779118057)
XLA Ops:
  0.6 2.2 %bitcast_convert_fusion.4 = bf16[6,384,256]{2,1,0:T(8,128)(2,1)S(1)} fusion(bf16[384,2,192]{0,2,1:T(8,128)(2,1)} %constant.152, bf16[1,2,192,6,256]{4,2,3,1,0:T(8,128)(2,1)} %param.7), kind=kOutput, calls=%fused_computation.20 | convolution fusion | flops 453574656 | bytes 2654208 | tf_op jit(solution)/shard_map/ypcx,cxyz->ypz/dot_general | solution.py:312
  3.3 1.9 copy.30
  5.2 18.3 %all-to-all-start = ((bf16[32,2,6,6,256]{4,1,3,2,0:T(2,128)(2,1)}), bf16[32,2,6,6,256]{4,1,3,2,0:T(2,128)(2,1)S(1)}, u32[]{:S(2)}, u32[]{:S(2)}) async-start(bf16[32,2,6,6,256]{4,1,3,2,0:T(2,128)(2,1)} %copy.30), calls=%async_computation | async-start | bytes 2359296 | tf_op jit(solution)/shard_map/all_to_all | solution.py:319
  24.5 0.8 fusion.92
  25.3 1.0 multiply_convert_fusion.2
  26.3 0.8 negate_convert_fusion.3
  27.1 1.0 negate_convert_fusion
  28.1 1.3 multiply_convert_fusion
  29.4 0.8 maximum_bitcast_fusion.8
  30.2 1.0 fusion.75
  31.8 0.6 add_select_fusion.6
  33.0 1.6 negate_convert_fusion.2
  34.7 48.0 %all-to-all-done = bf16[32,2,6,6,256]{4,1,3,2,0:T(2,128)(2,1)S(1)} async-done(((bf16[32,2,6,6,256]{4,1,3,2,0:T(2,128)(2,1)}), bf16[32,2,6,6,256]{4,1,3,2,0:T(2,128)(2,1)S(1)}, u32[]{:S(2)}, u32[]{:S(2)}) %all-to-all-start) | async-done | bytes 1179680 | tf_op jit(solution)/shard_map/all_to_all | solution.py:319
  82.7 2.7 %fusion.32 = bf16[2,6,192,256]{3,2,0,1:T(8,128)(2,1)S(1)} fusion(bf16[32,2,6,6,256,1]{4,1,3,2,0,5:T(2,128)(2,1)S(1)} %bitcast.168, bf16[1,2,256,256]{3,2,1,0:T(8,128)(2,1)} %get-tuple-element.23, bf16[1,2,256,256]{3,2,1,0:T(8,128)(2,1)} %get-tuple-element.24, bf16[1,1,192,32,6]{2,3,4,1,0:T(8,128)(2,1)} %get-tuple-element.35, ...), kind=kOutput, calls=%fused_computation.37 | convolution fusion | flops 1060372480 | bytes 3104768 | tf_op jit(solution)/shard_map/abzk,bxyk->axyz/dot_general | solution.py:326
  86.1 1.5 fusion.11
  88.4 0.7 slice_bitcast_fusion.8
  89.1 18.7 %shard_map.94 = (f32[8,128]{1,0:T(8,128)}, f32[2,3,4,64,128]{4,3,2,1,0:T(8,128)}) custom-call(bf16[2,4,64,128]{3,2,1,0:T(8,128)(2,1)} %get-tuple-element.20.to_left_ref, bf16[2,4,64,128]{3,2,1,0:T(8,128)(2,1)} %get-tuple-element.19.own_ref, bf16[2,4,64,128]{3,2,1,0:T(8,128)(2,1)} %get-tuple-element.18.to_right_ref, bf16[4,8,64,128]{3,2,1,0:T(8,128)(2,1)} %beta_ref.1, ...), custom_call_target="tpu_custom_call" | custom-call | flops 2097152 | bytes 1048576 | tf_op jit(solution)/shard_map/pallas_call | solution.py:219
  107.9 1.4 copy.42
  110.2 0.8 fusion.5
  111.1 0.8 fusion.1
  111.9 1.9 fusion.13
  113.8 1.9 fusion.16
  115.7 3.3 %fusion.34 = bf16[2,6,192,256]{3,2,0,1:T(8,128)(2,1)S(1)} fusion(f32[1,6,192,256]{3,2,0,1:T(8,128)} %bitcast.180, f32[1,6,192,256]{3,2,0,1:T(8,128)} %bitcast.179, bf16[2,6,192,256]{3,2,0,1:T(8,128)(2,1)S(1)} %fusion.32, f32[6,192,256]{2,1,0:T(8,128)S(1)} %convert_element_type.194, bf16[1,2,256,256]{3,2,1,0:T(8,128)(2,1)} %get-tuple-element.22, ...), kind=kOutput, calls=%fused_computation.39 | convolution fusion | flops 1062731776 | bytes 6717440 | tf_op jit(solution)/shard_map/abyk,bxkz->axyz/dot_general | solution.py:386
  119.0 2.4 %copy.44 = bf16[2,6,192,256]{3,0,1,2:T(2,128)(2,1)} copy(bf16[2,6,192,256]{3,2,0,1:T(8,128)(2,1)S(1)} %fusion.34) | data formatting | bytes 2359296 | tf_op jit(solution)/shard_map/convert_element_type | solution.py:388
  121.5 8.2 %all-to-all-start.1 = ((bf16[2,6,192,256]{3,0,1,2:T(2,128)(2,1)}), bf16[2,6,192,256]{3,0,1,2:T(2,128)(2,1)}, u32[]{:S(2)}, u32[]{:S(2)}) async-start(bf16[2,6,192,256]{3,0,1,2:T(2,128)(2,1)} %copy.44), calls=%async_computation.1 | async-start | bytes 2359296 | tf_op jit(solution)/shard_map/all_to_all | solution.py:392
  129.7 0.6 fusion.115
  130.8 2.3 %fusion.38.part_ref = bf16[16,144,128]{2,1,0:T(8,128)(2,1)} fusion(f32[16,144,128]{2,1,0:T(8,128)S(1)} %reshape.522, f32[16,144,128]{2,1,0:T(8,128)S(1)} %reshape.523, f32[]{:T(128)} %bitcast.65, f32[]{:T(128)} %bitcast.64), kind=kLoop, calls=%fused_computation.43 | loop fusion | flops 1769472 | bytes 2949128 | tf_op jit(solution)/shard_map/convert_element_type | solution.py:333
  133.4 27.0 %shard_map.95 = bf16[16,144,128]{2,1,0:T(8,128)(2,1)} custom-call(bf16[16,144,128]{2,1,0:T(8,128)(2,1)} %fusion.38.part_ref), custom_call_target="tpu_custom_call" | custom-call | flops 294912 | bytes 1769472 | tf_op jit(solution)/shard_map/pallas_call | solution.py:74
  160.3 2.0 %reshape.521 = bf16[6,192,256]{2,1,0:T(8,128)(2,1)} reshape(bf16[16,144,128]{2,1,0:T(8,128)(2,1)} %shard_map.95) | data formatting | bytes 1179648 | tf_op jit(solution)/shard_map/reshape | solution.py:89
  162.4 27.3 %all-to-all-done.1 = bf16[2,6,192,256]{3,0,1,2:T(2,128)(2,1)} async-done(((bf16[2,6,192,256]{3,0,1,2:T(2,128)(2,1)}), bf16[2,6,192,256]{3,0,1,2:T(2,128)(2,1)}, u32[]{:S(2)}, u32[]{:S(2)}) %all-to-all-start.1) | async-done | bytes 1179680 | tf_op jit(solution)/shard_map/all_to_all | solution.py:392
  189.7 2.2 %copy.46 = bf16[2,32,6,6,256]{4,0,3,2,1:T(2,128)(2,1)S(1)} copy(bf16[2,32,6,6,256]{4,0,2,3,1:T(2,128)(2,1)} %bitcast.58) | data formatting | bytes 2359296 | tf_op jit(solution)/shard_map/all_to_all | solution.py:392
  191.9 1.9 fusion.36
  (58 shorter events, 6.1 us)
Async XLA Ops:
  5.2 18.4 %copy-start.4 = (s32[128,64]{0,1:T(8,128)S(1)}, s32[128,64]{0,1:T(8,128)}, u32[]{:S(2)}) copy-start(s32[128,64]{0,1:T(8,128)} %param.12) | copy-start | bytes 98308
  5.2 19.0 %copy-start.5 = (f32[8,8]{1,0:T(8,128)S(1)}, f32[8,8]{1,0:T(8,128)}, u32[]{:S(2)}) copy-start(f32[8,8]{1,0:T(8,128)} %param.11) | copy-start | bytes 772
  5.2 19.1 %copy-start.3 = (bf16[6,192,256]{2,1,0:T(8,128)(2,1)S(1)}, bf16[6,192,256]{2,1,0:T(8,128)(2,1)}, u32[]{:S(2)}) copy-start(bf16[6,192,256]{2,1,0:T(8,128)(2,1)} %param.9) | copy-start | bytes 1769476
  5.2 77.4 %all-to-all-start = ((bf16[32,2,6,6,256]{4,1,3,2,0:T(2,128)(2,1)}), bf16[32,2,6,6,256]{4,1,3,2,0:T(2,128)(2,1)S(1)}, u32[]{:S(2)}, u32[]{:S(2)}) async-start(bf16[32,2,6,6,256]{4,1,3,2,0:T(2,128)(2,1)} %copy.30), calls=%async_computation | async-start | bytes 2359296 | tf_op jit(solution)/shard_map/all_to_all | solution.py:319
  85.4 0.7 copy-start.7
  85.4 0.7 copy-start.10
  109.5 0.7 copy-start.8
  109.6 0.7 copy-start.11
  121.5 8.3 %copy-start.9 = (f32[1,2]{1,0:T(1,128)S(1)}, f32[1,2]{1,0:T(1,128)}, u32[]{:S(2)}) copy-start(f32[1,2]{1,0:T(1,128)} %param.8) | copy-start | bytes 28
  121.5 68.2 %all-to-all-start.1 = ((bf16[2,6,192,256]{3,0,1,2:T(2,128)(2,1)}), bf16[2,6,192,256]{3,0,1,2:T(2,128)(2,1)}, u32[]{:S(2)}, u32[]{:S(2)}) async-start(bf16[2,6,192,256]{3,0,1,2:T(2,128)(2,1)} %copy.44), calls=%async_computation.1 | async-start | bytes 2359296 | tf_op jit(solution)/shard_map/all_to_all | solution.py:392
  189.7 2.2 %copy-start = (bf16[1,2,192,6,256]{4,2,3,1,0:T(8,128)(2,1)S(1)}, bf16[1,2,192,6,256]{4,2,3,1,0:T(8,128)(2,1)}, u32[]{:S(2)}) copy-start(bf16[1,2,192,6,256]{4,2,3,1,0:T(8,128)(2,1)} %param.7) | copy-start | bytes 3538948
  189.7 2.2 %copy-start.1 = (bf16[1,2,192,192]{3,2,1,0:T(8,128)(2,1)S(1)}, bf16[1,2,192,192]{3,2,1,0:T(8,128)(2,1)}, u32[]{:S(2)}) copy-start(bf16[1,2,192,192]{3,2,1,0:T(8,128)(2,1)} %get-tuple-element.25) | copy-start | bytes 442372
  189.7 2.2 %copy-start.2 = (bf16[1,2,192,192]{3,2,1,0:T(8,128)(2,1)S(1)}, bf16[1,2,192,192]{3,2,1,0:T(8,128)(2,1)}, u32[]{:S(2)}) copy-start(bf16[1,2,192,192]{3,2,1,0:T(8,128)(2,1)} %get-tuple-element.26) | copy-start | bytes 442372
  191.9 1.9 copy-start.6

commit v12 on v10

--- a/solution.py
+++ b/solution.py
@@ -144,8 +144,8 @@
 
 
 def halo_kernel(
-    to_left_ref, own_ref, to_right_ref, beta_ref, coupled_ref,
-    proj_ref, spread_ref,
+    to_left_ref, own_ref, to_right_ref, beta_ref, coupled_ref, lower_half_ref,
+    proj_ref, placed_ref,
     landed, outgoing, landed_spread, sems,
 ):
     count = lax.axis_size("fft")
@@ -205,24 +205,38 @@
                 for j in range(1, nproj):
                     energy = energy + sums[j] * coupled_ref[i, j]
                 spread = spread + beta_ref[a, i].astype(jnp.float32) * energy
-            spread_ref[c, 1, a] = spread
+            place(placed_ref, lower_half_ref, c, 1, a, spread)
             outgoing[c, a] = spread.astype(outgoing.dtype)
     swap(outgoing, outgoing, landed_spread, 4)
     for c in range(2):
-        spread_ref[c, 0] = landed_spread[1, c].astype(jnp.float32)
-        spread_ref[c, 2] = landed_spread[0, c].astype(jnp.float32)
-
-
-def halo_exchange(to_left, own, to_right, projectors, coupled):
+        for a in range(atoms):
+            place(placed_ref, lower_half_ref, c, 0, a, landed_spread[1, c, a].astype(jnp.float32))
+            place(placed_ref, lower_half_ref, c, 2, a, landed_spread[0, c, a].astype(jnp.float32))
+
+
+def place(placed_ref, lower_half_ref, c, side, a, value):
+    width = value.shape[-1]
+    keep = lower_half_ref[side, a]
+    upper = value.astype(jnp.bfloat16)
+    lower = (value - upper.astype(jnp.float32)).astype(jnp.bfloat16)
+    for part, piece in ((0, upper), (1, lower)):
+        piece = piece.astype(jnp.float32)
+        placed_ref[2 * part + c, side, a, :, pl.ds(0, width)] = (piece * keep).astype(jnp.bfloat16)
+        placed_ref[2 * part + c, side, a, :, pl.ds(width, width)] = (
+            piece * (1.0 - keep)
+        ).astype(jnp.bfloat16)
+
+
+def halo_exchange(to_left, own, to_right, projectors, coupled, lower_half):
     atoms = projectors.shape[0]
     vmem = pl.BlockSpec(memory_space=pltpu.VMEM)
     return pl.pallas_call(
         halo_kernel,
         out_shape=(
             jax.ShapeDtypeStruct((2 * atoms, 128), jnp.float32),
-            jax.ShapeDtypeStruct((2, 3) + own.shape[1:], jnp.float32),
-        ),
-        in_specs=[vmem, vmem, vmem, vmem, pl.BlockSpec(memory_space=pltpu.SMEM)],
+            jax.ShapeDtypeStruct((4, 3) + own.shape[1:-1] + (2 * own.shape[-1],), jnp.bfloat16),
+        ),
+        in_specs=[vmem, vmem, vmem, vmem, pl.BlockSpec(memory_space=pltpu.SMEM), vmem],
         out_specs=(vmem, vmem),
         scratch_shapes=[
             pltpu.VMEM((2,) + own.shape, jnp.bfloat16),
@@ -234,7 +248,7 @@
         cost_estimate=pl.CostEstimate(
             flops=8 * projectors.size, bytes_accessed=16 * own.size, transcendentals=0
         ),
-    )(to_left, own, to_right, projectors, coupled)
+    )(to_left, own, to_right, projectors, coupled, lower_half)
 
 
 def extended_2(shard, sides, width):
@@ -354,20 +368,18 @@
     for q in range(zblocks):
         picked = jnp.where(half_of == q, picked_rows[:, :, q], picked)
     picked = picked.astype(jnp.bfloat16).reshape(2, 3, atom_dev, -1, block_cells)
-    proj_rows, spread_all = halo_exchange(
-        picked[:, 0], picked[:, 1], picked[:, 2], projectors, coupled
+    lower_half = jnp.broadcast_to(
+        (half_of == 0).astype(jnp.float32).reshape(3, atom_dev, -1, 1),
+        (3, atom_dev, projectors.shape[2], block_cells),
+    )
+    proj_rows, placed = halo_exchange(
+        picked[:, 0], picked[:, 1], picked[:, 2], projectors, coupled, lower_half
     )
     projections_own = proj_rows[:, :nproj_count].reshape(atom_dev, 2, nproj_count)
-    spread_all = spread_all.reshape(2, -1, 1, block_cells)
-    placed_halves = jnp.concatenate(
-        [jnp.where(half_of[..., None] == q, spread_all, 0.0) for q in range(zblocks)], axis=2
-    ).reshape(2, -1, size_z)
-    upper = placed_halves.astype(jnp.bfloat16)
-    lower = (placed_halves - upper.astype(jnp.float32)).astype(jnp.bfloat16)
     nonlocal_parts = jnp.einsum(
         "er,cez->crz",
         selector,
-        jnp.concatenate([upper, lower]),
+        placed.reshape(4, -1, size_z),
         preferred_element_type=jnp.float32,
     )
     nonlocal_term = (nonlocal_parts[:2] + nonlocal_parts[2:]).reshape(

time: 193 us -> 193 us (level)
  no operation moved by 1% of the time
where the time goes in v12:
time: 193 us
  waiting for transfers between devices  75.9 us (39%)
  Pallas kernels  46.7 us (24%)
  starting transfers between devices  26.5 us (14%)
  local copies, waits for them, and re-layouts  15.1 us (8%)
  matrix products  14.7 us (8%)
  other arithmetic  12.7 us (7%)
    all_to_all x1, waiting for transfers between devices, per_device(): lax.all_to_all(along_x, 'fft', split_axis=0, concat_axis=0, tiled=True)  49 us
    pallas_call x1, Pallas kernels, band_sum(): pl.pallas_call(band_sum_kernel, out_shape=jax.ShapeDtypeStruct(chunks.sha...  27.3 us
    all_to_all x1, waiting for transfers between devices, per_device(): lax.all_to_all(back_y, 'fft', split_axis=2, concat_axis=1, tiled=True)  26.9 us
    pallas_call x1, Pallas kernels, halo_exchange(): pl.pallas_call(halo_kernel, out_shape=(jax.ShapeDtypeStruct((2 * atoms, 1...  19.4 us
    all_to_all x1, starting transfers between devices, per_device(): lax.all_to_all(along_x, 'fft', split_axis=0, concat_axis=0, tiled=True)  18.3 us
    all_to_all x1, starting transfers between devices, per_device(): lax.all_to_all(back_y, 'fft', split_axis=2, concat_axis=1, tiled=True)  8.18 us
    another operation x6, other arithmetic  5.81 us
    dot_general x1, matrix products, per_device(): jnp.einsum('er,cez->crz', selector, placed.reshape(4, -1, size_z), prefer...  3.88 us
  transfers between devices with their start and end apart: 2, of which 2 were waited for; matrix products, arithmetic and copies ran while one was open for 8% of the time, Pallas kernels for 14%

profile of v12, /device:TPU:6, one launch (start us, length us, event | category | flops | bytes accessed | tf_op | source)
XLA Modules:
  0.0 192.6 jit_solution(14880931717781811111)
XLA Ops:
  0.6 2.2 %bitcast_convert_fusion.4 = bf16[6,384,256]{2,1,0:T(8,128)(2,1)S(1)} fusion(bf16[384,2,192]{0,2,1:T(8,128)(2,1)} %constant.149, bf16[1,2,192,6,256]{4,2,3,1,0:T(8,128)(2,1)} %param.7), kind=kOutput, calls=%fused_computation.12 | convolution fusion | flops 453574656 | bytes 2654208 | tf_op jit(solution)/shard_map/ypcx,cxyz->ypz/dot_general | solution.py:326
  3.3 1.9 copy.32
  5.2 18.3 %all-to-all-start = ((bf16[32,2,6,6,256]{4,1,3,2,0:T(2,128)(2,1)}), bf16[32,2,6,6,256]{4,1,3,2,0:T(2,128)(2,1)S(1)}, u32[]{:S(2)}, u32[]{:S(2)}) async-start(bf16[32,2,6,6,256]{4,1,3,2,0:T(2,128)(2,1)} %copy.32), calls=%async_computation | async-start | bytes 2359296 | tf_op jit(solution)/shard_map/all_to_all | solution.py:333
  24.4 1.1 convert_element_type.193
  25.5 0.8 fusion.71
  26.3 1.0 multiply_convert_fusion.2
  27.3 0.8 negate_convert_fusion.3
  28.1 1.0 negate_convert_fusion
  29.1 1.3 multiply_convert_fusion
  30.4 0.8 maximum_bitcast_fusion.8
  31.3 0.9 fusion.54
  32.2 0.6 fusion.78.coupled_ref
  32.8 0.9 negate_convert_fusion.2
  33.7 49.0 %all-to-all-done = bf16[32,2,6,6,256]{4,1,3,2,0:T(2,128)(2,1)S(1)} async-done(((bf16[32,2,6,6,256]{4,1,3,2,0:T(2,128)(2,1)}), bf16[32,2,6,6,256]{4,1,3,2,0:T(2,128)(2,1)S(1)}, u32[]{:S(2)}, u32[]{:S(2)}) %all-to-all-start) | async-done | bytes 1179680 | tf_op jit(solution)/shard_map/all_to_all | solution.py:333
  82.7 1.5 fusion.11
  84.2 1.6 fusion.3
  86.6 0.8 slice_bitcast_fusion
  87.4 0.9 broadcast_in_dim.28.lower_half_ref
  88.3 19.4 %shard_map.94 = (f32[8,128]{1,0:T(8,128)}, bf16[4,3,4,64,256]{4,3,2,1,0:T(8,128)(2,1)}) custom-call(bf16[2,4,64,128]{3,2,1,0:T(8,128)(2,1)} %get-tuple-element.17.to_left_ref, bf16[2,4,64,128]{3,2,1,0:T(8,128)(2,1)} %get-tuple-element.16.own_ref, bf16[2,4,64,128]{3,2,1,0:T(8,128)(2,1)} %get-tuple-element.15.to_right_ref, bf16[4,8,64,128]{3,2,1,0:T(8,128)(2,1)} %beta_ref.1, ...), custom_call_target="tpu_custom_call" | custom-call | flops 2097152 | bytes 1048576 | tf_op jit(solution)/shard_map/pallas_call | solution.py:233
  107.6 3.9 %convolution_bitcast_fusion = f32[4,1152,256]{1,2,0:T(8,128)S(1)} fusion(bf16[4,768,256]{2,1,0:T(8,128)(2,1)} %bitcast.164, s32[768]{0:T(1024)S(1)} %add_select_fusion.5, pred[768]{0:T(1024)(128)(4,1)S(1)} %fusion.77), kind=kOutput, calls=%fused_computation | convolution fusion | flops 1813708800 | bytes 6295296 | tf_op jit(solution)/shard_map/er,cez->crz/dot_general | solution.py:379
  111.8 2.0 %copy.45 = f32[2,1152,256]{2,1,0:T(8,128)} copy(f32[2,1152,256]{1,2,0:T(8,128)S(1)} %slice_add_fusion) | data formatting | bytes 4718592 | tf_op jit(solution)/shard_map/add | solution.py:385
  113.8 3.7 %fusion.13 = bf16[2,6,192,256]{3,2,0,1:T(8,128)(2,1)S(1)} fusion(f32[2,6,192,256]{3,2,1,0:T(8,128)} %bitcast.151, bf16[2,6,192,256]{3,2,0,1:T(8,128)(2,1)S(1)} %fusion.11, f32[6,192,256]{2,1,0:T(8,128)} %convert_element_type.193, bf16[1,2,256,256]{3,2,1,0:T(8,128)(2,1)} %get-tuple-element.19, bf16[1,2,256,256]{3,2,1,0:T(8,128)(2,1)} %get-tuple-element.18, ...), kind=kOutput, calls=%fused_computation.23 | convolution fusion | flops 1062141952 | bytes 6717440 | tf_op jit(solution)/shard_map/abyk,bxkz->axyz/dot_general | solution.py:397
  117.4 2.2 %copy.47 = bf16[2,6,192,256]{3,0,1,2:T(2,128)(2,1)} copy(bf16[2,6,192,256]{3,2,0,1:T(8,128)(2,1)S(1)} %fusion.13) | data formatting | bytes 2359296 | tf_op jit(solution)/shard_map/convert_element_type | solution.py:399
  119.7 8.2 %all-to-all-start.1 = ((bf16[2,6,192,256]{3,0,1,2:T(2,128)(2,1)}), bf16[2,6,192,256]{3,0,1,2:T(2,128)(2,1)}, u32[]{:S(2)}, u32[]{:S(2)}) async-start(bf16[2,6,192,256]{3,0,1,2:T(2,128)(2,1)} %copy.47), calls=%async_computation.1 | async-start | bytes 2359296 | tf_op jit(solution)/shard_map/all_to_all | solution.py:403
  127.9 0.7 fusion.93
  129.0 2.3 %fusion.17.part_ref = bf16[16,144,128]{2,1,0:T(8,128)(2,1)} fusion(f32[16,144,128]{2,1,0:T(8,128)S(1)} %reshape.457, f32[16,144,128]{2,1,0:T(8,128)S(1)} %reshape.458, f32[]{:T(128)} %bitcast.60, f32[]{:T(128)} %bitcast.59), kind=kLoop, calls=%fused_computation.27 | loop fusion | flops 1769472 | bytes 2949128 | tf_op jit(solution)/shard_map/convert_element_type | solution.py:347
  131.6 27.3 %shard_map.95 = bf16[16,144,128]{2,1,0:T(8,128)(2,1)} custom-call(bf16[16,144,128]{2,1,0:T(8,128)(2,1)} %fusion.17.part_ref), custom_call_target="tpu_custom_call" | custom-call | flops 294912 | bytes 1769472 | tf_op jit(solution)/shard_map/pallas_call | solution.py:74
  158.9 2.0 %reshape.456 = bf16[6,192,256]{2,1,0:T(8,128)(2,1)} reshape(bf16[16,144,128]{2,1,0:T(8,128)(2,1)} %shard_map.95) | data formatting | bytes 1179648 | tf_op jit(solution)/shard_map/reshape | solution.py:89
  160.9 26.9 %all-to-all-done.1 = bf16[2,6,192,256]{3,0,1,2:T(2,128)(2,1)} async-done(((bf16[2,6,192,256]{3,0,1,2:T(2,128)(2,1)}), bf16[2,6,192,256]{3,0,1,2:T(2,128)(2,1)}, u32[]{:S(2)}, u32[]{:S(2)}) %all-to-all-start.1) | async-done | bytes 1179680 | tf_op jit(solution)/shard_map/all_to_all | solution.py:403
  187.9 2.2 %copy.49 = bf16[2,32,6,6,256]{4,0,3,2,1:T(2,128)(2,1)S(1)} copy(bf16[2,32,6,6,256]{4,0,2,3,1:T(2,128)(2,1)} %bitcast.53) | data formatting | bytes 2359296 | tf_op jit(solution)/shard_map/all_to_all | solution.py:403
  190.1 1.9 fusion.15
  192.0 0.6 copy.94
  (45 shorter events, 2.9 us)
Async XLA Ops:
  5.2 18.4 %copy-start.4 = (s32[128,64]{0,1:T(8,128)S(1)}, s32[128,64]{0,1:T(8,128)}, u32[]{:S(2)}) copy-start(s32[128,64]{0,1:T(8,128)} %param.12) | copy-start | bytes 98308
  5.2 19.0 %copy-start.5 = (f32[8,8]{1,0:T(8,128)S(1)}, f32[8,8]{1,0:T(8,128)}, u32[]{:S(2)}) copy-start(f32[8,8]{1,0:T(8,128)} %param.11) | copy-start | bytes 772
  5.2 19.1 %copy-start.3 = (bf16[6,192,256]{2,1,0:T(8,128)(2,1)S(1)}, bf16[6,192,256]{2,1,0:T(8,128)(2,1)}, u32[]{:S(2)}) copy-start(bf16[6,192,256]{2,1,0:T(8,128)(2,1)} %param.9) | copy-start | bytes 1769476
  5.2 77.4 %all-to-all-start = ((bf16[32,2,6,6,256]{4,1,3,2,0:T(2,128)(2,1)}), bf16[32,2,6,6,256]{4,1,3,2,0:T(2,128)(2,1)S(1)}, u32[]{:S(2)}, u32[]{:S(2)}) async-start(bf16[32,2,6,6,256]{4,1,3,2,0:T(2,128)(2,1)} %copy.32), calls=%async_computation | async-start | bytes 2359296 | tf_op jit(solution)/shard_map/all_to_all | solution.py:333
  119.7 8.2 %copy-start.7 = (f32[1,2]{1,0:T(1,128)S(1)}, f32[1,2]{1,0:T(1,128)}, u32[]{:S(2)}) copy-start(f32[1,2]{1,0:T(1,128)} %param.8) | copy-start | bytes 28
  119.7 68.2 %all-to-all-start.1 = ((bf16[2,6,192,256]{3,0,1,2:T(2,128)(2,1)}), bf16[2,6,192,256]{3,0,1,2:T(2,128)(2,1)}, u32[]{:S(2)}, u32[]{:S(2)}) async-start(bf16[2,6,192,256]{3,0,1,2:T(2,128)(2,1)} %copy.47), calls=%async_computation.1 | async-start | bytes 2359296 | tf_op jit(solution)/shard_map/all_to_all | solution.py:403
  187.9 2.2 %copy-start = (bf16[1,2,192,6,256]{4,2,3,1,0:T(8,128)(2,1)S(1)}, bf16[1,2,192,6,256]{4,2,3,1,0:T(8,128)(2,1)}, u32[]{:S(2)}) copy-start(bf16[1,2,192,6,256]{4,2,3,1,0:T(8,128)(2,1)} %param.7) | copy-start | bytes 3538948
  187.9 2.2 %copy-start.1 = (bf16[1,2,192,192]{3,2,1,0:T(8,128)(2,1)S(1)}, bf16[1,2,192,192]{3,2,1,0:T(8,128)(2,1)}, u32[]{:S(2)}) copy-start(bf16[1,2,192,192]{3,2,1,0:T(8,128)(2,1)} %get-tuple-element.22) | copy-start | bytes 442372
  187.9 2.2 %copy-start.2 = (bf16[1,2,192,192]{3,2,1,0:T(8,128)(2,1)S(1)}, bf16[1,2,192,192]{3,2,1,0:T(8,128)(2,1)}, u32[]{:S(2)}) copy-start(bf16[1,2,192,192]{3,2,1,0:T(8,128)(2,1)} %get-tuple-element.23) | copy-start | bytes 442372
  190.1 1.9 copy-start.6

commit v13 on v12

--- a/solution.py
+++ b/solution.py
@@ -368,10 +368,7 @@
     for q in range(zblocks):
         picked = jnp.where(half_of == q, picked_rows[:, :, q], picked)
     picked = picked.astype(jnp.bfloat16).reshape(2, 3, atom_dev, -1, block_cells)
-    lower_half = jnp.broadcast_to(
-        (half_of == 0).astype(jnp.float32).reshape(3, atom_dev, -1, 1),
-        (3, atom_dev, projectors.shape[2], block_cells),
-    )
+    lower_half = (half_of == 0).astype(jnp.float32).reshape(3, atom_dev, -1, 1)
     proj_rows, placed = halo_exchange(
         picked[:, 0], picked[:, 1], picked[:, 2], projectors, coupled, lower_half
     )

time: 193 us -> 192 us (level)
  transfers between devices with their start and end apart: 2 -> 2, of which waited for: 2 -> 2; matrix products, arithmetic and copies ran while one was open for 8% -> 9% of each run, Pallas kernels for 14% -> 14%
where the time goes in v13:
time: 192 us
  waiting for transfers between devices  74.9 us (39%)
  Pallas kernels  46.5 us (24%)
  starting transfers between devices  26.5 us (14%)
  matrix products  14.7 us (8%)
  local copies, waits for them, and re-layouts  14.6 us (8%)
  other arithmetic  13.7 us (7%)
    all_to_all x1, waiting for transfers between devices, per_device(): lax.all_to_all(along_x, 'fft', split_axis=0, concat_axis=0, tiled=True)  47.6 us
    all_to_all x1, waiting for transfers between devices, per_device(): lax.all_to_all(back_y, 'fft', split_axis=2, concat_axis=1, tiled=True)  27.3 us
    pallas_call x1, Pallas kernels, band_sum(): pl.pallas_call(band_sum_kernel, out_shape=jax.ShapeDtypeStruct(chunks.sha...  27 us
    pallas_call x1, Pallas kernels, halo_exchange(): pl.pallas_call(halo_kernel, out_shape=(jax.ShapeDtypeStruct((2 * atoms, 1...  19.5 us
    all_to_all x1, starting transfers between devices, per_device(): lax.all_to_all(along_x, 'fft', split_axis=0, concat_axis=0, tiled=True)  18.3 us
    all_to_all x1, starting transfers between devices, per_device(): lax.all_to_all(back_y, 'fft', split_axis=2, concat_axis=1, tiled=True)  8.17 us
    another operation x6, other arithmetic  5.81 us
    dot_general x1, matrix products, per_device(): jnp.einsum('er,cez->crz', selector, placed.reshape(4, -1, size_z), prefer...  3.88 us
  transfers between devices with their start and end apart: 2, of which 2 were waited for; matrix products, arithmetic and copies ran while one was open for 9% of the time, Pallas kernels for 14%

profile of v13, /device:TPU:6, one launch (start us, length us, event | category | flops | bytes accessed | tf_op | source)
XLA Modules:
  0.0 191.8 jit_solution(10293432970357533495)
XLA Ops:
  0.6 2.2 %bitcast_convert_fusion.4 = bf16[6,384,256]{2,1,0:T(8,128)(2,1)S(1)} fusion(bf16[384,2,192]{0,2,1:T(8,128)(2,1)} %constant.149, bf16[1,2,192,6,256]{4,2,3,1,0:T(8,128)(2,1)} %param.7), kind=kOutput, calls=%fused_computation.12 | convolution fusion | flops 453574656 | bytes 2654208 | tf_op jit(solution)/shard_map/ypcx,cxyz->ypz/dot_general | solution.py:326
  3.3 1.9 %copy.70 = bf16[32,2,6,6,256]{4,1,3,2,0:T(2,128)(2,1)} copy(bf16[32,2,6,6,256]{4,2,1,0,3:T(8,128)(2,1)S(1)} %bitcast.152) | data formatting | bytes 2359296 | tf_op jit(solution)/shard_map/transpose | solution.py:332
  5.2 18.3 %all-to-all-start = ((bf16[32,2,6,6,256]{4,1,3,2,0:T(2,128)(2,1)}), bf16[32,2,6,6,256]{4,1,3,2,0:T(2,128)(2,1)S(1)}, u32[]{:S(2)}, u32[]{:S(2)}) async-start(bf16[32,2,6,6,256]{4,1,3,2,0:T(2,128)(2,1)} %copy.70), calls=%async_computation | async-start | bytes 2359296 | tf_op jit(solution)/shard_map/all_to_all | solution.py:333
  24.8 1.1 convert_element_type.196
  26.0 0.8 fusion.74
  26.8 1.0 multiply_convert_fusion.2
  27.8 0.8 negate_convert_fusion.3
  28.6 1.0 negate_convert_fusion
  29.6 1.3 multiply_convert_fusion
  30.9 0.8 maximum_bitcast_fusion.8
  31.7 0.9 fusion.57
  32.6 0.6 fusion.81.coupled_ref
  33.2 0.9 negate_convert_fusion.2
  34.2 0.9 fusion.53.lower_half_ref
  35.1 47.6 %all-to-all-done = bf16[32,2,6,6,256]{4,1,3,2,0:T(2,128)(2,1)S(1)} async-done(((bf16[32,2,6,6,256]{4,1,3,2,0:T(2,128)(2,1)}), bf16[32,2,6,6,256]{4,1,3,2,0:T(2,128)(2,1)S(1)}, u32[]{:S(2)}, u32[]{:S(2)}) %all-to-all-start) | async-done | bytes 1179680 | tf_op jit(solution)/shard_map/all_to_all | solution.py:333
  82.7 1.5 fusion.11
  84.2 1.6 fusion.3
  86.6 0.8 slice_bitcast_fusion
  87.4 19.5 %shard_map.94 = (f32[8,128]{1,0:T(8,128)}, bf16[4,3,4,64,256]{4,3,2,1,0:T(8,128)(2,1)}) custom-call(bf16[2,4,64,128]{3,2,1,0:T(8,128)(2,1)} %get-tuple-element.18.to_left_ref, bf16[2,4,64,128]{3,2,1,0:T(8,128)(2,1)} %get-tuple-element.17.own_ref, bf16[2,4,64,128]{3,2,1,0:T(8,128)(2,1)} %get-tuple-element.16.to_right_ref, bf16[4,8,64,128]{3,2,1,0:T(8,128)(2,1)} %beta_ref.1, ...), custom_call_target="tpu_custom_call" | custom-call | flops 2097152 | bytes 1048576 | tf_op jit(solution)/shard_map/pallas_call | solution.py:233
  106.9 3.9 %convolution_bitcast_fusion = f32[4,1152,256]{1,2,0:T(8,128)S(1)} fusion(bf16[4,768,256]{2,1,0:T(8,128)(2,1)} %bitcast.170, s32[768]{0:T(1024)S(1)} %add_select_fusion.6, pred[768]{0:T(1024)(128)(4,1)S(1)} %fusion.80), kind=kOutput, calls=%fused_computation | convolution fusion | flops 1813708800 | bytes 6295296 | tf_op jit(solution)/shard_map/er,cez->crz/dot_general | solution.py:376
  111.0 2.0 %copy.91 = f32[2,1152,256]{2,1,0:T(8,128)} copy(f32[2,1152,256]{1,2,0:T(8,128)S(1)} %slice_add_fusion) | data formatting | bytes 4718592 | tf_op jit(solution)/shard_map/add | solution.py:382
  113.0 3.7 %fusion.13 = bf16[2,6,192,256]{3,2,0,1:T(8,128)(2,1)S(1)} fusion(f32[2,6,192,256]{3,2,1,0:T(8,128)} %bitcast.154, bf16[2,6,192,256]{3,2,0,1:T(8,128)(2,1)S(1)} %fusion.11, f32[6,192,256]{2,1,0:T(8,128)} %convert_element_type.196, bf16[1,2,256,256]{3,2,1,0:T(8,128)(2,1)} %get-tuple-element.20, bf16[1,2,256,256]{3,2,1,0:T(8,128)(2,1)} %get-tuple-element.19, ...), kind=kOutput, calls=%fused_computation.23 | convolution fusion | flops 1062141952 | bytes 6717440 | tf_op jit(solution)/shard_map/abyk,bxkz->axyz/dot_general | solution.py:394
  116.7 2.2 %copy.93 = bf16[2,6,192,256]{3,0,1,2:T(2,128)(2,1)} copy(bf16[2,6,192,256]{3,2,0,1:T(8,128)(2,1)S(1)} %fusion.13) | data formatting | bytes 2359296 | tf_op jit(solution)/shard_map/convert_element_type | solution.py:396
  118.9 8.2 %all-to-all-start.1 = ((bf16[2,6,192,256]{3,0,1,2:T(2,128)(2,1)}), bf16[2,6,192,256]{3,0,1,2:T(2,128)(2,1)}, u32[]{:S(2)}, u32[]{:S(2)}) async-start(bf16[2,6,192,256]{3,0,1,2:T(2,128)(2,1)} %copy.93), calls=%async_computation.1 | async-start | bytes 2359296 | tf_op jit(solution)/shard_map/all_to_all | solution.py:400
  127.1 0.6 fusion.95
  128.2 2.3 %fusion.17.part_ref = bf16[16,144,128]{2,1,0:T(8,128)(2,1)} fusion(f32[16,144,128]{2,1,0:T(8,128)S(1)} %reshape.503, f32[16,144,128]{2,1,0:T(8,128)S(1)} %reshape.504, f32[]{:T(128)} %bitcast.63, f32[]{:T(128)} %bitcast.62), kind=kLoop, calls=%fused_computation.27 | loop fusion | flops 1769472 | bytes 2949128 | tf_op jit(solution)/shard_map/convert_element_type | solution.py:347
  130.8 27.0 %shard_map.95 = bf16[16,144,128]{2,1,0:T(8,128)(2,1)} custom-call(bf16[16,144,128]{2,1,0:T(8,128)(2,1)} %fusion.17.part_ref), custom_call_target="tpu_custom_call" | custom-call | flops 294912 | bytes 1769472 | tf_op jit(solution)/shard_map/pallas_call | solution.py:74
  157.7 2.0 %reshape.502 = bf16[6,192,256]{2,1,0:T(8,128)(2,1)} reshape(bf16[16,144,128]{2,1,0:T(8,128)(2,1)} %shard_map.95) | data formatting | bytes 1179648 | tf_op jit(solution)/shard_map/reshape | solution.py:89
  159.8 27.3 %all-to-all-done.1 = bf16[2,6,192,256]{3,0,1,2:T(2,128)(2,1)} async-done(((bf16[2,6,192,256]{3,0,1,2:T(2,128)(2,1)}), bf16[2,6,192,256]{3,0,1,2:T(2,128)(2,1)}, u32[]{:S(2)}, u32[]{:S(2)}) %all-to-all-start.1) | async-done | bytes 1179680 | tf_op jit(solution)/shard_map/all_to_all | solution.py:400
  187.1 2.2 %copy.95 = bf16[2,32,6,6,256]{4,0,3,2,1:T(2,128)(2,1)S(1)} copy(bf16[2,32,6,6,256]{4,0,2,3,1:T(2,128)(2,1)} %bitcast.56) | data formatting | bytes 2359296 | tf_op jit(solution)/shard_map/all_to_all | solution.py:400
  189.3 1.9 fusion.15
  191.2 0.6 copy.155
  (48 shorter events, 3.4 us)
Async XLA Ops:
  5.2 18.4 %copy-start.4 = (s32[128,64]{0,1:T(8,128)S(1)}, s32[128,64]{0,1:T(8,128)}, u32[]{:S(2)}) copy-start(s32[128,64]{0,1:T(8,128)} %param.12) | copy-start | bytes 98308
  5.2 19.5 %copy-start.5 = (f32[8,8]{1,0:T(8,128)S(1)}, f32[8,8]{1,0:T(8,128)}, u32[]{:S(2)}) copy-start(f32[8,8]{1,0:T(8,128)} %param.11) | copy-start | bytes 772
  5.2 19.6 %copy-start.3 = (bf16[6,192,256]{2,1,0:T(8,128)(2,1)S(1)}, bf16[6,192,256]{2,1,0:T(8,128)(2,1)}, u32[]{:S(2)}) copy-start(bf16[6,192,256]{2,1,0:T(8,128)(2,1)} %param.9) | copy-start | bytes 1769476
  5.2 77.4 %all-to-all-start = ((bf16[32,2,6,6,256]{4,1,3,2,0:T(2,128)(2,1)}), bf16[32,2,6,6,256]{4,1,3,2,0:T(2,128)(2,1)S(1)}, u32[]{:S(2)}, u32[]{:S(2)}) async-start(bf16[32,2,6,6,256]{4,1,3,2,0:T(2,128)(2,1)} %copy.70), calls=%async_computation | async-start | bytes 2359296 | tf_op jit(solution)/shard_map/all_to_all | solution.py:333
  118.9 8.2 %copy-start.7 = (f32[1,2]{1,0:T(1,128)S(1)}, f32[1,2]{1,0:T(1,128)}, u32[]{:S(2)}) copy-start(f32[1,2]{1,0:T(1,128)} %param.8) | copy-start | bytes 28
  118.9 68.2 %all-to-all-start.1 = ((bf16[2,6,192,256]{3,0,1,2:T(2,128)(2,1)}), bf16[2,6,192,256]{3,0,1,2:T(2,128)(2,1)}, u32[]{:S(2)}, u32[]{:S(2)}) async-start(bf16[2,6,192,256]{3,0,1,2:T(2,128)(2,1)} %copy.93), calls=%async_computation.1 | async-start | bytes 2359296 | tf_op jit(solution)/shard_map/all_to_all | solution.py:400
  187.1 2.2 %copy-start = (bf16[1,2,192,6,256]{4,2,3,1,0:T(8,128)(2,1)S(1)}, bf16[1,2,192,6,256]{4,2,3,1,0:T(8,128)(2,1)}, u32[]{:S(2)}) copy-start(bf16[1,2,192,6,256]{4,2,3,1,0:T(8,128)(2,1)} %param.7) | copy-start | bytes 3538948
  187.1 2.2 %copy-start.1 = (bf16[1,2,192,192]{3,2,1,0:T(8,128)(2,1)S(1)}, bf16[1,2,192,192]{3,2,1,0:T(8,128)(2,1)}, u32[]{:S(2)}) copy-start(bf16[1,2,192,192]{3,2,1,0:T(8,128)(2,1)} %get-tuple-element.23) | copy-start | bytes 442372
  187.1 2.2 %copy-start.2 = (bf16[1,2,192,192]{3,2,1,0:T(8,128)(2,1)S(1)}, bf16[1,2,192,192]{3,2,1,0:T(8,128)(2,1)}, u32[]{:S(2)}) copy-start(bf16[1,2,192,192]{3,2,1,0:T(8,128)(2,1)} %get-tuple-element.24) | copy-start | bytes 442372
  189.3 1.9 copy-start.6

commit v14 on v13

--- a/solution.py
+++ b/solution.py
@@ -360,6 +360,7 @@
     selector = (
         (row_of[:, None] == jnp.arange(slab_rows, dtype=jnp.int32)[None, :]) & is_mine[:, None]
     ).astype(jnp.bfloat16)
+    selector = lax.optimization_barrier(selector)
     field_rows = wave_field.reshape(2, slab_rows, size_z)
     picked_rows = jnp.einsum(
         "er,crz->cez", selector, field_rows, preferred_element_type=jnp.float32

time: 192 us -> 198 us (1.031)
  local copies, waits for them, and re-layouts: 14.6 us -> 18.1 us
  other arithmetic: 13.7 us -> 16.1 us
    unnamed x20, local copies, waits for them, and re-layouts: 1.13 us -> 3.83 us
where the time goes in v14:
time: 198 us; the launch traced here: 197 us
  waiting for transfers between devices  73.5 us (37%)
  Pallas kernels  46.5 us (23%)
  starting transfers between devices  26.6 us (13%)
  local copies, waits for them, and re-layouts  18.1 us (9%)
  other arithmetic  16.1 us (8%)
  matrix products  15.5 us (8%)
    all_to_all x1, waiting for transfers between devices, per_device(): lax.all_to_all(along_x, 'fft', split_axis=0, concat_axis=0, tiled=True)  46.2 us
    all_to_all x1, waiting for transfers between devices, per_device(): lax.all_to_all(back_y, 'fft', split_axis=2, concat_axis=1, tiled=True)  27.3 us
    pallas_call x1, Pallas kernels, band_sum(): pl.pallas_call(band_sum_kernel, out_shape=jax.ShapeDtypeStruct(chunks.sha...  27 us
    pallas_call x1, Pallas kernels, halo_exchange(): pl.pallas_call(halo_kernel, out_shape=(jax.ShapeDtypeStruct((2 * atoms, 1...  19.5 us
    all_to_all x1, starting transfers between devices, per_device(): lax.all_to_all(along_x, 'fft', split_axis=0, concat_axis=0, tiled=True)  18.4 us
    all_to_all x1, starting transfers between devices, per_device(): lax.all_to_all(back_y, 'fft', split_axis=2, concat_axis=1, tiled=True)  8.2 us
    another operation x6, other arithmetic  6.51 us
  transfers between devices with their start and end apart: 2, of which 2 were waited for; matrix products, arithmetic and copies ran while one was open for 9% of the time, Pallas kernels for 14%

profile of v14, /device:TPU:6, one launch (start us, length us, event | category | flops | bytes accessed | tf_op | source)
XLA Modules:
  0.0 197.3 jit_solution(16035929526843355351)
XLA Ops:
  0.6 2.2 %bitcast_convert_fusion.4 = bf16[6,384,256]{2,1,0:T(8,128)(2,1)S(1)} fusion(bf16[384,2,192]{0,2,1:T(8,128)(2,1)} %constant.149, bf16[1,2,192,6,256]{4,2,3,1,0:T(8,128)(2,1)} %param.7), kind=kOutput, calls=%fused_computation.11 | convolution fusion | flops 453574656 | bytes 2654208 | tf_op jit(solution)/shard_map/ypcx,cxyz->ypz/dot_general | solution.py:326
  3.3 1.9 copy.70
  5.2 18.4 %all-to-all-start = ((bf16[32,2,6,6,256]{4,1,3,2,0:T(2,128)(2,1)}), bf16[32,2,6,6,256]{4,1,3,2,0:T(2,128)(2,1)}, u32[]{:S(2)}, u32[]{:S(2)}) async-start(bf16[32,2,6,6,256]{4,1,3,2,0:T(2,128)(2,1)} %copy.70), calls=%async_computation | async-start | bytes 2359296 | tf_op jit(solution)/shard_map/all_to_all | solution.py:333
  25.7 1.1 convert_element_type.198
  26.8 0.8 fusion.70
  27.6 1.0 multiply_convert_fusion.2
  28.6 0.8 negate_convert_fusion.3
  29.4 1.0 negate_convert_fusion
  30.4 1.3 multiply_convert_fusion
  31.7 0.8 maximum_bitcast_fusion.8
  32.6 0.9 fusion.53
  34.0 1.6 negate_convert_fusion.2
  35.6 1.0 fusion.49.lower_half_ref
  36.6 46.2 %all-to-all-done = bf16[32,2,6,6,256]{4,1,3,2,0:T(2,128)(2,1)} async-done(((bf16[32,2,6,6,256]{4,1,3,2,0:T(2,128)(2,1)}), bf16[32,2,6,6,256]{4,1,3,2,0:T(2,128)(2,1)}, u32[]{:S(2)}, u32[]{:S(2)}) %all-to-all-start) | async-done | bytes 1179680 | tf_op jit(solution)/shard_map/all_to_all | solution.py:333
  82.8 2.8 %fusion.7 = bf16[2,6,192,256]{3,2,0,1:T(8,128)(2,1)S(1)} fusion(bf16[32,2,6,6,256,1]{4,1,3,2,0,5:T(2,128)(2,1)} %bitcast.8, bf16[1,2,256,256]{3,2,1,0:T(8,128)(2,1)S(1)} %get-tuple-element.21, bf16[1,2,256,256]{3,2,1,0:T(8,128)(2,1)S(1)} %get-tuple-element.22, bf16[1,1,192,32,6]{2,3,4,1,0:T(8,128)(2,1)} %get-tuple-element.31, ...), kind=kOutput, calls=%fused_computation.19 | convolution fusion | flops 1060372480 | bytes 3104768 | tf_op jit(solution)/shard_map/abzk,bxyk->axyz/dot_general | solution.py:340
  85.7 1.2 fusion.5
  87.0 0.9 fusion.90
  87.9 1.2 copy.113
  89.1 1.9 copy.114
  91.0 1.3 fusion.26
  93.0 19.5 %shard_map.94 = (f32[8,128]{1,0:T(8,128)}, bf16[4,3,4,64,256]{4,3,2,1,0:T(8,128)(2,1)}) custom-call(bf16[2,4,64,128]{3,2,1,0:T(8,128)(2,1)} %get-tuple-element.18.to_left_ref, bf16[2,4,64,128]{3,2,1,0:T(8,128)(2,1)} %get-tuple-element.17.own_ref, bf16[2,4,64,128]{3,2,1,0:T(8,128)(2,1)} %get-tuple-element.16.to_right_ref, bf16[4,8,64,128]{3,2,1,0:T(8,128)(2,1)} %beta_ref.1, ...), custom_call_target="tpu_custom_call" | custom-call | flops 2097152 | bytes 1048576 | tf_op jit(solution)/shard_map/pallas_call | solution.py:233
  112.6 3.7 %convolution_bitcast_fusion = f32[4,1152,256]{1,2,0:T(8,128)S(1)} fusion(bf16[4,768,256]{2,1,0:T(8,128)(2,1)} %bitcast.170, bf16[768,1152]{1,0:T(8,128)(2,1)S(1)} %fusion.1), kind=kOutput, calls=%fused_computation | convolution fusion | flops 1811939328 | bytes 8060928 | tf_op jit(solution)/shard_map/er,cez->crz/dot_general | solution.py:377
  116.5 2.0 %copy.91 = f32[2,1152,256]{2,1,0:T(8,128)} copy(f32[2,1152,256]{1,2,0:T(8,128)S(1)} %slice_add_fusion) | data formatting | bytes 4718592 | tf_op jit(solution)/shard_map/add | solution.py:383
  118.5 3.7 %fusion.9 = bf16[2,6,192,256]{3,2,0,1:T(8,128)(2,1)S(1)} fusion(f32[2,6,192,256]{3,2,1,0:T(8,128)} %bitcast.155, bf16[2,6,192,256]{3,2,0,1:T(8,128)(2,1)S(1)} %fusion.7, f32[6,192,256]{2,1,0:T(8,128)} %convert_element_type.198, bf16[1,2,256,256]{3,2,1,0:T(8,128)(2,1)} %get-tuple-element.20, bf16[1,2,256,256]{3,2,1,0:T(8,128)(2,1)} %get-tuple-element.19, ...), kind=kOutput, calls=%fused_computation.21 | convolution fusion | flops 1062141952 | bytes 6717440 | tf_op jit(solution)/shard_map/abyk,bxkz->axyz/dot_general | solution.py:395
  122.1 2.2 %copy.93 = bf16[2,6,192,256]{3,0,1,2:T(2,128)(2,1)} copy(bf16[2,6,192,256]{3,2,0,1:T(8,128)(2,1)S(1)} %fusion.9) | data formatting | bytes 2359296 | tf_op jit(solution)/shard_map/convert_element_type | solution.py:397
  124.4 8.2 %all-to-all-start.1 = ((bf16[2,6,192,256]{3,0,1,2:T(2,128)(2,1)}), bf16[2,6,192,256]{3,0,1,2:T(2,128)(2,1)}, u32[]{:S(2)}, u32[]{:S(2)}) async-start(bf16[2,6,192,256]{3,0,1,2:T(2,128)(2,1)} %copy.93), calls=%async_computation.1 | async-start | bytes 2359296 | tf_op jit(solution)/shard_map/all_to_all | solution.py:401
  133.7 2.3 %fusion.13.part_ref = bf16[16,144,128]{2,1,0:T(8,128)(2,1)} fusion(f32[16,144,128]{2,1,0:T(8,128)S(1)} %reshape.503, f32[16,144,128]{2,1,0:T(8,128)S(1)} %reshape.504, f32[]{:T(128)} %bitcast.63, f32[]{:T(128)} %bitcast.62), kind=kLoop, calls=%fused_computation.25 | loop fusion | flops 1769472 | bytes 2949128 | tf_op jit(solution)/shard_map/convert_element_type | solution.py:347
  136.3 27.0 %shard_map.95 = bf16[16,144,128]{2,1,0:T(8,128)(2,1)} custom-call(bf16[16,144,128]{2,1,0:T(8,128)(2,1)} %fusion.13.part_ref), custom_call_target="tpu_custom_call" | custom-call | flops 294912 | bytes 1769472 | tf_op jit(solution)/shard_map/pallas_call | solution.py:74
  163.3 2.0 %reshape.502 = bf16[6,192,256]{2,1,0:T(8,128)(2,1)} reshape(bf16[16,144,128]{2,1,0:T(8,128)(2,1)} %shard_map.95) | data formatting | bytes 1179648 | tf_op jit(solution)/shard_map/reshape | solution.py:89
  165.3 27.3 %all-to-all-done.1 = bf16[2,6,192,256]{3,0,1,2:T(2,128)(2,1)} async-done(((bf16[2,6,192,256]{3,0,1,2:T(2,128)(2,1)}), bf16[2,6,192,256]{3,0,1,2:T(2,128)(2,1)}, u32[]{:S(2)}, u32[]{:S(2)}) %all-to-all-start.1) | async-done | bytes 1179680 | tf_op jit(solution)/shard_map/all_to_all | solution.py:401
  192.6 2.2 %copy.95 = bf16[2,32,6,6,256]{4,0,3,2,1:T(2,128)(2,1)S(1)} copy(bf16[2,32,6,6,256]{4,0,2,3,1:T(2,128)(2,1)} %bitcast.56) | data formatting | bytes 2359296 | tf_op jit(solution)/shard_map/all_to_all | solution.py:401
  194.9 1.9 fusion.11
  (49 shorter events, 5.9 us)
Async XLA Ops:
  5.2 18.5 %copy-start.4 = (s32[128,64]{0,1:T(8,128)S(1)}, s32[128,64]{0,1:T(8,128)}, u32[]{:S(2)}) copy-start(s32[128,64]{0,1:T(8,128)} %param.12) | copy-start | bytes 98308
  5.2 77.5 %all-to-all-start = ((bf16[32,2,6,6,256]{4,1,3,2,0:T(2,128)(2,1)}), bf16[32,2,6,6,256]{4,1,3,2,0:T(2,128)(2,1)}, u32[]{:S(2)}, u32[]{:S(2)}) async-start(bf16[32,2,6,6,256]{4,1,3,2,0:T(2,128)(2,1)} %copy.70), calls=%async_computation | async-start | bytes 2359296 | tf_op jit(solution)/shard_map/all_to_all | solution.py:333
  24.1 1.5 copy-start.5
  24.1 1.6 copy-start.3
  124.4 8.3 %copy-start.7 = (f32[1,2]{1,0:T(1,128)S(1)}, f32[1,2]{1,0:T(1,128)}, u32[]{:S(2)}) copy-start(f32[1,2]{1,0:T(1,128)} %param.8) | copy-start | bytes 28
  124.4 68.2 %all-to-all-start.1 = ((bf16[2,6,192,256]{3,0,1,2:T(2,128)(2,1)}), bf16[2,6,192,256]{3,0,1,2:T(2,128)(2,1)}, u32[]{:S(2)}, u32[]{:S(2)}) async-start(bf16[2,6,192,256]{3,0,1,2:T(2,128)(2,1)} %copy.93), calls=%async_computation.1 | async-start | bytes 2359296 | tf_op jit(solution)/shard_map/all_to_all | solution.py:401
  192.6 2.2 %copy-start = (bf16[1,2,192,6,256]{4,2,3,1,0:T(8,128)(2,1)S(1)}, bf16[1,2,192,6,256]{4,2,3,1,0:T(8,128)(2,1)}, u32[]{:S(2)}) copy-start(bf16[1,2,192,6,256]{4,2,3,1,0:T(8,128)(2,1)} %param.7) | copy-start | bytes 3538948
  192.6 2.2 %copy-start.1 = (bf16[1,2,192,192]{3,2,1,0:T(8,128)(2,1)S(1)}, bf16[1,2,192,192]{3,2,1,0:T(8,128)(2,1)}, u32[]{:S(2)}) copy-start(bf16[1,2,192,192]{3,2,1,0:T(8,128)(2,1)} %get-tuple-element.23) | copy-start | bytes 442372
  192.6 2.2 %copy-start.2 = (bf16[1,2,192,192]{3,2,1,0:T(8,128)(2,1)S(1)}, bf16[1,2,192,192]{3,2,1,0:T(8,128)(2,1)}, u32[]{:S(2)}) copy-start(bf16[1,2,192,192]{3,2,1,0:T(8,128)(2,1)} %get-tuple-element.24) | copy-start | bytes 442372
  194.8 1.9 copy-start.6

commit v15 on v13

--- a/solution.py
+++ b/solution.py
@@ -180,9 +180,10 @@
         for copy in copies:
             copy.start()
         for copy in copies:
-            copy.wait()
-
-    swap(to_left_ref, to_right_ref, landed, 0)
+            copy.wait_recv()
+        return copies
+
+    first = swap(to_left_ref, to_right_ref, landed, 0)
     atoms, nproj = beta_ref.shape[0], beta_ref.shape[1]
     lane = lax.broadcasted_iota(jnp.int32, (1, 128), 1)
     for c in range(2):
@@ -207,11 +208,13 @@
                 spread = spread + beta_ref[a, i].astype(jnp.float32) * energy
             place(placed_ref, lower_half_ref, c, 1, a, spread)
             outgoing[c, a] = spread.astype(outgoing.dtype)
-    swap(outgoing, outgoing, landed_spread, 4)
+    second = swap(outgoing, outgoing, landed_spread, 4)
     for c in range(2):
         for a in range(atoms):
             place(placed_ref, lower_half_ref, c, 0, a, landed_spread[1, c, a].astype(jnp.float32))
             place(placed_ref, lower_half_ref, c, 2, a, landed_spread[0, c, a].astype(jnp.float32))
+    for copy in first + second:
+        copy.wait_send()
 
 
 def place(placed_ref, lower_half_ref, c, side, a, value):

time: 192 us -> 192 us (level)
  no operation moved by 1% of the time
where the time goes in v15:
time: 192 us
  waiting for transfers between devices  74.9 us (39%)
  Pallas kernels  46.5 us (24%)
  starting transfers between devices  26.5 us (14%)
  matrix products  14.7 us (8%)
  local copies, waits for them, and re-layouts  14.6 us (8%)
  other arithmetic  13.7 us (7%)
    all_to_all x1, waiting for transfers between devices, per_device(): lax.all_to_all(along_x, 'fft', split_axis=0, concat_axis=0, tiled=True)  47.6 us
    all_to_all x1, waiting for transfers between devices, per_device(): lax.all_to_all(back_y, 'fft', split_axis=2, concat_axis=1, tiled=True)  27.3 us
    pallas_call x1, Pallas kernels, band_sum(): pl.pallas_call(band_sum_kernel, out_shape=jax.ShapeDtypeStruct(chunks.sha...  27 us
    pallas_call x1, Pallas kernels, halo_exchange(): pl.pallas_call(halo_kernel, out_shape=(jax.ShapeDtypeStruct((2 * atoms, 1...  19.5 us
    all_to_all x1, starting transfers between devices, per_device(): lax.all_to_all(along_x, 'fft', split_axis=0, concat_axis=0, tiled=True)  18.3 us
    all_to_all x1, starting transfers between devices, per_device(): lax.all_to_all(back_y, 'fft', split_axis=2, concat_axis=1, tiled=True)  8.17 us
    another operation x6, other arithmetic  5.81 us
    dot_general x1, matrix products, per_device(): jnp.einsum('er,cez->crz', selector, placed.reshape(4, -1, size_z), prefer...  3.88 us
  transfers between devices with their start and end apart: 2, of which 2 were waited for; matrix products, arithmetic and copies ran while one was open for 9% of the time, Pallas kernels for 14%

profile of v15, /device:TPU:6, one launch (start us, length us, event | category | flops | bytes accessed | tf_op | source)
XLA Modules:
  0.0 191.8 jit_solution(16209104865415160089)
XLA Ops:
  0.6 2.2 %bitcast_convert_fusion.4 = bf16[6,384,256]{2,1,0:T(8,128)(2,1)S(1)} fusion(bf16[384,2,192]{0,2,1:T(8,128)(2,1)} %constant.149, bf16[1,2,192,6,256]{4,2,3,1,0:T(8,128)(2,1)} %param.7), kind=kOutput, calls=%fused_computation.12 | convolution fusion | flops 453574656 | bytes 2654208 | tf_op jit(solution)/shard_map/ypcx,cxyz->ypz/dot_general | solution.py:329
  3.3 1.9 %copy.70 = bf16[32,2,6,6,256]{4,1,3,2,0:T(2,128)(2,1)} copy(bf16[32,2,6,6,256]{4,2,1,0,3:T(8,128)(2,1)S(1)} %bitcast.152) | data formatting | bytes 2359296 | tf_op jit(solution)/shard_map/transpose | solution.py:335
  5.2 18.3 %all-to-all-start = ((bf16[32,2,6,6,256]{4,1,3,2,0:T(2,128)(2,1)}), bf16[32,2,6,6,256]{4,1,3,2,0:T(2,128)(2,1)S(1)}, u32[]{:S(2)}, u32[]{:S(2)}) async-start(bf16[32,2,6,6,256]{4,1,3,2,0:T(2,128)(2,1)} %copy.70), calls=%async_computation | async-start | bytes 2359296 | tf_op jit(solution)/shard_map/all_to_all | solution.py:336
  24.8 1.1 convert_element_type.196
  26.0 0.8 fusion.74
  26.8 1.0 multiply_convert_fusion.2
  27.8 0.8 negate_convert_fusion.3
  28.6 1.0 negate_convert_fusion
  29.6 1.3 multiply_convert_fusion
  30.9 0.8 maximum_bitcast_fusion.8
  31.7 0.9 fusion.57
  32.6 0.6 fusion.81.coupled_ref
  33.2 0.9 negate_convert_fusion.2
  34.2 0.9 fusion.53.lower_half_ref
  35.1 47.6 %all-to-all-done = bf16[32,2,6,6,256]{4,1,3,2,0:T(2,128)(2,1)S(1)} async-done(((bf16[32,2,6,6,256]{4,1,3,2,0:T(2,128)(2,1)}), bf16[32,2,6,6,256]{4,1,3,2,0:T(2,128)(2,1)S(1)}, u32[]{:S(2)}, u32[]{:S(2)}) %all-to-all-start) | async-done | bytes 1179680 | tf_op jit(solution)/shard_map/all_to_all | solution.py:336
  82.7 1.5 fusion.11
  84.2 1.6 fusion.3
  86.6 0.8 slice_bitcast_fusion
  87.4 19.5 %shard_map.94 = (f32[8,128]{1,0:T(8,128)}, bf16[4,3,4,64,256]{4,3,2,1,0:T(8,128)(2,1)}) custom-call(bf16[2,4,64,128]{3,2,1,0:T(8,128)(2,1)} %get-tuple-element.18.to_left_ref, bf16[2,4,64,128]{3,2,1,0:T(8,128)(2,1)} %get-tuple-element.17.own_ref, bf16[2,4,64,128]{3,2,1,0:T(8,128)(2,1)} %get-tuple-element.16.to_right_ref, bf16[4,8,64,128]{3,2,1,0:T(8,128)(2,1)} %beta_ref.1, ...), custom_call_target="tpu_custom_call" | custom-call | flops 2097152 | bytes 1048576 | tf_op jit(solution)/shard_map/pallas_call | solution.py:236
  106.9 3.9 %convolution_bitcast_fusion = f32[4,1152,256]{1,2,0:T(8,128)S(1)} fusion(bf16[4,768,256]{2,1,0:T(8,128)(2,1)} %bitcast.170, s32[768]{0:T(1024)S(1)} %add_select_fusion.6, pred[768]{0:T(1024)(128)(4,1)S(1)} %fusion.80), kind=kOutput, calls=%fused_computation | convolution fusion | flops 1813708800 | bytes 6295296 | tf_op jit(solution)/shard_map/er,cez->crz/dot_general | solution.py:379
  111.0 2.0 %copy.91 = f32[2,1152,256]{2,1,0:T(8,128)} copy(f32[2,1152,256]{1,2,0:T(8,128)S(1)} %slice_add_fusion) | data formatting | bytes 4718592 | tf_op jit(solution)/shard_map/add | solution.py:385
  113.0 3.7 %fusion.13 = bf16[2,6,192,256]{3,2,0,1:T(8,128)(2,1)S(1)} fusion(f32[2,6,192,256]{3,2,1,0:T(8,128)} %bitcast.154, bf16[2,6,192,256]{3,2,0,1:T(8,128)(2,1)S(1)} %fusion.11, f32[6,192,256]{2,1,0:T(8,128)} %convert_element_type.196, bf16[1,2,256,256]{3,2,1,0:T(8,128)(2,1)} %get-tuple-element.20, bf16[1,2,256,256]{3,2,1,0:T(8,128)(2,1)} %get-tuple-element.19, ...), kind=kOutput, calls=%fused_computation.23 | convolution fusion | flops 1062141952 | bytes 6717440 | tf_op jit(solution)/shard_map/abyk,bxkz->axyz/dot_general | solution.py:397
  116.7 2.2 %copy.93 = bf16[2,6,192,256]{3,0,1,2:T(2,128)(2,1)} copy(bf16[2,6,192,256]{3,2,0,1:T(8,128)(2,1)S(1)} %fusion.13) | data formatting | bytes 2359296 | tf_op jit(solution)/shard_map/convert_element_type | solution.py:399
  118.9 8.2 %all-to-all-start.1 = ((bf16[2,6,192,256]{3,0,1,2:T(2,128)(2,1)}), bf16[2,6,192,256]{3,0,1,2:T(2,128)(2,1)}, u32[]{:S(2)}, u32[]{:S(2)}) async-start(bf16[2,6,192,256]{3,0,1,2:T(2,128)(2,1)} %copy.93), calls=%async_computation.1 | async-start | bytes 2359296 | tf_op jit(solution)/shard_map/all_to_all | solution.py:403
  127.1 0.6 fusion.95
  128.2 2.3 %fusion.17.part_ref = bf16[16,144,128]{2,1,0:T(8,128)(2,1)} fusion(f32[16,144,128]{2,1,0:T(8,128)S(1)} %reshape.503, f32[16,144,128]{2,1,0:T(8,128)S(1)} %reshape.504, f32[]{:T(128)} %bitcast.63, f32[]{:T(128)} %bitcast.62), kind=kLoop, calls=%fused_computation.27 | loop fusion | flops 1769472 | bytes 2949128 | tf_op jit(solution)/shard_map/convert_element_type | solution.py:350
  130.8 27.0 %shard_map.95 = bf16[16,144,128]{2,1,0:T(8,128)(2,1)} custom-call(bf16[16,144,128]{2,1,0:T(8,128)(2,1)} %fusion.17.part_ref), custom_call_target="tpu_custom_call" | custom-call | flops 294912 | bytes 1769472 | tf_op jit(solution)/shard_map/pallas_call | solution.py:74
  157.7 2.0 %reshape.502 = bf16[6,192,256]{2,1,0:T(8,128)(2,1)} reshape(bf16[16,144,128]{2,1,0:T(8,128)(2,1)} %shard_map.95) | data formatting | bytes 1179648 | tf_op jit(solution)/shard_map/reshape | solution.py:89
  159.8 27.3 %all-to-all-done.1 = bf16[2,6,192,256]{3,0,1,2:T(2,128)(2,1)} async-done(((bf16[2,6,192,256]{3,0,1,2:T(2,128)(2,1)}), bf16[2,6,192,256]{3,0,1,2:T(2,128)(2,1)}, u32[]{:S(2)}, u32[]{:S(2)}) %all-to-all-start.1) | async-done | bytes 1179680 | tf_op jit(solution)/shard_map/all_to_all | solution.py:403
  187.1 2.2 %copy.95 = bf16[2,32,6,6,256]{4,0,3,2,1:T(2,128)(2,1)S(1)} copy(bf16[2,32,6,6,256]{4,0,2,3,1:T(2,128)(2,1)} %bitcast.56) | data formatting | bytes 2359296 | tf_op jit(solution)/shard_map/all_to_all | solution.py:403
  189.3 1.9 fusion.15
  191.2 0.6 copy.155
  (48 shorter events, 3.4 us)
Async XLA Ops:
  5.2 18.4 %copy-start.4 = (s32[128,64]{0,1:T(8,128)S(1)}, s32[128,64]{0,1:T(8,128)}, u32[]{:S(2)}) copy-start(s32[128,64]{0,1:T(8,128)} %param.12) | copy-start | bytes 98308
  5.2 19.5 %copy-start.5 = (f32[8,8]{1,0:T(8,128)S(1)}, f32[8,8]{1,0:T(8,128)}, u32[]{:S(2)}) copy-start(f32[8,8]{1,0:T(8,128)} %param.11) | copy-start | bytes 772
  5.2 19.6 %copy-start.3 = (bf16[6,192,256]{2,1,0:T(8,128)(2,1)S(1)}, bf16[6,192,256]{2,1,0:T(8,128)(2,1)}, u32[]{:S(2)}) copy-start(bf16[6,192,256]{2,1,0:T(8,128)(2,1)} %param.9) | copy-start | bytes 1769476
  5.2 77.4 %all-to-all-start = ((bf16[32,2,6,6,256]{4,1,3,2,0:T(2,128)(2,1)}), bf16[32,2,6,6,256]{4,1,3,2,0:T(2,128)(2,1)S(1)}, u32[]{:S(2)}, u32[]{:S(2)}) async-start(bf16[32,2,6,6,256]{4,1,3,2,0:T(2,128)(2,1)} %copy.70), calls=%async_computation | async-start | bytes 2359296 | tf_op jit(solution)/shard_map/all_to_all | solution.py:336
  118.9 8.2 %copy-start.7 = (f32[1,2]{1,0:T(1,128)S(1)}, f32[1,2]{1,0:T(1,128)}, u32[]{:S(2)}) copy-start(f32[1,2]{1,0:T(1,128)} %param.8) | copy-start | bytes 28
  118.9 68.2 %all-to-all-start.1 = ((bf16[2,6,192,256]{3,0,1,2:T(2,128)(2,1)}), bf16[2,6,192,256]{3,0,1,2:T(2,128)(2,1)}, u32[]{:S(2)}, u32[]{:S(2)}) async-start(bf16[2,6,192,256]{3,0,1,2:T(2,128)(2,1)} %copy.93), calls=%async_computation.1 | async-start | bytes 2359296 | tf_op jit(solution)/shard_map/all_to_all | solution.py:403
  187.1 2.2 %copy-start = (bf16[1,2,192,6,256]{4,2,3,1,0:T(8,128)(2,1)S(1)}, bf16[1,2,192,6,256]{4,2,3,1,0:T(8,128)(2,1)}, u32[]{:S(2)}) copy-start(bf16[1,2,192,6,256]{4,2,3,1,0:T(8,128)(2,1)} %param.7) | copy-start | bytes 3538948
  187.1 2.2 %copy-start.1 = (bf16[1,2,192,192]{3,2,1,0:T(8,128)(2,1)S(1)}, bf16[1,2,192,192]{3,2,1,0:T(8,128)(2,1)}, u32[]{:S(2)}) copy-start(bf16[1,2,192,192]{3,2,1,0:T(8,128)(2,1)} %get-tuple-element.23) | copy-start | bytes 442372
  187.1 2.2 %copy-start.2 = (bf16[1,2,192,192]{3,2,1,0:T(8,128)(2,1)S(1)}, bf16[1,2,192,192]{3,2,1,0:T(8,128)(2,1)}, u32[]{:S(2)}) copy-start(bf16[1,2,192,192]{3,2,1,0:T(8,128)(2,1)} %get-tuple-element.24) | copy-start | bytes 442372
  189.3 1.9 copy-start.6
